TPU v7x, 32 devices: a whole 2x2x4 slice. The times are simulated.
32 devices in a mesh: flow: 8 (over z, x), lat: 4 (over y, core).
Axes of the slice: x: 2, y: 2, z: 4, core: 2. Of those that a mesh axis runs over, the one named last changes fastest.
Arguments:
- conc_old: float32 [2, 64, 64, 2048], P(None, 'flow', None, 'lat'), may hold values from -6 to 6
- lat_velocity: float32 [64, 2048], P('flow', 'lat'), may hold values from -3 to 3
- elem_type: int32 [64, 2048], P('flow', 'lat'), may hold values from 0 to 3
- inlet_trace: float32 [2, 16, 2048], P(None, None, 'lat'), may hold values from -6 to 6
- solve_table: float32 [2, 4, 64, 80], replicated, may hold values from -0.65 to 1.25
Outputs:
- conc_new: bfloat16 [2, 64, 64, 2048], P(None, 'flow', None, 'lat')
All inputs are finite; a program needn't handle non-finite values.
Results may differ from a plain program's by a relative error of at most 0.001.
Values sent between devices are 32-bit elements; how exact they have to be, the bound alone decides.
No kernel may reach another device: no remote copies, remote signals or barrier semaphores. Data moves between devices by JAX's collectives and lax.ppermute only.
A program may use at most 64 MiB of HBM per device.

v0:
```python
import jax
import jax.numpy as jnp
from jax import lax
from jax.sharding import PartitionSpec as P

precise = lax.Precision.HIGHEST


def shifted(block, axis, distance):
    devices = range(lax.axis_size(axis))
    route = [(i - distance, i) for i in devices if i - distance in devices]
    return lax.ppermute(block, axis, route)


def add_faces(conc_old, flux_left, flux_right):
    shp = conc_old.shape
    dof_grid = conc_old.reshape(shp[0], shp[1], shp[2] // 4, 4, shp[3])
    dof_grid = dof_grid.at[:, :, :, 0, :].add(flux_left)
    dof_grid = dof_grid.at[:, :, :, 3, :].add(-flux_right)
    return dof_grid.reshape(shp)


def pick_type(onehot, per_type):
    return jnp.einsum("tc,st...c->s...c", onehot, per_type, precision=precise)


def apply_map(slab_map, offset, trace_in):
    return jnp.einsum("sijc,sjc->sic", slab_map, trace_in, precision=precise) + offset


def on_device(conc_old, lat_velocity, elem_type, inlet_trace, solve_table):
    species, levels, dof_count, columns = conc_old.shape
    type_count = solve_table.shape[1]
    trace_size = inlet_trace.shape[1]
    type_ids = jnp.arange(type_count, dtype=jnp.int32)
    right_tr = conc_old[:, :, 3::4, :]
    left_tr = conc_old[:, :, 0::4, :]
    rim_trace = shifted(right_tr[:, :, :, columns - 1 :], "lat", 1)
    upwind = jnp.concatenate([rim_trace, right_tr[:, :, :, : columns - 1]], axis=3)
    velocity = lat_velocity[None, :, None, :]
    flux_left = jnp.maximum(velocity, 0.0) * upwind + jnp.minimum(velocity, 0.0) * left_tr
    next_flux = shifted(flux_left[:, :, :, :1], "lat", -1)
    flux_right = jnp.concatenate([flux_left[:, :, :, 1:], next_flux], axis=3)
    source = add_faces(conc_old, flux_left, flux_right)
    interior_part = solve_table[:, :, :, :dof_count]
    coupling_part = solve_table[:, :, :, dof_count:]
    top_rows = coupling_part[:, :, dof_count - trace_size :, :]
    onehots = [
        (elem_type[level][None, :] == type_ids[:, None]).astype(jnp.float32)
        for level in range(levels)
    ]
    source_terms = []
    for level in range(levels):
        per_type = jnp.einsum("stij,sjc->stic", interior_part, source[:, level], precision=precise)
        source_terms.append(pick_type(onehots[level], per_type))
    identity_map = jnp.broadcast_to(
        jnp.eye(trace_size, dtype=jnp.float32)[None, :, :, None],
        (species, trace_size, trace_size, columns),
    )
    zero_offset = jnp.zeros((species, trace_size, columns), jnp.float32)
    slab_map = identity_map
    offset = zero_offset
    for level in range(levels):
        per_type = jnp.einsum("stij,sjkc->stikc", top_rows, slab_map, precision=precise)
        slab_map = pick_type(onehots[level], per_type)
        moved = jnp.einsum("stij,sjc->stic", top_rows, offset, precision=precise)
        offset = (
            pick_type(onehots[level], moved) + source_terms[level][:, dof_count - trace_size :, :]
        )
    flow_index = lax.axis_index("flow")
    flow_count = lax.axis_size("flow")

    def chain_step(turn, carry):
        trace_in, trace_out = carry
        received = shifted(trace_out, "flow", 1)
        trace_in = jnp.where(flow_index == 0, inlet_trace, received)
        return (trace_in, apply_map(slab_map, offset, trace_in))

    start_out = apply_map(slab_map, offset, inlet_trace)
    trace_in, last_out = lax.fori_loop(0, flow_count - 1, chain_step, (inlet_trace, start_out))
    solved_levels = []
    for level in range(levels):
        per_type = jnp.einsum("stij,sjc->stic", coupling_part, trace_in, precision=precise)
        solved_level = source_terms[level] + pick_type(onehots[level], per_type)
        solved_levels.append(solved_level)
        trace_in = solved_level[:, dof_count - trace_size :, :]
    return jnp.stack(solved_levels, axis=1).astype(jnp.bfloat16)


def solution(mesh):
    in_specs = (
        P(None, "flow", None, "lat"),
        P("flow", "lat"),
        P("flow", "lat"),
        P(None, None, "lat"),
        P(),
    )
    out_specs = P(None, "flow", None, "lat")
    return jax.shard_map(
        on_device, mesh=mesh, in_specs=in_specs, out_specs=out_specs, check_vma=False
    )
```

profile of v0, /device:TPU:28, one launch (start us, length us, event | category | flops | bytes accessed | tf_op | source)
XLA Modules:
  0.0 138.4 jit_solution(15301933321906517009)
XLA Ops:
  0.0 2.9 %copy.15 = f32[2,8,64,512]{3,1,2,0:T(8,128)S(1)} copy(f32[2,8,64,512]{3,2,1,0:T(8,128)} %param.11) | data formatting | bytes 4194304 | tf_op args[0]
  7.2 3.9 %fusion.7 = f32[512,2,16,16]{0,2,3,1:T(8,128)S(1)} fusion(f32[512,4]{0,1:T(4,128)S(1)} %fusion.123, f32[16,16]{0,1:T(8,128)S(1)} %fusion.124, f32[2,4,64,80]{3,2,1,0:T(8,128)S(1)} %copy-done), kind=kOutput, calls=%fused_computation.18 | convolution fusion | flops 203161600 | bytes 1130496 | tf_op jit(solution)/shard_map/stij,sjkc->stikc/dot_general | solution.py:64
  11.1 3.9 %fusion.6 = f32[512,2,16,16]{0,2,3,1:T(8,128)S(1)} fusion(f32[512,4]{0,1:T(4,128)S(1)} %fusion.126, f32[512,2,16,16]{0,2,3,1:T(8,128)S(1)} %fusion.7, f32[2,4,64,80]{3,2,1,0:T(8,128)S(1)} %copy-done), kind=kOutput, calls=%fused_computation.16 | convolution fusion | flops 203161600 | bytes 2170880 | tf_op jit(solution)/shard_map/stij,sjkc->stikc/dot_general | solution.py:64
  15.0 3.9 %fusion.5 = f32[512,2,16,16]{0,2,3,1:T(8,128)S(1)} fusion(f32[512,4]{0,1:T(4,128)S(1)} %fusion.128, f32[512,2,16,16]{0,2,3,1:T(8,128)S(1)} %fusion.6, f32[2,4,64,80]{3,2,1,0:T(8,128)S(1)} %copy-done), kind=kOutput, calls=%fused_computation.14 | convolution fusion | flops 203161600 | bytes 2170880 | tf_op jit(solution)/shard_map/stij,sjkc->stikc/dot_general | solution.py:64
  18.8 3.9 %fusion.4 = f32[512,2,16,16]{0,2,3,1:T(8,128)S(1)} fusion(f32[512,4]{0,1:T(4,128)S(1)} %fusion.130, f32[512,2,16,16]{0,2,3,1:T(8,128)S(1)} %fusion.5, f32[2,4,64,80]{3,2,1,0:T(8,128)S(1)} %copy-done), kind=kOutput, calls=%fused_computation.12 | convolution fusion | flops 203161600 | bytes 2170880 | tf_op jit(solution)/shard_map/stij,sjkc->stikc/dot_general | solution.py:64
  22.7 3.9 %fusion.3 = f32[512,2,16,16]{0,2,3,1:T(8,128)S(1)} fusion(f32[512,4]{0,1:T(4,128)S(1)} %fusion.132, f32[512,2,16,16]{0,2,3,1:T(8,128)S(1)} %fusion.4, f32[2,4,64,80]{3,2,1,0:T(8,128)S(1)} %copy-done), kind=kOutput, calls=%fused_computation.10 | convolution fusion | flops 203161600 | bytes 2170880 | tf_op jit(solution)/shard_map/stij,sjkc->stikc/dot_general | solution.py:64
  26.6 3.9 %fusion.2 = f32[512,2,16,16]{0,2,3,1:T(8,128)S(1)} fusion(f32[512,4]{0,1:T(4,128)S(1)} %fusion.134, f32[512,2,16,16]{0,2,3,1:T(8,128)S(1)} %fusion.3, f32[2,4,64,80]{3,2,1,0:T(8,128)S(1)} %copy-done), kind=kOutput, calls=%fused_computation.8 | convolution fusion | flops 203161600 | bytes 2170880 | tf_op jit(solution)/shard_map/stij,sjkc->stikc/dot_general | solution.py:64
  30.5 3.9 %fusion.1 = f32[512,2,16,16]{0,2,3,1:T(8,128)S(1)} fusion(f32[512,4]{0,1:T(4,128)S(1)} %fusion.136, f32[512,2,16,16]{0,2,3,1:T(8,128)S(1)} %fusion.2, f32[2,4,64,80]{3,2,1,0:T(8,128)S(1)} %copy-done), kind=kOutput, calls=%fused_computation.6 | convolution fusion | flops 203161600 | bytes 2170880 | tf_op jit(solution)/shard_map/stij,sjkc->stikc/dot_general | solution.py:64
  34.4 4.0 %fusion = f32[512,2,16,16]{0,2,3,1:T(8,128)S(1)} fusion(f32[512,4]{0,1:T(4,128)S(1)} %fusion.138, f32[512,2,16,16]{0,2,3,1:T(8,128)S(1)} %fusion.1, f32[2,4,64,80]{3,2,1,0:T(8,128)S(1)} %copy-done), kind=kOutput, calls=%fused_computation.4 | convolution fusion | flops 203161600 | bytes 2170880 | tf_op jit(solution)/shard_map/stij,sjkc->stikc/dot_general | solution.py:64
  42.6 2.3 %fusion.68 = (f32[2,8,16,4,512]{4,1,3,2,0:T(8,128)}, f32[2,8,16,512]{3,1,2,0:T(8,128)S(1)}) fusion(f32[2,8,16,4,512]{4,1,3,2,0:T(8,128)} %copy.330, f32[2,8,64,512]{3,1,2,0:T(8,128)S(1)} %copy.15, f32[8,512]{1,0:T(8,128)} %get-tuple-element.151, f32[2,8,16,511]{3,1,2,0:T(8,128)} %bitcast.655, f32[2,8,16,1]{3,1,2,0:T(8,128)} %collective-permute-done.1, ...), kind=kLoop, calls=%fused_computation.108 | loop fusion | flops 655360 | bytes 2785280 | tf_op jit(solution)/shard_map/scatter-add | solution.py:18
  45.0 3.6 %collective-permute-start.2 = (f32[2,8,16,1]{3,1,2,0:T(8,128)S(1)}, f32[2,8,16,1]{3,1,2,0:T(8,128)S(1)}, u32[]{:S(2)}, u32[]{:S(2)}) collective-permute-start(f32[2,8,16,1]{3,1,2,0:T(8,128)S(1)} %slice.232), channel_id=1, source_target_pairs={{1,0},{2,1},{3,2},{5,4},{6,5},{7,6},{9,8},{10,9},{11,10},{13,12},{... | collective-permute-start | bytes 3080 | tf_op jit(solution)/shard_map/ppermute | solution.py:12
  48.8 2.3 %collective-permute-done.2 = f32[2,8,16,1]{3,1,2,0:T(8,128)S(1)} collective-permute-done((f32[2,8,16,1]{3,1,2,0:T(8,128)S(1)}, f32[2,8,16,1]{3,1,2,0:T(8,128)S(1)}, u32[]{:S(2)}, u32[]{:S(2)}) %collective-permute-start.2) | collective-permute-done | bytes 1056 | tf_op jit(solution)/shard_map/ppermute | solution.py:12
  51.5 2.0 %fusion.65 = f32[2,8,16,4,512]{4,1,3,2,0:T(8,128)} fusion(f32[2,8,16,4,512]{4,1,3,2,0:T(8,128)} %get-tuple-element.140, f32[2,8,16,1,1]{4,1,3,2,0:T(8,128)S(1)} %copy.21, f32[2,8,16,1,511]{4,1,3,2,0:T(8,128)S(1)} %slice_bitcast_fusion), kind=kLoop, calls=%fused_computation.104 | loop fusion | flops 393216 | bytes 1572864 | tf_op jit(solution)/shard_map/scatter-add | solution.py:19
  53.5 8.9 %fusion.157 = (f32[2,1,64,512]{3,1,2,0:T(1,128)S(1)}, f32[2,1,64,512]{3,1,2,0:T(1,128)S(1)}, f32[2,1,64,512]{3,1,2,0:T(1,128)S(1)}, f32[2,1,64,512]{3,1,2,0:T(1,...) fusion(f32[2,8,64,512]{3,1,2,0:T(8,128)} %bitcast.651), kind=kLoop, calls=%fused_computation.241 | loop fusion | bytes 4194304 | tf_op jit(solution)/shard_map/slice | solution.py:54
  73.5 54.3 %while.16 = (s32[]{:T(128)}, f32[2,16,512]{2,1,0:T(8,128)}, f32[2,16,512]{2,1,0:T(8,128)S(1)}, pred[]{:T(512)}, f32[2,16,512]{2,1,0:T(8,128)S(1)}, /*index=5*/f3...) while((s32[]{:T(128)}, f32[2,16,512]{2,1,0:T(8,128)}, f32[2,16,512]{2,1,0:T(8,128)S(1)}, ...), condition=%wide.region_1.0_spmd, body=%wide.region_0.0_spmd.sunk | while | flops 540674 | bytes 2097306 | solution.py:80
  73.7 3.4 %collective-permute-start = (f32[2,16,512]{2,1,0:T(8,128)S(1)}, f32[2,16,512]{2,1,0:T(8,128)S(1)}, u32[]{:S(2)}, u32[]{:S(2)}) collective-permute-start(f32[2,16,512]{2,1,0:T(8,128)S(1)} %get-tuple-element.211), channel_id=1, source_target_pairs={{0,4},{4,8},{8,12},{12,16},{16,20},{20,24},{24,28},{1,5},{5,9},{9,... | collective-permute-start | bytes 196616 | tf_op jit(solution)/shard_map/while/body/eval_jaxpr/ppermute | solution.py:12
  77.1 3.7 %collective-permute-done = f32[2,16,512]{2,1,0:T(8,128)S(1)} collective-permute-done((f32[2,16,512]{2,1,0:T(8,128)S(1)}, f32[2,16,512]{2,1,0:T(8,128)S(1)}, u32[]{:S(2)}, u32[]{:S(2)}) %collective-permute-start) | collective-permute-done | bytes 65568 | tf_op jit(solution)/shard_map/while/body/eval_jaxpr/ppermute | solution.py:12
  81.4 2.5 %collective-permute-start = (f32[2,16,512]{2,1,0:T(8,128)S(1)}, f32[2,16,512]{2,1,0:T(8,128)S(1)}, u32[]{:S(2)}, u32[]{:S(2)}) collective-permute-start(f32[2,16,512]{2,1,0:T(8,128)S(1)} %get-tuple-element.211), channel_id=1, source_target_pairs={{0,4},{4,8},{8,12},{12,16},{16,20},{20,24},{24,28},{1,5},{5,9},{9,... | collective-permute-start | bytes 196616 | tf_op jit(solution)/shard_map/while/body/eval_jaxpr/ppermute | solution.py:12
  83.9 4.6 %collective-permute-done = f32[2,16,512]{2,1,0:T(8,128)S(1)} collective-permute-done((f32[2,16,512]{2,1,0:T(8,128)S(1)}, f32[2,16,512]{2,1,0:T(8,128)S(1)}, u32[]{:S(2)}, u32[]{:S(2)}) %collective-permute-start) | collective-permute-done | bytes 65568 | tf_op jit(solution)/shard_map/while/body/eval_jaxpr/ppermute | solution.py:12
  91.0 5.3 %collective-permute-done = f32[2,16,512]{2,1,0:T(8,128)S(1)} collective-permute-done((f32[2,16,512]{2,1,0:T(8,128)S(1)}, f32[2,16,512]{2,1,0:T(8,128)S(1)}, u32[]{:S(2)}, u32[]{:S(2)}) %collective-permute-start) | collective-permute-done | bytes 65568 | tf_op jit(solution)/shard_map/while/body/eval_jaxpr/ppermute | solution.py:12
  98.9 5.2 %collective-permute-done = f32[2,16,512]{2,1,0:T(8,128)S(1)} collective-permute-done((f32[2,16,512]{2,1,0:T(8,128)S(1)}, f32[2,16,512]{2,1,0:T(8,128)S(1)}, u32[]{:S(2)}, u32[]{:S(2)}) %collective-permute-start) | collective-permute-done | bytes 65568 | tf_op jit(solution)/shard_map/while/body/eval_jaxpr/ppermute | solution.py:12
  106.6 5.1 %collective-permute-done = f32[2,16,512]{2,1,0:T(8,128)S(1)} collective-permute-done((f32[2,16,512]{2,1,0:T(8,128)S(1)}, f32[2,16,512]{2,1,0:T(8,128)S(1)}, u32[]{:S(2)}, u32[]{:S(2)}) %collective-permute-start) | collective-permute-done | bytes 65568 | tf_op jit(solution)/shard_map/while/body/eval_jaxpr/ppermute | solution.py:12
  114.3 5.1 %collective-permute-done = f32[2,16,512]{2,1,0:T(8,128)S(1)} collective-permute-done((f32[2,16,512]{2,1,0:T(8,128)S(1)}, f32[2,16,512]{2,1,0:T(8,128)S(1)}, u32[]{:S(2)}, u32[]{:S(2)}) %collective-permute-start) | collective-permute-done | bytes 65568 | tf_op jit(solution)/shard_map/while/body/eval_jaxpr/ppermute | solution.py:12
  122.0 5.1 %collective-permute-done = f32[2,16,512]{2,1,0:T(8,128)S(1)} collective-permute-done((f32[2,16,512]{2,1,0:T(8,128)S(1)}, f32[2,16,512]{2,1,0:T(8,128)S(1)}, u32[]{:S(2)}, u32[]{:S(2)}) %collective-permute-start) | collective-permute-done | bytes 65568 | tf_op jit(solution)/shard_map/while/body/eval_jaxpr/ppermute | solution.py:12
  (137 shorter events, 44.1 us)
Async XLA Ops:
  0.0 6.4 %copy-start.19 = (f32[8,512]{1,0:T(8,128)S(1)}, f32[8,512]{1,0:T(8,128)}, u32[]{:S(2)}) copy-start(f32[8,512]{1,0:T(8,128)} %param.12) | copy-start | bytes 49156
  0.0 7.0 %copy-start.20 = (s32[8,512]{1,0:T(8,128)S(1)}, s32[8,512]{1,0:T(8,128)}, u32[]{:S(2)}) copy-start(s32[8,512]{1,0:T(8,128)} %param.13) | copy-start | bytes 49156
  0.0 7.2 %copy-start = (f32[2,4,64,80]{3,2,1,0:T(8,128)S(1)}, f32[2,4,64,80]{3,2,1,0:T(8,128)}, u32[]{:S(2)}) copy-start(f32[2,4,64,80]{3,2,1,0:T(8,128)} %param.15) | copy-start | bytes 491524
  4.5 38.2 %collective-permute-start.1 = (f32[2,8,16,1]{3,1,2,0:T(8,128)}, f32[2,8,16,1]{3,1,2,0:T(8,128)}, u32[]{:S(2)}, u32[]{:S(2)}) collective-permute-start(f32[2,8,16,1]{3,1,2,0:T(8,128)} %slice.228), channel_id=1, source_target_pairs={{0,1},{1,2},{2,3},{4,5},{5,6},{6,7},{8,9},{9,10},{10,11},{12,13},{... | collective-permute-start | bytes 3080 | tf_op jit(solution)/shard_map/ppermute | solution.py:12
  7.0 32.1 %copy-start.16 = (f32[512,4]{0,1:T(4,128)}, f32[512,4]{0,1:T(4,128)S(1)}, u32[]{:S(2)}) copy-start(f32[512,4]{0,1:T(4,128)S(1)} %fusion.123) | copy-start | bytes 24580
  7.1 7.9 %copy-start.14 = (f32[512,4]{0,1:T(4,128)}, f32[512,4]{0,1:T(4,128)S(1)}, u32[]{:S(2)}) copy-start(f32[512,4]{0,1:T(4,128)S(1)} %fusion.126) | copy-start | bytes 24580
  7.1 7.9 %copy-start.12 = (f32[512,4]{0,1:T(4,128)}, f32[512,4]{0,1:T(4,128)S(1)}, u32[]{:S(2)}) copy-start(f32[512,4]{0,1:T(4,128)S(1)} %fusion.128) | copy-start | bytes 24580
  7.1 11.7 %copy-start.10 = (f32[512,4]{0,1:T(4,128)}, f32[512,4]{0,1:T(4,128)S(1)}, u32[]{:S(2)}) copy-start(f32[512,4]{0,1:T(4,128)S(1)} %fusion.130) | copy-start | bytes 24580
  7.1 15.6 %copy-start.8 = (f32[512,4]{0,1:T(4,128)}, f32[512,4]{0,1:T(4,128)S(1)}, u32[]{:S(2)}) copy-start(f32[512,4]{0,1:T(4,128)S(1)} %fusion.132) | copy-start | bytes 24580
  7.1 19.4 %copy-start.6 = (f32[512,4]{0,1:T(4,128)}, f32[512,4]{0,1:T(4,128)S(1)}, u32[]{:S(2)}) copy-start(f32[512,4]{0,1:T(4,128)S(1)} %fusion.134) | copy-start | bytes 24580
  30.5 7.9 %copy-start.1 = (f32[2,16,512]{2,1,0:T(8,128)S(1)}, f32[2,16,512]{2,1,0:T(8,128)}, u32[]{:S(2)}) copy-start(f32[2,16,512]{2,1,0:T(8,128)} %param.14) | copy-start | bytes 196612
  45.0 6.1 %collective-permute-start.2 = (f32[2,8,16,1]{3,1,2,0:T(8,128)S(1)}, f32[2,8,16,1]{3,1,2,0:T(8,128)S(1)}, u32[]{:S(2)}, u32[]{:S(2)}) collective-permute-start(f32[2,8,16,1]{3,1,2,0:T(8,128)S(1)} %slice.232), channel_id=1, source_target_pairs={{1,0},{2,1},{3,2},{5,4},{6,5},{7,6},{9,8},{10,9},{11,10},{13,12},{... | collective-permute-start | bytes 3080 | tf_op jit(solution)/shard_map/ppermute | solution.py:12
  53.5 9.0 %copy-start.17 = (f32[512,4]{0,1:T(4,128)S(1)}, f32[512,4]{0,1:T(4,128)}, u32[]{:S(2)}) copy-start(f32[512,4]{0,1:T(4,128)} %copy-done.16) | copy-start | bytes 24580
  53.5 10.0 %copy-start.15 = (f32[512,4]{0,1:T(4,128)S(1)}, f32[512,4]{0,1:T(4,128)}, u32[]{:S(2)}) copy-start(f32[512,4]{0,1:T(4,128)} %copy-done.14) | copy-start | bytes 24580
  53.5 11.0 %copy-start.13 = (f32[512,4]{0,1:T(4,128)S(1)}, f32[512,4]{0,1:T(4,128)}, u32[]{:S(2)}) copy-start(f32[512,4]{0,1:T(4,128)} %copy-done.12) | copy-start | bytes 24580
  62.4 5.0 %copy-start.7 = (f32[512,4]{0,1:T(4,128)S(1)}, f32[512,4]{0,1:T(4,128)}, u32[]{:S(2)}) copy-start(f32[512,4]{0,1:T(4,128)} %copy-done.6) | copy-start | bytes 24580
  65.4 5.0 %copy-start.18 = (f32[512,2,16]{0,2,1:T(8,128)S(1)}, f32[512,2,16]{0,2,1:T(8,128)}, u32[]{:S(2)}) copy-start(f32[512,2,16]{0,2,1:T(8,128)} %fusion.48) | copy-start | bytes 196612
  73.7 7.1 %collective-permute-start = (f32[2,16,512]{2,1,0:T(8,128)S(1)}, f32[2,16,512]{2,1,0:T(8,128)S(1)}, u32[]{:S(2)}, u32[]{:S(2)}) collective-permute-start(f32[2,16,512]{2,1,0:T(8,128)S(1)} %get-tuple-element.211), channel_id=1, source_target_pairs={{0,4},{4,8},{8,12},{12,16},{16,20},{20,24},{24,28},{1,5},{5,9},{9,... | collective-permute-start | bytes 196616 | tf_op jit(solution)/shard_map/while/body/eval_jaxpr/ppermute | solution.py:12
  81.4 7.0 %collective-permute-start = (f32[2,16,512]{2,1,0:T(8,128)S(1)}, f32[2,16,512]{2,1,0:T(8,128)S(1)}, u32[]{:S(2)}, u32[]{:S(2)}) collective-permute-start(f32[2,16,512]{2,1,0:T(8,128)S(1)} %get-tuple-element.211), channel_id=1, source_target_pairs={{0,4},{4,8},{8,12},{12,16},{16,20},{20,24},{24,28},{1,5},{5,9},{9,... | collective-permute-start | bytes 196616 | tf_op jit(solution)/shard_map/while/body/eval_jaxpr/ppermute | solution.py:12
  89.1 7.2 %collective-permute-start = (f32[2,16,512]{2,1,0:T(8,128)S(1)}, f32[2,16,512]{2,1,0:T(8,128)S(1)}, u32[]{:S(2)}, u32[]{:S(2)}) collective-permute-start(f32[2,16,512]{2,1,0:T(8,128)S(1)} %get-tuple-element.211), channel_id=1, source_target_pairs={{0,4},{4,8},{8,12},{12,16},{16,20},{20,24},{24,28},{1,5},{5,9},{9,... | collective-permute-start | bytes 196616 | tf_op jit(solution)/shard_map/while/body/eval_jaxpr/ppermute | solution.py:12
  97.0 7.1 %collective-permute-start = (f32[2,16,512]{2,1,0:T(8,128)S(1)}, f32[2,16,512]{2,1,0:T(8,128)S(1)}, u32[]{:S(2)}, u32[]{:S(2)}) collective-permute-start(f32[2,16,512]{2,1,0:T(8,128)S(1)} %get-tuple-element.211), channel_id=1, source_target_pairs={{0,4},{4,8},{8,12},{12,16},{16,20},{20,24},{24,28},{1,5},{5,9},{9,... | collective-permute-start | bytes 196616 | tf_op jit(solution)/shard_map/while/body/eval_jaxpr/ppermute | solution.py:12
  104.7 7.0 %collective-permute-start = (f32[2,16,512]{2,1,0:T(8,128)S(1)}, f32[2,16,512]{2,1,0:T(8,128)S(1)}, u32[]{:S(2)}, u32[]{:S(2)}) collective-permute-start(f32[2,16,512]{2,1,0:T(8,128)S(1)} %get-tuple-element.211), channel_id=1, source_target_pairs={{0,4},{4,8},{8,12},{12,16},{16,20},{20,24},{24,28},{1,5},{5,9},{9,... | collective-permute-start | bytes 196616 | tf_op jit(solution)/shard_map/while/body/eval_jaxpr/ppermute | solution.py:12
  112.4 7.0 %collective-permute-start = (f32[2,16,512]{2,1,0:T(8,128)S(1)}, f32[2,16,512]{2,1,0:T(8,128)S(1)}, u32[]{:S(2)}, u32[]{:S(2)}) collective-permute-start(f32[2,16,512]{2,1,0:T(8,128)S(1)} %get-tuple-element.211), channel_id=1, source_target_pairs={{0,4},{4,8},{8,12},{12,16},{16,20},{20,24},{24,28},{1,5},{5,9},{9,... | collective-permute-start | bytes 196616 | tf_op jit(solution)/shard_map/while/body/eval_jaxpr/ppermute | solution.py:12
  120.1 7.0 %collective-permute-start = (f32[2,16,512]{2,1,0:T(8,128)S(1)}, f32[2,16,512]{2,1,0:T(8,128)S(1)}, u32[]{:S(2)}, u32[]{:S(2)}) collective-permute-start(f32[2,16,512]{2,1,0:T(8,128)S(1)} %get-tuple-element.211), channel_id=1, source_target_pairs={{0,4},{4,8},{8,12},{12,16},{16,20},{20,24},{24,28},{1,5},{5,9},{9,... | collective-permute-start | bytes 196616 | tf_op jit(solution)/shard_map/while/body/eval_jaxpr/ppermute | solution.py:12
  (12 other events, 18.5 us)
where the time goes:
time: 139 us; the launch traced here: 138 us
  matrix products  51.9 us (37%)
  waiting for transfers between devices  36.4 us (26%)
  starting transfers between devices  21 us (15%)
  local copies, waits for them, and re-layouts  20.1 us (14%)
  other arithmetic  7.78 us (6%)
    ppermute x9, waiting for transfers between devices, shifted(): return lax.ppermute(block, axis, route)  36.4 us
    dot_general x8, matrix products, on_device(): jnp.einsum('stij,sjkc->stikc', top_rows, slab_map, precision=precise)  31.1 us
    ppermute x9, starting transfers between devices, shifted(): return lax.ppermute(block, axis, route)  21 us
    dot_general x8, matrix products, on_device(): jnp.einsum('stij,sjc->stic', coupling_part, trace_in, precision=precise)  9.09 us
    slice x1, local copies, waits for them, and re-layouts, on_device(): source[:, level]  8.91 us
    dot_general x8, matrix products, on_device(): jnp.einsum('stij,sjc->stic', interior_part, source[:, level], precision=p...  7.9 us
    unnamed x43, local copies, waits for them, and re-layouts  5.69 us
    dot_general x8, matrix products, on_device(): moved = jnp.einsum('stij,sjc->stic', top_rows, offset, precision=precise)  3.85 us
  transfers between devices with their start and end apart: 9, of which 8 were waited for; matrix products, arithmetic and copies ran while one was open for 26% of the time, Pallas kernels for 0%

commit v1 on v0

v1 whole, which is shorter than its diff:
```python
import functools

import jax
import jax.numpy as jnp
from jax import lax
from jax.experimental import pallas as pl
from jax.experimental.pallas import tpu as pltpu
from jax.sharding import PartitionSpec as P

F32 = jnp.float32
BF16 = jnp.bfloat16
VMEM = pl.BlockSpec(memory_space=pltpu.VMEM)
ANY = pl.BlockSpec(memory_space=pl.ANY)


def lane_index(shape):
    return lax.broadcasted_iota(jnp.int32, shape, len(shape) - 1)


def split(x):
    hi = x.astype(BF16)
    return hi, (x - hi.astype(F32)).astype(BF16)


def stacked_parts(x):
    hi, lo = split(x)
    return jnp.concatenate([hi, lo, hi], axis=0)


def pick(per_type, types, rows):
    count = per_type.shape[0] // rows
    out = per_type[:rows]
    for t in range(1, count):
        out = jnp.where(types == t, per_type[t * rows : (t + 1) * rows], out)
    return out


def mm(a, b):
    return jnp.dot(a, b, preferred_element_type=F32)


def local_kernel(
    conc_hbm, vel_ref, type_ref, table_ref, s_ref, inner_ref, couple_ref, x_ref, sems
):
    species, levels, dofs, columns = x_ref.shape
    copies = []
    for s in range(species):
        for l in range(levels):
            k = s * levels + l
            copies.append(pltpu.make_async_copy(conc_hbm.at[s, l], x_ref.at[s, l], sems.at[k]))
            copies[-1].start()
    types_n, lanes = table_ref.shape[1], table_ref.shape[3]
    trace = couple_ref.shape[2] // 3
    for s in range(species):
        table = table_ref[s].reshape(types_n * dofs, lanes)
        hi = table.astype(BF16).astype(F32)
        lo = table - hi
        lane = lane_index(table.shape)
        twice = jnp.where(lane < dofs, hi, pltpu.roll(hi, dofs, 1))
        inner_ref[s] = jnp.concatenate([twice, lo[:, :dofs]], axis=1).astype(BF16)
        first = pltpu.roll(hi, lanes - dofs, 1)
        second = pltpu.roll(hi, lanes - dofs + trace, 1)
        third = pltpu.roll(lo, lanes - dofs + 2 * trace, 1)
        joined = jnp.where(lane < trace, first, jnp.where(lane < 2 * trace, second, third))
        couple_ref[s] = joined[:, : 3 * trace].astype(BF16)
    row = lax.broadcasted_iota(jnp.int32, (8, columns), 0) % 4
    lane = lane_index((8, columns))
    for l in range(levels):
        velocity = jnp.broadcast_to(vel_ref[l : l + 1], (8, columns))
        following = pltpu.roll(velocity, columns - 1, 1)
        following = jnp.where(lane == columns - 1, 0.0, following)
        own = 1.0 + jnp.where(
            row == 0,
            jnp.minimum(velocity, 0.0),
            jnp.where(row == 3, -jnp.maximum(following, 0.0), 0.0),
        )
        left = jnp.where((row == 0) & (lane > 0), jnp.maximum(velocity, 0.0), 0.0)
        right = jnp.where(row == 3, -jnp.minimum(following, 0.0), 0.0)
        types = type_ref[l : l + 1]
        for s in range(species):
            copies[s * levels + l].wait()
            x = x_ref[s, l].reshape(dofs // 8, 8, columns)
            up = pltpu.roll(pltpu.roll(x, 1, 2), 5, 1)
            down = pltpu.roll(pltpu.roll(x, columns - 1, 2), 3, 1)
            source = own[None] * x + left[None] * up + right[None] * down
            parts = stacked_parts(source.reshape(dofs, columns))
            s_ref[s, l] = pick(mm(inner_ref[s], parts), types, dofs)


def edge_kernel(
    top_rows, s_ref, type_ref, vel_ref, inlet_ref, inner_ref, couple_ref, own_ref, left_ref, right_ref,
    corr_ref, send_ref,
):
    species, levels, dofs, columns = s_ref.shape
    trace = inlet_ref.shape[1]
    pairs = species * levels
    types_n = inner_ref.shape[1] // dofs
    lat, lat_n = lax.axis_index("lat"), lax.axis_size("lat")
    has_left = (lat > 0).astype(F32)
    has_right = (lat < lat_n - 1).astype(F32)
    rim, nxt = left_ref[...] * has_left, right_ref[...] * has_right
    own_last = own_ref[pairs:]
    lanes = rim.shape[1]
    lane = lane_index(rim.shape)
    inside = lane < dofs
    own_vel = pltpu.roll(own_ref[:pairs], dofs, 1)
    nxt_vel = pltpu.roll(nxt, dofs, 1)
    first = jnp.where(
        inside & (lane % 4 == 0), jnp.maximum(own_vel, 0.0) * pltpu.roll(rim, lanes - 3, 1), 0.0
    )
    last = jnp.where(
        inside & (lane % 4 == 3),
        -(jnp.maximum(nxt_vel, 0.0) * own_last + jnp.minimum(nxt_vel, 0.0) * pltpu.roll(nxt, 3, 1)),
        0.0,
    )
    sub = lax.broadcasted_iota(jnp.int32, (levels, lanes), 0)
    on_diag = lane_index((levels, lanes)) % levels == sub
    types = type_ref[...]
    contract = (((1,), (1,)), ((), ()))
    for e, (delta, col) in enumerate(((first, 0), (last, columns - 1))):
        hi = delta.astype(BF16).astype(F32)
        lo = delta - hi
        parts = jnp.concatenate(
            [jnp.where(inside, hi, pltpu.roll(lo, dofs, 1)), hi[:, :dofs]], axis=1
        ).astype(BF16)
        edge_type = jnp.broadcast_to(types[:, col : col + 1], (levels, lanes))
        edge_type = jnp.sum(jnp.where(on_diag, edge_type, 0), axis=0, keepdims=True)[:, :pairs]
        for s in range(species):
            per_type = lax.dot_general(inner_ref[s], parts, contract, preferred_element_type=F32)
            corr_ref[e, s, :, :pairs] = pick(per_type, edge_type, dofs)
    flow = lax.axis_index("flow")
    start = (flow == 0).astype(F32)
    traces = [inlet_ref[s] * start for s in range(species)]
    for l in range(levels):
        tl = types[l : l + 1]
        for s in range(species):
            moved = pick(mm(top_rows(couple_ref, s), stacked_parts(traces[s])), tl, trace)
            fixed = edge_fix(corr_ref, s, l, levels, dofs - trace, trace, columns)
            traces[s] = moved + s_ref[s, l, dofs - trace :] + fixed
    width = send_ref.shape[2]
    if width == 128:
        half = width // 2
        low = lane_index((trace, width)) < half
        low_t = lane_index((levels, width)) < half
        ftypes = types.astype(F32)
        for k in range(columns // width):
            a, b = (traces[s][:, k * width : (k + 1) * width] for s in (0, 1))
            t = ftypes[:, k * width : (k + 1) * width]
            swapped = pltpu.roll(t, half, 1)
            send_ref[2 * k, :trace] = jnp.where(low, a, pltpu.roll(b, half, 1))
            send_ref[2 * k + 1, :trace] = jnp.where(low, pltpu.roll(a, half, 1), b)
            send_ref[2 * k, trace:] = jnp.where(low_t, t, swapped)
            send_ref[2 * k + 1, trace:] = jnp.where(low_t, swapped, t)
    else:
        for s in range(species):
            send_ref[s, :trace] = traces[s]
            send_ref[s, trace:] = types.astype(F32)


def edge_fix(corr_ref, s, l, levels, start, rows, columns):
    at = s * levels + l
    lane = lane_index((rows, 128))
    first = pltpu.roll(corr_ref[0, s, start : start + rows], (128 - at) % 128, 1)
    last = pltpu.roll(corr_ref[1, s, start : start + rows], 127 - at, 1)
    first = jnp.where(lane == 0, first, 0.0)
    last = jnp.where(lane == 127, last, 0.0)
    middle = jnp.zeros((rows, columns - 256), F32)
    return jnp.concatenate([first, middle, last], axis=1)


def owner_kernel(table_ref, got_ref, out_ref, coef_ref):
    slabs, _, width = got_ref.shape
    species, types_n, trace, _ = table_ref.shape
    levels = got_ref.shape[1] - trace
    half = width // species
    which = lane_index((trace, width)) // half
    for t in range(types_n):
        for j in range(trace):
            value = jnp.broadcast_to(table_ref[0, t, :, j : j + 1], (trace, width))
            for s in range(1, species):
                other = jnp.broadcast_to(table_ref[s, t, :, j : j + 1], (trace, width))
                value = jnp.where(which == s, other, value)
            coef_ref[t, j] = value
    out_ref[0] = jnp.zeros((trace, width), F32)

    def slab(g, state):
        out_ref[g] = state
        for l in range(levels):
            types = jnp.broadcast_to(got_ref[g, trace + l : trace + l + 1], (trace, width))
            chosen = [types == float(t) for t in range(1, types_n)]
            terms = []
            for j in range(trace):
                coef = coef_ref[0, j]
                for t in range(1, types_n):
                    coef = jnp.where(chosen[t - 1], coef_ref[t, j], coef)
                terms.append(coef * state[j : j + 1])
            while len(terms) > 1:
                terms = [a + b for a, b in zip(terms[::2], terms[1::2])]
            state = terms[0]
        return state + got_ref[g, :trace]

    last = lax.fori_loop(1, slabs - 1, slab, got_ref[0, :trace])
    out_ref[slabs - 1] = last


def final_kernel(
    s_ref, type_ref, inlet_ref, couple_ref, corr_ref, got_ref, out_hbm, o_ref, sems
):
    species, levels, dofs, columns = s_ref.shape
    trace = inlet_ref.shape[1]
    width = got_ref.shape[2]
    is_first = lax.axis_index("flow") == 0
    traces = []
    if width == 128:
        half = width // 2
        low = lane_index((trace, width)) < half
        tiles = [[], []]
        for k in range(columns // width):
            a, b = got_ref[2 * k], got_ref[2 * k + 1]
            tiles[0].append(jnp.where(low, a, pltpu.roll(b, half, 1)))
            tiles[1].append(jnp.where(low, pltpu.roll(a, half, 1), b))
        received = [jnp.concatenate(t, axis=1) for t in tiles]
    else:
        received = [got_ref[s] for s in range(species)]
    traces = [jnp.where(is_first, inlet_ref[s], received[s]) for s in range(species)]
    copies = []
    for l in range(levels):
        types = type_ref[l : l + 1]
        for s in range(species):
            moved = pick(mm(couple_ref[s], stacked_parts(traces[s])), types, dofs)
            out = moved + s_ref[s, l] + edge_fix(corr_ref, s, l, levels, 0, dofs, columns)
            traces[s] = out[dofs - trace :]
            o_ref[s, l] = out.astype(BF16)
            copies.append(
                pltpu.make_async_copy(o_ref.at[s, l], out_hbm.at[s, l], sems.at[s * levels + l])
            )
            copies[-1].start()
    for copy in copies:
        copy.wait()


def on_device(conc_old, lat_velocity, elem_type, inlet_trace, solve_table):
    species, levels, dofs, columns = conc_old.shape
    types_n = solve_table.shape[1]
    trace = inlet_trace.shape[1]
    flow_n = lax.axis_size("flow")
    lat_n = lax.axis_size("lat")
    pairs = species * levels
    shape = jax.ShapeDtypeStruct

    face = jnp.broadcast_to(lat_velocity[None, :, :1], (species, levels, dofs)).reshape(pairs, dofs)
    first = jnp.concatenate([conc_old[:, :, :, 0].reshape(pairs, dofs), face], axis=1)
    last = jnp.concatenate([conc_old[:, :, :, columns - 1].reshape(pairs, dofs), face], axis=1)
    from_left = lax.ppermute(last, "lat", [(i, (i + 1) % lat_n) for i in range(lat_n)])
    from_right = lax.ppermute(first, "lat", [((i + 1) % lat_n, i) for i in range(lat_n)])
    own = jnp.concatenate([first, last], axis=0)

    table = jnp.pad(solve_table, ((0, 0), (0, 0), (0, 0), (0, 128 - dofs - trace)))
    source, inner, couple = pl.pallas_call(
        local_kernel,
        out_shape=(
            shape((species, levels, dofs, columns), F32),
            shape((species, types_n * dofs, 3 * dofs), BF16),
            shape((species, types_n * dofs, 3 * trace), BF16),
        ),
        in_specs=[ANY, VMEM, VMEM, VMEM],
        out_specs=(VMEM, VMEM, VMEM),
        scratch_shapes=[
            pltpu.VMEM((species, levels, dofs, columns), F32),
            pltpu.SemaphoreType.DMA((pairs,)),
        ],
        cost_estimate=pl.CostEstimate(
            flops=2 * 3 * types_n * dofs * dofs * columns * pairs,
            bytes_accessed=8 * species * levels * dofs * columns,
            transcendentals=0,
        ),
        name="local_sources",
    )(conc_old, lat_velocity, elem_type, table)

    packed = 2 * columns == 128 * flow_n and species == 2

    def top_rows(couple_ref, s):
        return jnp.concatenate(
            [couple_ref[s, (t + 1) * dofs - trace : (t + 1) * dofs] for t in range(types_n)], axis=0
        )

    send_shape = (flow_n, trace + levels, 128) if packed else (species, trace + levels, columns)
    corr, send = pl.pallas_call(
        functools.partial(edge_kernel, top_rows),
        out_shape=(shape((2, species, dofs, 128), F32), shape(send_shape, F32)),
        in_specs=[VMEM] * 9,
        out_specs=(VMEM, VMEM),
        name="edge_offsets",
    )(source, elem_type, lat_velocity, inlet_trace, inner, couple, own, from_left, from_right)
    if not packed:
        part = columns // flow_n
        send = send.reshape(species, trace + levels, flow_n, part)
        send = send.transpose(2, 1, 0, 3).reshape(flow_n, trace + levels, species * part)
    got = lax.all_to_all(send, "flow", 0, 0, tiled=True)

    top_table = solve_table[:, :, dofs - trace :, dofs:]
    back = pl.pallas_call(
        owner_kernel,
        out_shape=shape((flow_n, trace, got.shape[2]), F32),
        in_specs=[VMEM, VMEM],
        out_specs=VMEM,
        scratch_shapes=[pltpu.VMEM((types_n, trace, trace, got.shape[2]), F32)],
        name="owner_sweep",
    )(top_table, got)
    traces = lax.all_to_all(back, "flow", 0, 0, tiled=True)
    if not packed:
        traces = traces.reshape(flow_n, trace, species, part)
        traces = traces.transpose(2, 1, 0, 3).reshape(species, trace, columns)

    return pl.pallas_call(
        final_kernel,
        out_shape=shape((species, levels, dofs, columns), BF16),
        in_specs=[VMEM] * 6,
        out_specs=ANY,
        scratch_shapes=[
            pltpu.VMEM((species, levels, dofs, columns), BF16),
            pltpu.SemaphoreType.DMA((pairs,)),
        ],
        name="final_sweep",
    )(source, elem_type, inlet_trace, couple, corr, traces)


def solution(mesh):
    in_specs = (
        P(None, "flow", None, "lat"),
        P("flow", "lat"),
        P("flow", "lat"),
        P(None, None, "lat"),
        P(),
    )
    out_specs = P(None, "flow", None, "lat")
    return jax.shard_map(
        on_device, mesh=mesh, in_specs=in_specs, out_specs=out_specs, check_vma=False
    )
```

time: 139 us -> 53.5 us (0.38)
  the two profiles are of different devices: /device:TPU:28 before, /device:TPU:0 now
where the time goes in v1:
time: 53.5 us; the launch traced here: 53 us
  Pallas kernels  20.9 us (39%)
  blocking collectives  10.9 us (20%)
  starting transfers between devices  8.26 us (15%)
  waiting for transfers between devices  6.69 us (13%)
  local copies, waits for them, and re-layouts  5.5 us (10%)
  other arithmetic  0.76 us (1%)
    all_to_all x1, blocking collectives, on_device(): traces = lax.all_to_all(back, 'flow', 0, 0, tiled=True)  10.9 us
    pallas_call x1, Pallas kernels, on_device(): pl.pallas_call(local_kernel, out_shape=(shape((species, levels, dofs, col...  9.13 us
    all_to_all x1, waiting for transfers between devices, on_device(): got = lax.all_to_all(send, 'flow', 0, 0, tiled=True)  6.68 us
    all_to_all x1, starting transfers between devices, on_device(): got = lax.all_to_all(send, 'flow', 0, 0, tiled=True)  5.8 us
    pallas_call x1, Pallas kernels, on_device(): pl.pallas_call(final_kernel, out_shape=shape((species, levels, dofs, colu...  4.34 us
    pallas_call x1, Pallas kernels, on_device(): pl.pallas_call(functools.partial(edge_kernel, top_rows), out_shape=(shape...  4.04 us
    pallas_call x1, Pallas kernels, on_device(): pl.pallas_call(owner_kernel, out_shape=shape((flow_n, trace, got.shape[2]...  3.42 us
    ppermute x1, starting transfers between devices, on_device(): lax.ppermute(first, 'lat', [((i + 1) % lat_n, i) for i in range(lat_n)])  2.46 us
  transfers between devices with their start and end apart: 3, of which 1 were waited for; matrix products, arithmetic and copies ran while one was open for 4% of the time, Pallas kernels for 17%

profile of v1, /device:TPU:0, one launch (start us, length us, event | category | flops | bytes accessed | tf_op | source)
XLA Modules:
  0.0 53.0 jit_solution(3938928291405847742)
XLA Ops:
  0.0 0.8 %slice_reduce_fusion = f32[8]{0:T(128)S(1)} fusion(f32[8,512]{1,0:T(8,128)} %vel_ref.3), kind=kLoop, calls=%fused_computation.3 | loop fusion | bytes 64 | tf_op jit(solution)/shard_map/slice | solution.py:251
  0.9 0.1 broadcast_in_dim.14
  0.9 1.4 %fusion = (f32[2,8,64,1]{3,2,1,0:T(8,128)S(1)}, f32[2,8,64,1]{3,2,1,0:T(8,128)S(1)}) fusion(f32[2,8,64,512]{3,2,1,0:T(8,128)} %conc_hbm.1), kind=kLoop, calls=%fused_computation.4 | loop fusion | bytes 16384 | tf_op jit(solution)/shard_map/slice | solution.py:252
  2.4 0.2 copy.8
  2.6 0.2 copy.9
  2.8 0.1 broadcast_in_dim.15
  2.8 0.1 pad_maximum_fusion
  2.9 2.5 %collective-permute-start.1 = (f32[16,128]{1,0:T(8,128)S(1)}, f32[16,128]{1,0:T(8,128)S(1)}, u32[]{:S(2)}, u32[]{:S(2)}) collective-permute-start(f32[16,128]{1,0:T(8,128)S(1)} %get-tuple-element.17), channel_id=1, source_target_pairs={{1,0},{2,1},{3,2},{0,3},{5,4},{6,5},{7,6},{4,7},{9,8},{10,9},{11,1... | collective-permute-start | bytes 24584 | tf_op jit(solution)/shard_map/ppermute | solution.py:255
  5.4 0.0 collective-permute-start
  5.4 0.7 %maximum_maximum_fusion.own_ref = f32[32,128]{1,0:T(8,128)} fusion(f32[16,64]{1,0:T(8,128)S(1)} %broadcast_in_dim.15, f32[16,64]{1,0:T(8,128)S(1)} %bitcast.5, f32[16,64]{1,0:T(8,128)S(1)} %bitcast.3), kind=kLoop, calls=%fused_computation | loop fusion | flops 12288 | bytes 28672 | tf_op jit(solution)/shard_map/concatenate | solution.py:256
  6.1 0.7 %pad.4.table_ref = f32[2,4,64,128]{3,2,1,0:T(8,128)} pad(f32[2,4,64,80]{3,2,1,0:T(8,128)S(1)} %copy-done, f32[]{:T(128)} %constant.2.clone.1), padding=0_0x0_0x0_0x0_48 | pad | bytes 425988 | tf_op jit(solution)/shard_map/jit(_pad)/pad | solution.py:258
  6.8 9.1 %local_sources.1 = (f32[2,8,64,512]{3,2,1,0:T(8,128)}, bf16[2,256,192]{2,1,0:T(8,128)(2,1)}, bf16[2,256,48]{2,1,0:T(8,128)(2,1)}) custom-call(f32[2,8,64,512]{3,2,1,0:T(8,128)} %conc_hbm.1, f32[8,512]{1,0:T(8,128)} %vel_ref.3, s32[8,512]{1,0:T(8,128)} %type_ref.5, f32[2,4,64,128]{3,2,1,0:T(8,128)} %pad.4.table_ref), custom_call_target="tpu_custom_call" | custom-call | flops 805306368 | bytes 4194304 | tf_op jit(solution)/shard_map/local_sources/pallas_call | solution.py:259
  15.9 0.0 collective-permute-done.1.right_ref
  15.9 0.0 collective-permute-done.left_ref
  16.0 0.6 %copy-done.2 = f32[16,128]{1,0:T(8,128)} copy-done((f32[16,128]{1,0:T(8,128)}, f32[16,128]{1,0:T(8,128)S(1)}, u32[]{:S(2)}) %copy-start.2) | copy-done | bytes 8216
  16.5 0.0 copy-done.3
  16.5 4.0 %edge_offsets.1 = (f32[2,2,64,128]{3,2,1,0:T(8,128)}, f32[8,24,128]{2,1,0:T(8,128)}) custom-call(f32[2,8,64,512]{3,2,1,0:T(8,128)} %get-tuple-element.10.s_ref, s32[8,512]{1,0:T(8,128)} %type_ref.5, f32[8,512]{1,0:T(8,128)} %vel_ref.3, f32[2,16,512]{2,1,0:T(8,128)} %inlet_ref.3, bf16[2,256,192]{2,1,0:T(8,128)(2,1)} %get-tuple-element.12.inner_ref, ...), custom_call_target="tpu_custom_call" | custom-call | tf_op jit(solution)/shard_map/edge_offsets/pallas_call | solution.py:288
  20.6 5.8 %all-to-all-start = ((f32[8,24,128]{2,1,0:T(8,128)}), f32[8,24,128]{2,1,0:T(8,128)S(1)}, u32[]{:S(2)}, u32[]{:S(2)}) async-start(f32[8,24,128]{2,1,0:T(8,128)} %get-tuple-element.14), calls=%async_computation | async-start | bytes 196608 | tf_op jit(solution)/shard_map/all_to_all | solution.py:299
  26.4 0.7 %slice.15.table_ref = f32[2,4,16,16]{3,2,1,0:T(8,128)} slice(f32[2,4,64,80]{3,2,1,0:T(8,128)S(1)} %copy-done), slice={[0:2], [0:4], [48:64], [64:80]} | slice | bytes 16384 | tf_op jit(solution)/shard_map/slice | solution.py:301
  27.1 6.7 %all-to-all-done.got_ref = f32[8,24,128]{2,1,0:T(8,128)S(1)} async-done(((f32[8,24,128]{2,1,0:T(8,128)}), f32[8,24,128]{2,1,0:T(8,128)S(1)}, u32[]{:S(2)}, u32[]{:S(2)}) %all-to-all-start) | async-done | bytes 98336 | tf_op jit(solution)/shard_map/all_to_all | solution.py:299
  33.8 0.6 %copy-done.1 = f32[8,24,128]{2,1,0:T(8,128)} copy-done((f32[8,24,128]{2,1,0:T(8,128)}, f32[8,24,128]{2,1,0:T(8,128)S(1)}, u32[]{:S(2)}) %copy-start.1) | copy-done | bytes 98328
  34.4 3.4 %owner_sweep.1 = f32[8,16,128]{2,1,0:T(8,128)} custom-call(f32[2,4,16,16]{3,2,1,0:T(8,128)} %slice.15.table_ref, f32[8,24,128]{2,1,0:T(8,128)} %copy-done.1), custom_call_target="tpu_custom_call" | custom-call | tf_op jit(solution)/shard_map/owner_sweep/pallas_call | solution.py:302
  37.8 10.9 %all_to_all.10.got_ref = f32[8,16,128]{2,1,0:T(8,128)} all-to-all(f32[8,16,128]{2,1,0:T(8,128)} %owner_sweep.1), channel_id=1, replica_groups=mesh['flow'=8,'lat'=4] {'flow'}, dimensions={0} | all-to-all | bytes 131072 | tf_op jit(solution)/shard_map/all_to_all | solution.py:310
  48.7 4.3 %final_sweep.1 = bf16[2,8,64,512]{3,2,1,0:T(8,128)(2,1)} custom-call(f32[2,8,64,512]{3,2,1,0:T(8,128)} %get-tuple-element.10.s_ref, s32[8,512]{1,0:T(8,128)} %type_ref.5, f32[2,16,512]{2,1,0:T(8,128)} %inlet_ref.3, bf16[2,256,48]{2,1,0:T(8,128)(2,1)} %get-tuple-element.11.couple_ref, f32[2,2,64,128]{3,2,1,0:T(8,128)} %get-tuple-element.13.corr_ref, ...), custom_call_target="tpu_custom_call" | custom-call | tf_op jit(solution)/shard_map/final_sweep/pallas_call | solution.py:315
  (6 shorter events, 0.0 us)
Async XLA Ops:
  0.0 6.1 %copy-start = (f32[2,4,64,80]{3,2,1,0:T(8,128)S(1)}, f32[2,4,64,80]{3,2,1,0:T(8,128)}, u32[]{:S(2)}) copy-start(f32[2,4,64,80]{3,2,1,0:T(8,128)} %param.9) | copy-start | bytes 491524
  2.9 13.0 %collective-permute-start.1 = (f32[16,128]{1,0:T(8,128)S(1)}, f32[16,128]{1,0:T(8,128)S(1)}, u32[]{:S(2)}, u32[]{:S(2)}) collective-permute-start(f32[16,128]{1,0:T(8,128)S(1)} %get-tuple-element.17), channel_id=1, source_target_pairs={{1,0},{2,1},{3,2},{0,3},{5,4},{6,5},{7,6},{4,7},{9,8},{10,9},{11,1... | collective-permute-start | bytes 24584 | tf_op jit(solution)/shard_map/ppermute | solution.py:255
  5.4 10.6 %collective-permute-start = (f32[16,128]{1,0:T(8,128)S(1)}, f32[16,128]{1,0:T(8,128)S(1)}, u32[]{:S(2)}, u32[]{:S(2)}) collective-permute-start(f32[16,128]{1,0:T(8,128)S(1)} %get-tuple-element.18), channel_id=1, source_target_pairs={{0,1},{1,2},{2,3},{3,0},{4,5},{5,6},{6,7},{7,4},{8,9},{9,10},{10,1... | collective-permute-start | bytes 24584 | tf_op jit(solution)/shard_map/ppermute | solution.py:254
  15.9 0.6 %copy-start.2 = (f32[16,128]{1,0:T(8,128)}, f32[16,128]{1,0:T(8,128)S(1)}, u32[]{:S(2)}) copy-start(f32[16,128]{1,0:T(8,128)S(1)} %collective-permute-done.1.right_ref) | copy-start | bytes 24580
  16.0 0.6 %copy-start.3 = (f32[16,128]{1,0:T(8,128)}, f32[16,128]{1,0:T(8,128)S(1)}, u32[]{:S(2)}) copy-start(f32[16,128]{1,0:T(8,128)S(1)} %collective-permute-done.left_ref) | copy-start | bytes 24580
  20.6 13.2 %all-to-all-start = ((f32[8,24,128]{2,1,0:T(8,128)}), f32[8,24,128]{2,1,0:T(8,128)S(1)}, u32[]{:S(2)}, u32[]{:S(2)}) async-start(f32[8,24,128]{2,1,0:T(8,128)} %get-tuple-element.14), calls=%async_computation | async-start | bytes 196608 | tf_op jit(solution)/shard_map/all_to_all | solution.py:299
  33.8 0.6 %copy-start.1 = (f32[8,24,128]{2,1,0:T(8,128)}, f32[8,24,128]{2,1,0:T(8,128)S(1)}, u32[]{:S(2)}) copy-start(f32[8,24,128]{2,1,0:T(8,128)S(1)} %all-to-all-done.got_ref) | copy-start | bytes 294916

commit v2 on v1

v2 whole, which is shorter than its diff:
```python
import jax
import jax.numpy as jnp
from jax import lax
from jax.experimental import pallas as pl
from jax.experimental.pallas import tpu as pltpu
from jax.sharding import PartitionSpec as P

F32 = jnp.float32
BF16 = jnp.bfloat16
VMEM = pl.BlockSpec(memory_space=pltpu.VMEM)
ANY = pl.BlockSpec(memory_space=pl.ANY)
LANES = 128
PARAMS = pltpu.CompilerParams(vmem_limit_bytes=20 << 20)


def lane_index(shape):
    return lax.broadcasted_iota(jnp.int32, shape, len(shape) - 1)


def split(x):
    hi = x.astype(BF16)
    return hi, (x - hi.astype(F32)).astype(BF16)


def stacked_parts(x):
    hi, lo = split(x)
    return jnp.concatenate([hi, lo, hi], axis=0)


def pick(per_type, types, rows):
    columns = per_type.shape[1]
    grid = per_type.reshape(-1, rows // 8, 8, columns)
    out = grid[0]
    for t in range(1, grid.shape[0]):
        out = jnp.where((types == t)[None], grid[t], out)
    return out.reshape(rows, columns)


def masked_parts(x, onehot_ref, level):
    hi, lo = split(x)
    parts = []
    for t in range(onehot_ref.shape[1]):
        mask = onehot_ref[level, t]
        his = hi * mask
        parts += [his, lo * mask, his]
    return jnp.concatenate(parts, axis=0)


def mm(a, b):
    return jnp.dot(a, b, preferred_element_type=F32)


def load_kernel(conc_hbm, vel_ref, x_ref, right_ref, left_ref, sems):
    species, tiles, levels, dofs, _ = x_ref.shape
    trace = right_ref.shape[0]
    stride = dofs // trace
    copies = []
    for k in [0, tiles - 1, *range(1, tiles - 1)]:
        for s in range(species):
            block = conc_hbm.at[s, :, :, pl.ds(k * LANES, LANES)]
            copies.append(pltpu.make_async_copy(block, x_ref.at[s, k], sems.at[s * tiles + k]))
            copies[-1].start()
    lane = lane_index((levels, LANES))
    on_diag = lane % levels == lax.broadcasted_iota(jnp.int32, lane.shape, 0)
    face = jnp.broadcast_to(vel_ref[:, :1], (levels, LANES))
    face = jnp.sum(jnp.where(on_diag, face, 0.0), axis=0, keepdims=True)
    left_ref[trace:] = jnp.broadcast_to(face, (left_ref.shape[0] - trace, LANES))
    for copy in copies[: 2 * species]:
        copy.wait()
    lane = lane_index((trace, LANES))
    right = jnp.zeros((trace, LANES), F32)
    left = jnp.zeros((trace, LANES), F32)
    for p in range(species * levels):
        s, l = p // levels, p % levels
        last = x_ref[s, tiles - 1, l, pl.ds(stride - 1, trace, stride=stride), :]
        first = x_ref[s, 0, l, pl.ds(0, trace, stride=stride), :]
        right = jnp.where(lane == p, pltpu.roll(last, (p + 1) % LANES, 1), right)
        left = jnp.where(lane == p, pltpu.roll(first, p, 1) if p else first, left)
    right_ref[...] = right
    left_ref[:trace] = left
    for copy in copies[2 * species :]:
        copy.wait()


def inner_kernel(
    x_ref, vel_ref, type_ref, table_ref, mid_ref, rim_ref, top_ref, a_top_ref, a_rest_ref, c_ref, onehot_ref,
    delta_ref,
):
    species, tiles_n, levels, dofs, _ = x_ref.shape
    columns = tiles_n * LANES
    types_n, trace = onehot_ref.shape[1], onehot_ref.shape[2]
    stride = dofs // trace
    rest = dofs - trace
    for s in range(species):
        tops, rests = [], []
        pieces = [[], [], []]
        for t in range(types_n):
            table = table_ref[s, t]
            hi = table.astype(BF16).astype(F32)
            lo = table - hi
            lane = lane_index(table.shape)
            twice = jnp.where(lane < dofs, hi, pltpu.roll(hi, dofs, 1))
            wide = jnp.concatenate([twice, lo[:, :dofs]], axis=1).astype(BF16)
            tops.append(wide[rest:])
            rests.append(wide[:rest])
            pieces[0].append(hi)
            pieces[2].append(lo)
        a_top_ref[s] = jnp.concatenate(tops, axis=0)
        a_rest_ref[s] = jnp.concatenate(rests, axis=0)
        pieces[1] = pieces[0]
        count = 3 * types_n * trace
        tiles = []
        for start in range(0, count, LANES):
            lane = lane_index((dofs, LANES))
            tile = jnp.zeros((dofs, LANES), F32)
            for at in range(start, min(count, start + LANES), trace):
                k = at // trace
                piece = pltpu.roll(pieces[k % 3][k // 3], (at - start - dofs) % LANES, 1)
                inside = (lane >= at - start) & (lane < at - start + trace)
                tile = jnp.where(inside, piece, tile)
            tiles.append(jnp.concatenate([tile[rest:], tile[:rest]], axis=0).astype(BF16))
        c_ref[s] = jnp.concatenate(tiles, axis=1)[:, :count]
    for k in range(delta_ref.shape[0]):
        delta_ref[k] = jnp.zeros((tiles_n, dofs, LANES), F32)
    lane = lane_index((trace, columns))
    for l in range(levels):
        velocity = jnp.broadcast_to(vel_ref[l : l + 1], (trace, columns))
        plus = jnp.where(lane > 0, jnp.maximum(velocity, 0.0), 0.0)
        minus = jnp.minimum(velocity, 0.0)
        types = jnp.broadcast_to(type_ref[l : l + 1], (trace, columns))
        for t in range(types_n):
            onehot_ref[l, t] = jnp.where(types == t, 1.0, 0.0).astype(BF16)
        types_mid = types[:8, LANES : columns - LANES]
        for s in range(species):
            k = (l * species + s) % delta_ref.shape[0]
            zero, three = pl.ds(0, trace, stride=stride), pl.ds(stride - 1, trace, stride=stride)
            low = jnp.concatenate([x_ref[s, i, l, zero, :] for i in range(tiles_n)], axis=1)
            high = jnp.concatenate([x_ref[s, i, l, three, :] for i in range(tiles_n)], axis=1)
            flux = plus * pltpu.roll(high, 1, 1) + minus * low
            out = jnp.where(lane == columns - 1, 0.0, -pltpu.roll(flux, columns - 1, 1))
            source = []
            for i in range(tiles_n):
                delta_ref[k, i, zero, :] = flux[:, i * LANES : (i + 1) * LANES]
                delta_ref[k, i, three, :] = out[:, i * LANES : (i + 1) * LANES]
                source.append(x_ref[s, i, l] + delta_ref[k, i])
            mid = jnp.concatenate(source[1:-1], axis=1)
            mid_ref[s, l] = mid
            rim_ref[s, l, 0] = source[0]
            rim_ref[s, l, 1] = source[-1]
            top_ref[s, l] = pick(mm(a_top_ref[s], stacked_parts(mid)), types_mid, trace)


def offset_kernel(
    rim_ref, mid_top_ref, type_ref, onehot_ref, inlet_ref, a_top_ref, c_ref, own_right_ref, own_left_ref, from_left_ref,
    from_right_ref, edge_ref, top_ref, send_ref,
):
    species, levels, trace, columns = top_ref.shape
    dofs = rim_ref.shape[3]
    stride = dofs // trace
    lat, lat_n = lax.axis_index("lat"), lax.axis_size("lat")
    has_left = (lat > 0).astype(F32)
    has_right = (lat < lat_n - 1).astype(F32)

    def face(ref):
        return jnp.broadcast_to(ref[trace : trace + 1], (trace, LANES))

    coming = jnp.maximum(face(own_left_ref), 0.0) * from_left_ref[...] * has_left
    velocity = face(from_right_ref)
    leaving = jnp.maximum(velocity, 0.0) * own_right_ref[...]
    leaving = (leaving + jnp.minimum(velocity, 0.0) * from_right_ref[:trace]) * has_right
    lane = lane_index((trace, LANES))
    for l in range(levels):
        for s in range(species):
            p = s * levels + l
            first = jnp.where(lane == 0, pltpu.roll(coming, (LANES - p) % LANES, 1), 0.0)
            last = jnp.where(lane == LANES - 1, pltpu.roll(leaving, LANES - 1 - p, 1), 0.0)
            low, high = pl.ds(0, trace, stride=stride), pl.ds(stride - 1, trace, stride=stride)
            edge_ref[s, l] = rim_ref[s, l]
            edge_ref[s, l, 0, low, :] = rim_ref[s, l, 0, low, :] + first
            edge_ref[s, l, 1, high, :] = rim_ref[s, l, 1, high, :] - last
    for l in range(levels):
        types = jnp.broadcast_to(type_ref[l : l + 1], (8, columns))
        rim_types = jnp.concatenate([types[:, :LANES], types[:, columns - LANES :]], axis=1)
        for s in range(species):
            source = jnp.concatenate([edge_ref[s, l, 0], edge_ref[s, l, 1]], axis=1)
            top = pick(mm(a_top_ref[s], stacked_parts(source)), rim_types, trace)
            top_ref[s, l] = jnp.concatenate([top[:, :LANES], mid_top_ref[s, l], top[:, LANES:]], axis=1)
    start = (lax.axis_index("flow") == 0).astype(F32)
    traces = [inlet_ref[s] * start for s in range(species)]
    for l in range(levels):
        for s in range(species):
            moved = mm(c_ref[s, :trace], masked_parts(traces[s], onehot_ref, l))
            traces[s] = moved + top_ref[s, l]
    width = send_ref.shape[2]
    types = type_ref[...].astype(F32)
    if width == LANES:
        half = width // 2
        low = lane_index((trace, width)) < half
        low_t = lane_index((levels, width)) < half
        for k in range(columns // width):
            a, b = (traces[s][:, k * width : (k + 1) * width] for s in (0, 1))
            t = types[:, k * width : (k + 1) * width]
            swapped = pltpu.roll(t, half, 1)
            send_ref[2 * k, :trace] = jnp.where(low, a, pltpu.roll(b, half, 1))
            send_ref[2 * k + 1, :trace] = jnp.where(low, pltpu.roll(a, half, 1), b)
            send_ref[2 * k, trace:] = jnp.where(low_t, t, swapped)
            send_ref[2 * k + 1, trace:] = jnp.where(low_t, swapped, t)
    else:
        for s in range(species):
            send_ref[s, :trace] = traces[s]
            send_ref[s, trace:] = types


def rest_kernel(mid_ref, edge_ref, type_ref, a_rest_ref, table_ref, rest_ref, coef_ref):
    species, levels, rest, columns = rest_ref.shape
    types_n, trace, width = coef_ref.shape[0], coef_ref.shape[1], coef_ref.shape[3]
    dofs = rest + trace
    half = width // species
    which = lane_index((trace, width)) // half
    for t in range(types_n):
        for j in range(trace):
            column = slice(dofs + j, dofs + j + 1)
            value = jnp.broadcast_to(table_ref[0, t, rest:, column], (trace, width))
            for s in range(1, species):
                other = jnp.broadcast_to(table_ref[s, t, rest:, column], (trace, width))
                value = jnp.where(which == s, other, value)
            coef_ref[t, j] = value
    for l in range(levels):
        types = jnp.broadcast_to(type_ref[l : l + 1], (8, columns))
        for s in range(species):
            source = jnp.concatenate([edge_ref[s, l, 0], mid_ref[s, l], edge_ref[s, l, 1]], axis=1)
            rest_ref[s, l] = pick(mm(a_rest_ref[s], stacked_parts(source)), types, rest)


def owner_kernel(coef_ref, got_ref, out_ref):
    slabs, _, width = got_ref.shape
    types_n, trace = coef_ref.shape[:2]
    levels = got_ref.shape[1] - trace
    out_ref[0] = jnp.zeros((trace, width), F32)

    def slab(g, state):
        out_ref[g] = state
        for l in range(levels):
            types = jnp.broadcast_to(got_ref[g, trace + l : trace + l + 1], (trace, width))
            chosen = [types == float(t) for t in range(1, types_n)]
            terms = []
            for j in range(trace):
                coef = coef_ref[0, j]
                for t in range(1, types_n):
                    coef = jnp.where(chosen[t - 1], coef_ref[t, j], coef)
                terms.append(coef * state[j : j + 1])
            while len(terms) > 1:
                terms = [a + b for a, b in zip(terms[::2], terms[1::2])]
            state = terms[0]
        return state + got_ref[g, :trace]

    last = lax.fori_loop(1, slabs - 1, slab, got_ref[0, :trace])
    out_ref[slabs - 1] = last


def final_kernel(top_ref, rest_ref, onehot_ref, inlet_ref, c_ref, got_ref, out_hbm, o_ref, sems):
    species, levels, trace, columns = top_ref.shape
    rest = rest_ref.shape[2]
    width = got_ref.shape[2]
    is_first = lax.axis_index("flow") == 0
    if width == LANES:
        half = width // 2
        low = lane_index((trace, width)) < half
        tiles = [[], []]
        for k in range(columns // width):
            a, b = got_ref[2 * k], got_ref[2 * k + 1]
            tiles[0].append(jnp.where(low, a, pltpu.roll(b, half, 1)))
            tiles[1].append(jnp.where(low, pltpu.roll(a, half, 1), b))
        received = [jnp.concatenate(t, axis=1) for t in tiles]
    else:
        received = [got_ref[s] for s in range(species)]
    traces = [jnp.where(is_first, inlet_ref[s], received[s]) for s in range(species)]
    copies = []
    for l in range(levels):
        for s in range(species):
            moved = mm(c_ref[s], masked_parts(traces[s], onehot_ref, l))
            traces[s] = moved[:trace] + top_ref[s, l]
            o_ref[s, l, rest:] = traces[s].astype(BF16)
            o_ref[s, l, :rest] = (moved[trace:] + rest_ref[s, l]).astype(BF16)
            copies.append(
                pltpu.make_async_copy(o_ref.at[s, l], out_hbm.at[s, l], sems.at[s * levels + l])
            )
            copies[-1].start()
    for copy in copies:
        copy.wait()


def on_device(conc_old, lat_velocity, elem_type, inlet_trace, solve_table):
    species, levels, dofs, columns = conc_old.shape
    types_n = solve_table.shape[1]
    trace = inlet_trace.shape[1]
    flow_n = lax.axis_size("flow")
    lat_n = lax.axis_size("lat")
    pairs = species * levels
    tiles = columns // LANES
    inner = columns - 2 * LANES
    rest = dofs - trace

    def shape(dims, kind=F32):
        return jax.ShapeDtypeStruct(dims, kind)

    def cost(rows, count):
        flops = 2 * 3 * types_n * rows * dofs * count * pairs
        return pl.CostEstimate(
            flops=flops, bytes_accessed=8 * pairs * dofs * columns, transcendentals=0
        )

    x, right, left = pl.pallas_call(
        load_kernel,
        out_shape=(shape((species, tiles, levels, dofs, LANES)), shape((trace, LANES)), shape((trace + 8, LANES))),
        in_specs=[ANY, VMEM],
        out_specs=(VMEM, VMEM, VMEM),
        scratch_shapes=[pltpu.SemaphoreType.DMA((species * tiles,))],
        compiler_params=PARAMS,
        name="load_edges",
    )(conc_old, lat_velocity)
    from_left = lax.ppermute(right, "lat", [(i, (i + 1) % lat_n) for i in range(lat_n)])
    from_right = lax.ppermute(left, "lat", [((i + 1) % lat_n, i) for i in range(lat_n)])


    table = jnp.pad(solve_table, ((0, 0), (0, 0), (0, 0), (0, LANES - dofs - trace)))
    mid, rim, mid_top, a_top, a_rest, c_all, onehot = pl.pallas_call(
        inner_kernel,
        out_shape=(
            shape((species, levels, dofs, inner)),
            shape((species, levels, 2, dofs, LANES)),
            shape((species, levels, trace, inner)),
            shape((species, types_n * trace, 3 * dofs), BF16),
            shape((species, types_n * rest, 3 * dofs), BF16),
            shape((species, dofs, 3 * types_n * trace), BF16),
            shape((levels, types_n, trace, columns), BF16),
        ),
        in_specs=[VMEM] * 4,
        out_specs=(VMEM,) * 7,
        scratch_shapes=[pltpu.VMEM((4, tiles, dofs, LANES), F32)],
        compiler_params=PARAMS,
        cost_estimate=cost(dofs, columns),
        name="inner_sources",
    )(x, lat_velocity, elem_type, table)

    packed = 2 * columns == LANES * flow_n and species == 2
    send_shape = (flow_n, trace + levels, LANES) if packed else (species, trace + levels, columns)
    edge, top, send = pl.pallas_call(
        offset_kernel,
        out_shape=(
            shape((species, levels, 2, dofs, LANES)),
            shape((species, levels, trace, columns)),
            shape(send_shape),
        ),
        in_specs=[VMEM] * 11,
        out_specs=(VMEM, VMEM, VMEM),
        compiler_params=PARAMS,
        name="slab_offsets",
    )(
        rim, mid_top, elem_type, onehot, inlet_trace, a_top, c_all, right, left, from_left, from_right
    )
    part = columns // flow_n
    if not packed:
        send = send.reshape(species, trace + levels, flow_n, part)
        send = send.transpose(2, 1, 0, 3).reshape(flow_n, trace + levels, species * part)
    got = lax.all_to_all(send, "flow", 0, 0, tiled=True)

    rest_terms, coef = pl.pallas_call(
        rest_kernel,
        out_shape=(
            shape((species, levels, rest, columns)),
            shape((types_n, trace, trace, species * part)),
        ),
        in_specs=[VMEM] * 5,
        out_specs=(VMEM, VMEM),
        compiler_params=PARAMS,
        cost_estimate=cost(rest, columns),
        name="rest_sources",
    )(mid, edge, elem_type, a_rest, table)
    back = pl.pallas_call(
        owner_kernel,
        out_shape=shape((flow_n, trace, species * part)),
        in_specs=[VMEM, VMEM],
        out_specs=VMEM,
        compiler_params=PARAMS,
        name="owner_sweep",
    )(coef, got)
    traces = lax.all_to_all(back, "flow", 0, 0, tiled=True)
    if not packed:
        traces = traces.reshape(flow_n, trace, species, part)
        traces = traces.transpose(2, 1, 0, 3).reshape(species, trace, columns)

    return pl.pallas_call(
        final_kernel,
        out_shape=shape(conc_old.shape, BF16),
        in_specs=[VMEM] * 6,
        out_specs=ANY,
        scratch_shapes=[
            pltpu.VMEM(conc_old.shape, BF16),
            pltpu.SemaphoreType.DMA((pairs,)),
        ],
        compiler_params=PARAMS,
        name="final_sweep",
    )(top, rest_terms, onehot, inlet_trace, c_all, traces)


def solution(mesh):
    in_specs = (
        P(None, "flow", None, "lat"),
        P("flow", "lat"),
        P("flow", "lat"),
        P(None, None, "lat"),
        P(),
    )
    out_specs = P(None, "flow", None, "lat")
    return jax.shard_map(
        on_device, mesh=mesh, in_specs=in_specs, out_specs=out_specs, check_vma=False
    )
```

time: 53.5 us -> 42.3 us (0.79)
  Pallas kernels: 20.9 us -> 8.27 us
  local copies, waits for them, and re-layouts: 5.5 us -> 10.8 us
  waiting for transfers between devices: 6.69 us -> 3.85 us
  blocking collectives: 10.9 us -> 9.59 us
  starting transfers between devices: 8.26 us -> 9.08 us
  other arithmetic: 0.76 us -> 0 us
    pallas_call x4 -> x6, Pallas kernels: 20.9 us -> 8.27 us  [the longest x1 2.29 us: on_device(): pl.pallas_call(offset_kernel, out_shape=(shape((species, levels, 2, dofs,...]
    unnamed x10 -> x34, local copies, waits for them, and re-layouts: 1.65 us -> 10.8 us
    all_to_all x1, waiting for transfers between devices: 6.68 us -> 3.46 us  [on_device(): got = lax.all_to_all(send, 'flow', 0, 0, tiled=True)]
    slice x3 -> x0, local copies, waits for them, and re-layouts: 2.97 us -> none  [the longest x1 1.42 us: on_device(): conc_old[:, :, :, 0].reshape(pairs, dofs)]
    all_to_all x1, blocking collectives: 10.9 us -> 9.59 us  [on_device(): traces = lax.all_to_all(back, 'flow', 0, 0, tiled=True)]
    concatenate x2 -> x0, other arithmetic: 0.76 us -> none  [the longest x1 0.68 us: on_device(): own = jnp.concatenate([first, last], axis=0)]
    all_to_all x1, starting transfers between devices: 5.8 us -> 6.53 us  [on_device(): got = lax.all_to_all(send, 'flow', 0, 0, tiled=True)]
    pad x1, local copies, waits for them, and re-layouts: 0.72 us -> 0.02 us  [on_device(): jnp.pad(solve_table, ((0, 0), (0, 0), (0, 0), (0, LANES - dofs - trace)))]
  transfers between devices with their start and end apart: 3 -> 3, of which waited for: 1 -> 3; matrix products, arithmetic and copies ran while one was open for 4% -> 0% of each run, Pallas kernels for 17% -> 5%
where the time goes in v2:
time: 42.3 us; the launch traced here: 41.7 us
  local copies, waits for them, and re-layouts  10.8 us (26%)
  blocking collectives  9.59 us (23%)
  starting transfers between devices  9.08 us (21%)
  Pallas kernels  8.27 us (20%)
  waiting for transfers between devices  3.85 us (9%)
    unnamed x34, local copies, waits for them, and re-layouts  10.8 us
    all_to_all x1, blocking collectives, on_device(): traces = lax.all_to_all(back, 'flow', 0, 0, tiled=True)  9.59 us
    all_to_all x1, starting transfers between devices, on_device(): got = lax.all_to_all(send, 'flow', 0, 0, tiled=True)  6.53 us
    all_to_all x1, waiting for transfers between devices, on_device(): got = lax.all_to_all(send, 'flow', 0, 0, tiled=True)  3.46 us
    pallas_call x1, Pallas kernels, on_device(): pl.pallas_call(offset_kernel, out_shape=(shape((species, levels, 2, dofs,...  2.29 us
    pallas_call x1, Pallas kernels, on_device(): pl.pallas_call(final_kernel, out_shape=shape(conc_old.shape, BF16), in_sp...  2.14 us
    ppermute x1, starting transfers between devices, on_device(): lax.ppermute(left, 'lat', [((i + 1) % lat_n, i) for i in range(lat_n)])  2.01 us
    pallas_call x1, Pallas kernels, on_device(): pl.pallas_call(owner_kernel, out_shape=shape((flow_n, trace, species * pa...  1.34 us
  transfers between devices with their start and end apart: 3, of which 3 were waited for; matrix products, arithmetic and copies ran while one was open for 0% of the time, Pallas kernels for 5%

profile of v2, /device:TPU:0, one launch (start us, length us, event | category | flops | bytes accessed | tf_op | source)
XLA Modules:
  0.0 41.7 jit_solution(2392184309557195312)
XLA Ops:
  0.0 1.6 %copy-done = f32[2,8,64,512]{3,2,1,0:T(8,128)S(1)} copy-done((f32[2,8,64,512]{3,2,1,0:T(8,128)S(1)}, f32[2,8,64,512]{3,2,1,0:T(8,128)}, u32[]{:S(2)}) %copy-start) | copy-done | bytes 2097176
  1.6 0.7 %copy-done.14 = f32[8,512]{1,0:T(8,128)S(1)} copy-done((f32[8,512]{1,0:T(8,128)S(1)}, f32[8,512]{1,0:T(8,128)}, u32[]{:S(2)}) %copy-start.14) | copy-done | bytes 16408
  2.3 0.6 %load_edges.1 = (f32[2,4,8,64,128]{4,3,2,1,0:T(8,128)S(1)}, f32[16,128]{1,0:T(8,128)S(1)}, f32[24,128]{1,0:T(8,128)S(1)}) custom-call(f32[2,8,64,512]{3,2,1,0:T(8,128)S(1)} %copy-done, f32[8,512]{1,0:T(8,128)S(1)} %copy-done.14), custom_call_target="tpu_custom_call" | custom-call | tf_op jit(solution)/shard_map/load_edges/pallas_call | solution.py:313
  2.9 0.5 %collective-permute-start = (f32[16,128]{1,0:T(8,128)S(1)}, f32[16,128]{1,0:T(8,128)S(1)}, u32[]{:S(2)}, u32[]{:S(2)}) collective-permute-start(f32[16,128]{1,0:T(8,128)S(1)} %get-tuple-element.26.own_right_ref), channel_id=1, source_target_pairs={{0,1},{1,2},{2,3},{3,0},{4,5},{5,6},{6,7},{7,4},{8,9},{9,10},{10,1... | collective-permute-start | bytes 24584 | tf_op jit(solution)/shard_map/ppermute | solution.py:322
  3.5 2.0 %collective-permute-start.1 = (f32[24,128]{1,0:T(8,128)S(1)}, f32[24,128]{1,0:T(8,128)S(1)}, u32[]{:S(2)}, u32[]{:S(2)}) collective-permute-start(f32[24,128]{1,0:T(8,128)S(1)} %get-tuple-element.27.own_left_ref), channel_id=1, source_target_pairs={{1,0},{2,1},{3,2},{0,3},{5,4},{6,5},{7,6},{4,7},{9,8},{10,9},{11,1... | collective-permute-start | bytes 36872 | tf_op jit(solution)/shard_map/ppermute | solution.py:323
  5.5 0.9 %inner_sources.1 = (f32[2,8,64,256]{3,2,1,0:T(8,128)S(1)}, f32[2,8,2,64,128]{4,3,2,1,0:T(8,128)S(1)}, f32[2,8,16,256]{3,2,1,0:T(8,128)S(1)}, bf16[2,64,192]{2,1,...) custom-call(f32[2,4,8,64,128]{4,3,2,1,0:T(8,128)S(1)} %get-tuple-ele, ...), custom_call_target="tpu_custom_call" | custom-call | flops 805306368 | bytes 4194304 | tf_op jit(solution)/shard_map/inner_sources/pallas_call | solution.py:327
  6.5 0.3 collective-permute-done.from_left_ref
  6.7 0.1 collective-permute-done.1.from_right_ref
  6.9 2.3 %slab_offsets.1 = (f32[2,8,2,64,128]{4,3,2,1,0:T(8,128)S(1)}, f32[2,8,16,512]{3,2,1,0:T(8,128)S(1)}, f32[8,24,128]{2,1,0:T(8,128)}) custom-call(f32[2,8,2,64,128]{4,3,2,1,0:T(8,128)S(1)} %get-tuple-element.21.rim_ref, f32[2,8,16,256]{3,2,1,0:T(8,128)S(1)} %get-tuple-element.22.mid_top_ref, s32[8,512]{1,0:T(8,128)S(1)} %copy-done.13, ...), custom_call_target="tpu_custom_call" | custom-call | tf_op jit(solution)/shard_map/slab_offsets/pallas_call | solution.py:348
  9.2 1.0 %copy-done.1 = f32[2,8,2,64,128]{4,3,2,1,0:T(8,128)} copy-done((f32[2,8,2,64,128]{4,3,2,1,0:T(8,128)}, f32[2,8,2,64,128]{4,3,2,1,0:T(8,128)S(1)}, u32[]{:S(2)}) %copy-start.1) | copy-done | bytes 1048600
  10.1 0.8 %copy-done.5 = f32[2,8,16,512]{3,2,1,0:T(8,128)} copy-done((f32[2,8,16,512]{3,2,1,0:T(8,128)}, f32[2,8,16,512]{3,2,1,0:T(8,128)S(1)}, u32[]{:S(2)}) %copy-start.5) | copy-done | bytes 524312
  10.9 6.5 %all-to-all-start = ((f32[8,24,128]{2,1,0:T(8,128)}), f32[8,24,128]{2,1,0:T(8,128)S(1)}, u32[]{:S(2)}, u32[]{:S(2)}) async-start(f32[8,24,128]{2,1,0:T(8,128)} %get-tuple-element.34), calls=%async_computation | async-start | bytes 196608 | tf_op jit(solution)/shard_map/all_to_all | solution.py:366
  17.5 1.2 %copy-done.2 = f32[2,8,2,64,128]{4,3,2,1,0:T(8,128)S(1)} copy-done((f32[2,8,2,64,128]{4,3,2,1,0:T(8,128)S(1)}, f32[2,8,2,64,128]{4,3,2,1,0:T(8,128)}, u32[]{:S(2)}) %copy-start.2) | copy-done | bytes 1048600
  18.7 0.9 %copy-done.12 = bf16[2,192,192]{2,1,0:T(8,128)(2,1)S(1)} copy-done((bf16[2,192,192]{2,1,0:T(8,128)(2,1)S(1)}, bf16[2,192,192]{2,1,0:T(8,128)(2,1)}, u32[]{:S(2)}) %copy-start.12) | copy-done | bytes 147480
  19.6 1.0 %rest_sources.1 = (f32[2,8,48,512]{3,2,1,0:T(8,128)S(1)}, f32[4,16,16,128]{3,2,1,0:T(8,128)S(1)}) custom-call(f32[2,8,64,256]{3,2,1,0:T(8,128)S(1)} %get-tuple-element.29.mid_ref, f32[2,8,2,64,128]{4,3,2,1,0:T(8,128)S(1)} %copy-done.2, s32[8,512]{1,0:T(8,128)S(1)} %copy-done.13, bf16[2,192,192]{2,1,0:T(8,128)(2,1)S(1)} %copy-done.12, ...), custom_call_target="tpu_custom_call" | custom-call | flops 603979776 | bytes 4194304 | tf_op jit(solution)/shard_map/rest_sources/pallas_call | solution.py:368
  20.6 0.8 %copy-done.3 = f32[4,16,16,128]{3,2,1,0:T(8,128)} copy-done((f32[4,16,16,128]{3,2,1,0:T(8,128)}, f32[4,16,16,128]{3,2,1,0:T(8,128)S(1)}, u32[]{:S(2)}) %copy-start.3) | copy-done | bytes 524312
  21.4 3.5 %all-to-all-done.got_ref = f32[8,24,128]{2,1,0:T(8,128)S(1)} async-done(((f32[8,24,128]{2,1,0:T(8,128)}), f32[8,24,128]{2,1,0:T(8,128)S(1)}, u32[]{:S(2)}, u32[]{:S(2)}) %all-to-all-start) | async-done | bytes 98336 | tf_op jit(solution)/shard_map/all_to_all | solution.py:366
  24.9 1.0 %copy-done.4 = f32[4,16,16,128]{3,2,1,0:T(8,128)S(1)} copy-done((f32[4,16,16,128]{3,2,1,0:T(8,128)S(1)}, f32[4,16,16,128]{3,2,1,0:T(8,128)}, u32[]{:S(2)}) %copy-start.4) | copy-done | bytes 524312
  25.9 1.3 %owner_sweep.1 = f32[8,16,128]{2,1,0:T(8,128)S(1)} custom-call(f32[4,16,16,128]{3,2,1,0:T(8,128)S(1)} %copy-done.4, f32[8,24,128]{2,1,0:T(8,128)S(1)} %all-to-all-done.got_ref), custom_call_target="tpu_custom_call" | custom-call | tf_op jit(solution)/shard_map/owner_sweep/pallas_call | solution.py:380
  27.3 9.6 %all_to_all.10.got_ref = f32[8,16,128]{2,1,0:T(8,128)S(1)} all-to-all(f32[8,16,128]{2,1,0:T(8,128)S(1)} %owner_sweep.1), channel_id=1, replica_groups=mesh['flow'=8,'lat'=4] {'flow'}, dimensions={0} | all-to-all | bytes 131072 | tf_op jit(solution)/shard_map/all_to_all | solution.py:388
  36.9 1.0 %copy-done.6 = f32[2,8,16,512]{3,2,1,0:T(8,128)S(1)} copy-done((f32[2,8,16,512]{3,2,1,0:T(8,128)S(1)}, f32[2,8,16,512]{3,2,1,0:T(8,128)}, u32[]{:S(2)}) %copy-start.6) | copy-done | bytes 524312
  37.9 0.8 %copy-done.8 = f32[2,16,512]{2,1,0:T(8,128)S(1)} copy-done((f32[2,16,512]{2,1,0:T(8,128)S(1)}, f32[2,16,512]{2,1,0:T(8,128)}, u32[]{:S(2)}) %copy-start.8) | copy-done | bytes 65560
  38.8 0.8 %copy-done.10 = bf16[2,64,192]{2,1,0:T(8,128)(2,1)S(1)} copy-done((bf16[2,64,192]{2,1,0:T(8,128)(2,1)S(1)}, bf16[2,64,192]{2,1,0:T(8,128)(2,1)}, u32[]{:S(2)}) %copy-start.10) | copy-done | bytes 49176
  39.6 2.1 %final_sweep.1 = bf16[2,8,64,512]{3,2,1,0:T(8,128)(2,1)} custom-call(f32[2,8,16,512]{3,2,1,0:T(8,128)S(1)} %copy-done.6, f32[2,8,48,512]{3,2,1,0:T(8,128)S(1)} %get-tuple-element.32.rest_ref, bf16[8,4,16,512]{3,2,1,0:T(8,128)(2,1)S(1)} %get-tuple-element.23.onehot_ref, f32[2,16,512]{2,1,0:T(8,128)S(1)} %copy-done.8, bf16[2,64,192]{2,1,0:T(8,128)(2,1)S(1)} %copy-done.10, ...), custom_call_target="tpu_custom_call" | custom-call | tf_op jit(solution)/shard_map/final_sweep/pallas_call | solution.py:393
  (24 shorter events, 0.1 us)
Async XLA Ops:
  0.0 1.6 %copy-start = (f32[2,8,64,512]{3,2,1,0:T(8,128)S(1)}, f32[2,8,64,512]{3,2,1,0:T(8,128)}, u32[]{:S(2)}) copy-start(f32[2,8,64,512]{3,2,1,0:T(8,128)} %conc_hbm.1) | copy-start | bytes 6291460
  1.6 0.7 %copy-start.14 = (f32[8,512]{1,0:T(8,128)S(1)}, f32[8,512]{1,0:T(8,128)}, u32[]{:S(2)}) copy-start(f32[8,512]{1,0:T(8,128)} %vel_ref.3) | copy-start | bytes 49156
  2.3 3.2 %copy-start.16 = (f32[2,4,64,80]{3,2,1,0:T(8,128)S(1)}, f32[2,4,64,80]{3,2,1,0:T(8,128)}, u32[]{:S(2)}) copy-start(f32[2,4,64,80]{3,2,1,0:T(8,128)} %param.9) | copy-start | bytes 491524
  2.3 3.2 %copy-start.13 = (s32[8,512]{1,0:T(8,128)S(1)}, s32[8,512]{1,0:T(8,128)}, u32[]{:S(2)}) copy-start(s32[8,512]{1,0:T(8,128)} %type_ref.5) | copy-start | bytes 49156
  2.3 3.2 %copy-start.15 = (f32[8,512]{1,0:T(8,128)S(1)}, f32[8,512]{1,0:T(8,128)}, u32[]{:S(2)}) copy-start(f32[8,512]{1,0:T(8,128)} %vel_ref.3) | copy-start | bytes 49156
  2.9 4.0 %copy-start.7 = (f32[2,16,512]{2,1,0:T(8,128)S(1)}, f32[2,16,512]{2,1,0:T(8,128)}, u32[]{:S(2)}) copy-start(f32[2,16,512]{2,1,0:T(8,128)} %inlet_ref.3) | copy-start | bytes 196612
  2.9 3.8 %collective-permute-start = (f32[16,128]{1,0:T(8,128)S(1)}, f32[16,128]{1,0:T(8,128)S(1)}, u32[]{:S(2)}, u32[]{:S(2)}) collective-permute-start(f32[16,128]{1,0:T(8,128)S(1)} %get-tuple-element.26.own_right_ref), channel_id=1, source_target_pairs={{0,1},{1,2},{2,3},{3,0},{4,5},{5,6},{6,7},{7,4},{8,9},{9,10},{10,1... | collective-permute-start | bytes 24584 | tf_op jit(solution)/shard_map/ppermute | solution.py:322
  3.5 3.4 %collective-permute-start.1 = (f32[24,128]{1,0:T(8,128)S(1)}, f32[24,128]{1,0:T(8,128)S(1)}, u32[]{:S(2)}, u32[]{:S(2)}) collective-permute-start(f32[24,128]{1,0:T(8,128)S(1)} %get-tuple-element.27.own_left_ref), channel_id=1, source_target_pairs={{1,0},{2,1},{3,2},{0,3},{5,4},{6,5},{7,6},{4,7},{9,8},{10,9},{11,1... | collective-permute-start | bytes 36872 | tf_op jit(solution)/shard_map/ppermute | solution.py:323
  6.5 2.7 %copy-start.11 = (bf16[2,192,192]{2,1,0:T(8,128)(2,1)}, bf16[2,192,192]{2,1,0:T(8,128)(2,1)S(1)}, u32[]{:S(2)}) copy-start(bf16[2,192,192]{2,1,0:T(8,128)(2,1)S(1)} %get-tuple-element.31.a_rest_ref) | copy-start | bytes 442372
  6.5 11.0 %copy-start.9 = (bf16[2,64,192]{2,1,0:T(8,128)(2,1)}, bf16[2,64,192]{2,1,0:T(8,128)(2,1)S(1)}, u32[]{:S(2)}) copy-start(bf16[2,64,192]{2,1,0:T(8,128)(2,1)S(1)} %get-tuple-element.25.c_ref) | copy-start | bytes 147460
  9.2 1.0 %copy-start.1 = (f32[2,8,2,64,128]{4,3,2,1,0:T(8,128)}, f32[2,8,2,64,128]{4,3,2,1,0:T(8,128)S(1)}, u32[]{:S(2)}) copy-start(f32[2,8,2,64,128]{4,3,2,1,0:T(8,128)S(1)} %get-tuple-element.30.edge_ref) | copy-start | bytes 3145732
  10.1 0.8 %copy-start.5 = (f32[2,8,16,512]{3,2,1,0:T(8,128)}, f32[2,8,16,512]{3,2,1,0:T(8,128)S(1)}, u32[]{:S(2)}) copy-start(f32[2,8,16,512]{3,2,1,0:T(8,128)S(1)} %get-tuple-element.28.top_ref) | copy-start | bytes 1572868
  10.9 14.0 %all-to-all-start = ((f32[8,24,128]{2,1,0:T(8,128)}), f32[8,24,128]{2,1,0:T(8,128)S(1)}, u32[]{:S(2)}, u32[]{:S(2)}) async-start(f32[8,24,128]{2,1,0:T(8,128)} %get-tuple-element.34), calls=%async_computation | async-start | bytes 196608 | tf_op jit(solution)/shard_map/all_to_all | solution.py:366
  17.5 1.2 %copy-start.2 = (f32[2,8,2,64,128]{4,3,2,1,0:T(8,128)S(1)}, f32[2,8,2,64,128]{4,3,2,1,0:T(8,128)}, u32[]{:S(2)}) copy-start(f32[2,8,2,64,128]{4,3,2,1,0:T(8,128)} %copy-done.1) | copy-start | bytes 3145732
  18.7 0.9 %copy-start.12 = (bf16[2,192,192]{2,1,0:T(8,128)(2,1)S(1)}, bf16[2,192,192]{2,1,0:T(8,128)(2,1)}, u32[]{:S(2)}) copy-start(bf16[2,192,192]{2,1,0:T(8,128)(2,1)} %copy-done.11) | copy-start | bytes 442372
  20.6 0.8 %copy-start.3 = (f32[4,16,16,128]{3,2,1,0:T(8,128)}, f32[4,16,16,128]{3,2,1,0:T(8,128)S(1)}, u32[]{:S(2)}) copy-start(f32[4,16,16,128]{3,2,1,0:T(8,128)S(1)} %get-tuple-element.33.coef_ref) | copy-start | bytes 1572868
  24.9 1.0 %copy-start.4 = (f32[4,16,16,128]{3,2,1,0:T(8,128)S(1)}, f32[4,16,16,128]{3,2,1,0:T(8,128)}, u32[]{:S(2)}) copy-start(f32[4,16,16,128]{3,2,1,0:T(8,128)} %copy-done.3) | copy-start | bytes 1572868
  36.9 1.0 %copy-start.6 = (f32[2,8,16,512]{3,2,1,0:T(8,128)S(1)}, f32[2,8,16,512]{3,2,1,0:T(8,128)}, u32[]{:S(2)}) copy-start(f32[2,8,16,512]{3,2,1,0:T(8,128)} %copy-done.5) | copy-start | bytes 1572868
  37.9 0.8 %copy-start.8 = (f32[2,16,512]{2,1,0:T(8,128)S(1)}, f32[2,16,512]{2,1,0:T(8,128)}, u32[]{:S(2)}) copy-start(f32[2,16,512]{2,1,0:T(8,128)} %inlet_ref.3) | copy-start | bytes 196612
  38.8 0.8 %copy-start.10 = (bf16[2,64,192]{2,1,0:T(8,128)(2,1)S(1)}, bf16[2,64,192]{2,1,0:T(8,128)(2,1)}, u32[]{:S(2)}) copy-start(bf16[2,64,192]{2,1,0:T(8,128)(2,1)} %copy-done.9) | copy-start | bytes 147460

commit v3 on v2

--- a/solution.py
+++ b/solution.py
@@ -8,7 +8,7 @@
 F32 = jnp.float32
 BF16 = jnp.bfloat16
 VMEM = pl.BlockSpec(memory_space=pltpu.VMEM)
-ANY = pl.BlockSpec(memory_space=pl.ANY)
+HBM = pl.BlockSpec(memory_space=pltpu.HBM)
 LANES = 128
 PARAMS = pltpu.CompilerParams(vmem_limit_bytes=20 << 20)
 
@@ -36,21 +36,28 @@
     return out.reshape(rows, columns)
 
 
-def masked_parts(x, onehot_ref, level):
+def masked_parts(x, masks):
     hi, lo = split(x)
     parts = []
-    for t in range(onehot_ref.shape[1]):
-        mask = onehot_ref[level, t]
+    for mask in masks:
         his = hi * mask
         parts += [his, lo * mask, his]
     return jnp.concatenate(parts, axis=0)
 
 
+def masks_of(type_ref, level, types_n, rows):
+    types = jnp.broadcast_to(type_ref[level : level + 1], (rows, type_ref.shape[1]))
+    return [jnp.where(types == t, 1.0, 0.0).astype(BF16) for t in range(types_n)]
+
+
 def mm(a, b):
     return jnp.dot(a, b, preferred_element_type=F32)
 
 
-def load_kernel(conc_hbm, vel_ref, x_ref, right_ref, left_ref, sems):
+def load_kernel(
+    conc_hbm, vel_hbm, type_hbm, table_hbm, inlet_hbm, x_ref, vel_ref, type_ref, table_ref, inlet_ref, right_ref, left_ref,
+    sems, small_sems,
+):
     species, tiles, levels, dofs, _ = x_ref.shape
     trace = right_ref.shape[0]
     stride = dofs // trace
@@ -60,6 +67,12 @@
             block = conc_hbm.at[s, :, :, pl.ds(k * LANES, LANES)]
             copies.append(pltpu.make_async_copy(block, x_ref.at[s, k], sems.at[s * tiles + k]))
             copies[-1].start()
+        if k == tiles - 1:
+            small = ((vel_hbm, vel_ref), (type_hbm, type_ref), (table_hbm, table_ref), (inlet_hbm, inlet_ref))
+            small = [pltpu.make_async_copy(*ends, small_sems.at[i]) for i, ends in enumerate(small)]
+            for copy in small:
+                copy.start()
+    small[0].wait()
     lane = lane_index((levels, LANES))
     on_diag = lane % levels == lax.broadcasted_iota(jnp.int32, lane.shape, 0)
     face = jnp.broadcast_to(vel_ref[:, :1], (levels, LANES))
@@ -78,17 +91,16 @@
         left = jnp.where(lane == p, pltpu.roll(first, p, 1) if p else first, left)
     right_ref[...] = right
     left_ref[:trace] = left
-    for copy in copies[2 * species :]:
+    for copy in copies[2 * species :] + small[1:]:
         copy.wait()
 
 
 def inner_kernel(
-    x_ref, vel_ref, type_ref, table_ref, mid_ref, rim_ref, top_ref, a_top_ref, a_rest_ref, c_ref, onehot_ref,
-    delta_ref,
+    x_ref, vel_ref, type_ref, table_ref, rest_ref, rim_ref, top_ref, a_top_ref, a_rest_ref, c_ref, small_ref, delta_ref
 ):
     species, tiles_n, levels, dofs, _ = x_ref.shape
     columns = tiles_n * LANES
-    types_n, trace = onehot_ref.shape[1], onehot_ref.shape[2]
+    types_n, trace = small_ref.shape[1], small_ref.shape[2]
     stride = dofs // trace
     rest = dofs - trace
     for s in range(species):
@@ -96,11 +108,13 @@
         pieces = [[], [], []]
         for t in range(types_n):
             table = table_ref[s, t]
+            table = jnp.concatenate([table, jnp.zeros((dofs, LANES - table.shape[1]), F32)], axis=1)
             hi = table.astype(BF16).astype(F32)
             lo = table - hi
             lane = lane_index(table.shape)
             twice = jnp.where(lane < dofs, hi, pltpu.roll(hi, dofs, 1))
             wide = jnp.concatenate([twice, lo[:, :dofs]], axis=1).astype(BF16)
+            small_ref[s, t] = table_ref[s, t, rest:, dofs:]
             tops.append(wide[rest:])
             rests.append(wide[:rest])
             pieces[0].append(hi)
@@ -127,10 +141,7 @@
         velocity = jnp.broadcast_to(vel_ref[l : l + 1], (trace, columns))
         plus = jnp.where(lane > 0, jnp.maximum(velocity, 0.0), 0.0)
         minus = jnp.minimum(velocity, 0.0)
-        types = jnp.broadcast_to(type_ref[l : l + 1], (trace, columns))
-        for t in range(types_n):
-            onehot_ref[l, t] = jnp.where(types == t, 1.0, 0.0).astype(BF16)
-        types_mid = types[:8, LANES : columns - LANES]
+        types = jnp.broadcast_to(type_ref[l : l + 1], (8, columns))[:, LANES : columns - LANES]
         for s in range(species):
             k = (l * species + s) % delta_ref.shape[0]
             zero, three = pl.ds(0, trace, stride=stride), pl.ds(stride - 1, trace, stride=stride)
@@ -143,16 +154,16 @@
                 delta_ref[k, i, zero, :] = flux[:, i * LANES : (i + 1) * LANES]
                 delta_ref[k, i, three, :] = out[:, i * LANES : (i + 1) * LANES]
                 source.append(x_ref[s, i, l] + delta_ref[k, i])
-            mid = jnp.concatenate(source[1:-1], axis=1)
-            mid_ref[s, l] = mid
+            parts = stacked_parts(jnp.concatenate(source[1:-1], axis=1))
             rim_ref[s, l, 0] = source[0]
             rim_ref[s, l, 1] = source[-1]
-            top_ref[s, l] = pick(mm(a_top_ref[s], stacked_parts(mid)), types_mid, trace)
+            top_ref[s, l] = pick(mm(a_top_ref[s], parts), types, trace)
+            rest_ref[s, l] = pick(mm(a_rest_ref[s], parts), types, rest)
 
 
 def offset_kernel(
-    rim_ref, mid_top_ref, type_ref, onehot_ref, inlet_ref, a_top_ref, c_ref, own_right_ref, own_left_ref, from_left_ref,
-    from_right_ref, edge_ref, top_ref, send_ref,
+    rim_ref, mid_top_ref, type_ref, inlet_ref, a_top_ref, c_ref, own_right_ref, own_left_ref, from_left_ref, from_right_ref,
+    edge_hbm, top_ref, send_ref, edge_ref, sems,
 ):
     species, levels, trace, columns = top_ref.shape
     dofs = rim_ref.shape[3]
@@ -178,6 +189,9 @@
             edge_ref[s, l] = rim_ref[s, l]
             edge_ref[s, l, 0, low, :] = rim_ref[s, l, 0, low, :] + first
             edge_ref[s, l, 1, high, :] = rim_ref[s, l, 1, high, :] - last
+    copies = [pltpu.make_async_copy(edge_ref.at[s], edge_hbm.at[s], sems.at[s]) for s in range(species)]
+    for copy in copies:
+        copy.start()
     for l in range(levels):
         types = jnp.broadcast_to(type_ref[l : l + 1], (8, columns))
         rim_types = jnp.concatenate([types[:, :LANES], types[:, columns - LANES :]], axis=1)
@@ -188,8 +202,9 @@
     start = (lax.axis_index("flow") == 0).astype(F32)
     traces = [inlet_ref[s] * start for s in range(species)]
     for l in range(levels):
-        for s in range(species):
-            moved = mm(c_ref[s, :trace], masked_parts(traces[s], onehot_ref, l))
+        masks = masks_of(type_ref, l, a_top_ref.shape[1] // trace, trace)
+        for s in range(species):
+            moved = mm(c_ref[s, :trace], masked_parts(traces[s], masks))
             traces[s] = moved + top_ref[s, l]
     width = send_ref.shape[2]
     types = type_ref[...].astype(F32)
@@ -209,26 +224,33 @@
         for s in range(species):
             send_ref[s, :trace] = traces[s]
             send_ref[s, trace:] = types
-
-
-def rest_kernel(mid_ref, edge_ref, type_ref, a_rest_ref, table_ref, rest_ref, coef_ref):
-    species, levels, rest, columns = rest_ref.shape
+    for copy in copies:
+        copy.wait()
+
+
+def rest_kernel(edge_hbm, type_ref, a_rest_ref, small_ref, rest_ref, coef_ref, edge_ref, sems):
+    species, levels, rest, _ = rest_ref.shape
+    columns = type_ref.shape[1]
     types_n, trace, width = coef_ref.shape[0], coef_ref.shape[1], coef_ref.shape[3]
-    dofs = rest + trace
+    copies = [pltpu.make_async_copy(edge_hbm.at[s], edge_ref.at[s], sems.at[s]) for s in range(species)]
+    for copy in copies:
+        copy.start()
     half = width // species
     which = lane_index((trace, width)) // half
     for t in range(types_n):
         for j in range(trace):
-            column = slice(dofs + j, dofs + j + 1)
-            value = jnp.broadcast_to(table_ref[0, t, rest:, column], (trace, width))
+            value = jnp.broadcast_to(small_ref[0, t, :, j : j + 1], (trace, width))
             for s in range(1, species):
-                other = jnp.broadcast_to(table_ref[s, t, rest:, column], (trace, width))
+                other = jnp.broadcast_to(small_ref[s, t, :, j : j + 1], (trace, width))
                 value = jnp.where(which == s, other, value)
             coef_ref[t, j] = value
+    for copy in copies:
+        copy.wait()
     for l in range(levels):
         types = jnp.broadcast_to(type_ref[l : l + 1], (8, columns))
-        for s in range(species):
-            source = jnp.concatenate([edge_ref[s, l, 0], mid_ref[s, l], edge_ref[s, l, 1]], axis=1)
+        types = jnp.concatenate([types[:, :LANES], types[:, columns - LANES :]], axis=1)
+        for s in range(species):
+            source = jnp.concatenate([edge_ref[s, l, 0], edge_ref[s, l, 1]], axis=1)
             rest_ref[s, l] = pick(mm(a_rest_ref[s], stacked_parts(source)), types, rest)
 
 
@@ -258,9 +280,12 @@
     out_ref[slabs - 1] = last
 
 
-def final_kernel(top_ref, rest_ref, onehot_ref, inlet_ref, c_ref, got_ref, out_hbm, o_ref, sems):
+def final_kernel(
+    top_ref, inner_rest_ref, outer_rest_ref, type_ref, inlet_ref, c_ref, got_ref, out_hbm, o_ref, sems
+):
     species, levels, trace, columns = top_ref.shape
-    rest = rest_ref.shape[2]
+    rest = inner_rest_ref.shape[2]
+    types_n = c_ref.shape[2] // (3 * trace)
     width = got_ref.shape[2]
     is_first = lax.axis_index("flow") == 0
     if width == LANES:
@@ -277,11 +302,14 @@
     traces = [jnp.where(is_first, inlet_ref[s], received[s]) for s in range(species)]
     copies = []
     for l in range(levels):
-        for s in range(species):
-            moved = mm(c_ref[s], masked_parts(traces[s], onehot_ref, l))
+        masks = masks_of(type_ref, l, types_n, trace)
+        for s in range(species):
+            moved = mm(c_ref[s], masked_parts(traces[s], masks))
             traces[s] = moved[:trace] + top_ref[s, l]
             o_ref[s, l, rest:] = traces[s].astype(BF16)
-            o_ref[s, l, :rest] = (moved[trace:] + rest_ref[s, l]).astype(BF16)
+            outer = outer_rest_ref[s, l]
+            fixed = jnp.concatenate([outer[:, :LANES], inner_rest_ref[s, l], outer[:, LANES:]], axis=1)
+            o_ref[s, l, :rest] = (moved[trace:] + fixed).astype(BF16)
             copies.append(
                 pltpu.make_async_copy(o_ref.at[s, l], out_hbm.at[s, l], sems.at[s * levels + l])
             )
@@ -304,36 +332,49 @@
     def shape(dims, kind=F32):
         return jax.ShapeDtypeStruct(dims, kind)
 
+    def held(dims, kind=F32):
+        return pltpu.VMEM(dims, kind)
+
+    def far(array):
+        return pltpu.with_memory_space_constraint(array, pltpu.HBM)
+
     def cost(rows, count):
         flops = 2 * 3 * types_n * rows * dofs * count * pairs
         return pl.CostEstimate(
             flops=flops, bytes_accessed=8 * pairs * dofs * columns, transcendentals=0
         )
 
-    x, right, left = pl.pallas_call(
+    x, velocity, types, table, inlet, right, left = pl.pallas_call(
         load_kernel,
-        out_shape=(shape((species, tiles, levels, dofs, LANES)), shape((trace, LANES)), shape((trace + 8, LANES))),
-        in_specs=[ANY, VMEM],
-        out_specs=(VMEM, VMEM, VMEM),
-        scratch_shapes=[pltpu.SemaphoreType.DMA((species * tiles,))],
+        out_shape=(
+            held((species, tiles, levels, dofs, LANES)),
+            held(lat_velocity.shape),
+            held(elem_type.shape, elem_type.dtype),
+            held(solve_table.shape),
+            held(inlet_trace.shape),
+            shape((trace, LANES)),
+            shape((trace + 8, LANES)),
+        ),
+        in_specs=[HBM] * 5,
+        out_specs=(VMEM,) * 7,
+        scratch_shapes=[pltpu.SemaphoreType.DMA((species * tiles,)), pltpu.SemaphoreType.DMA((4,))],
         compiler_params=PARAMS,
         name="load_edges",
-    )(conc_old, lat_velocity)
+    )(far(conc_old), far(lat_velocity), far(elem_type), far(solve_table), far(inlet_trace))
     from_left = lax.ppermute(right, "lat", [(i, (i + 1) % lat_n) for i in range(lat_n)])
     from_right = lax.ppermute(left, "lat", [((i + 1) % lat_n, i) for i in range(lat_n)])
 
 
-    table = jnp.pad(solve_table, ((0, 0), (0, 0), (0, 0), (0, LANES - dofs - trace)))
-    mid, rim, mid_top, a_top, a_rest, c_all, onehot = pl.pallas_call(
+    inner_rest, rim, mid_top, a_top, a_rest, c_all, small = pl.pallas_call(
         inner_kernel,
         out_shape=(
-            shape((species, levels, dofs, inner)),
-            shape((species, levels, 2, dofs, LANES)),
-            shape((species, levels, trace, inner)),
-            shape((species, types_n * trace, 3 * dofs), BF16),
-            shape((species, types_n * rest, 3 * dofs), BF16),
-            shape((species, dofs, 3 * types_n * trace), BF16),
-            shape((levels, types_n, trace, columns), BF16),
+            held((species, levels, rest, inner)),
+            held((species, levels, 2, dofs, LANES)),
+            held((species, levels, trace, inner)),
+            held((species, types_n * trace, 3 * dofs), BF16),
+            held((species, types_n * rest, 3 * dofs), BF16),
+            held((species, dofs, 3 * types_n * trace), BF16),
+            held((species, types_n, trace, trace)),
         ),
         in_specs=[VMEM] * 4,
         out_specs=(VMEM,) * 7,
@@ -341,23 +382,25 @@
         compiler_params=PARAMS,
         cost_estimate=cost(dofs, columns),
         name="inner_sources",
-    )(x, lat_velocity, elem_type, table)
-
+    )(x, velocity, types, table)
+
+    edge_shape = (species, levels, 2, dofs, LANES)
     packed = 2 * columns == LANES * flow_n and species == 2
     send_shape = (flow_n, trace + levels, LANES) if packed else (species, trace + levels, columns)
     edge, top, send = pl.pallas_call(
         offset_kernel,
         out_shape=(
-            shape((species, levels, 2, dofs, LANES)),
-            shape((species, levels, trace, columns)),
+            pltpu.HBM(edge_shape, F32),
+            held((species, levels, trace, columns)),
             shape(send_shape),
         ),
-        in_specs=[VMEM] * 11,
-        out_specs=(VMEM, VMEM, VMEM),
+        in_specs=[VMEM] * 10,
+        out_specs=(HBM, VMEM, VMEM),
+        scratch_shapes=[pltpu.VMEM(edge_shape, F32), pltpu.SemaphoreType.DMA((species,))],
         compiler_params=PARAMS,
         name="slab_offsets",
     )(
-        rim, mid_top, elem_type, onehot, inlet_trace, a_top, c_all, right, left, from_left, from_right
+        rim, mid_top, types, inlet, a_top, c_all, right, left, from_left, from_right
     )
     part = columns // flow_n
     if not packed:
@@ -365,18 +408,19 @@
         send = send.transpose(2, 1, 0, 3).reshape(flow_n, trace + levels, species * part)
     got = lax.all_to_all(send, "flow", 0, 0, tiled=True)
 
-    rest_terms, coef = pl.pallas_call(
+    outer_rest, coef = pl.pallas_call(
         rest_kernel,
         out_shape=(
-            shape((species, levels, rest, columns)),
-            shape((types_n, trace, trace, species * part)),
+            held((species, levels, rest, 2 * LANES)),
+            held((types_n, trace, trace, species * part)),
         ),
-        in_specs=[VMEM] * 5,
+        in_specs=[HBM] + [VMEM] * 3,
         out_specs=(VMEM, VMEM),
+        scratch_shapes=[pltpu.VMEM(edge_shape, F32), pltpu.SemaphoreType.DMA((species,))],
         compiler_params=PARAMS,
         cost_estimate=cost(rest, columns),
         name="rest_sources",
-    )(mid, edge, elem_type, a_rest, table)
+    )(far(edge), types, a_rest, small)
     back = pl.pallas_call(
         owner_kernel,
         out_shape=shape((flow_n, trace, species * part)),
@@ -393,15 +437,15 @@
     return pl.pallas_call(
         final_kernel,
         out_shape=shape(conc_old.shape, BF16),
-        in_specs=[VMEM] * 6,
-        out_specs=ANY,
+        in_specs=[VMEM] * 7,
+        out_specs=HBM,
         scratch_shapes=[
             pltpu.VMEM(conc_old.shape, BF16),
             pltpu.SemaphoreType.DMA((pairs,)),
         ],
         compiler_params=PARAMS,
         name="final_sweep",
-    )(top, rest_terms, onehot, inlet_trace, c_all, traces)
+    )(top, inner_rest, outer_rest, types, inlet, c_all, traces)
 
 
 def solution(mesh):

time: 42.3 us -> 35.6 us (0.84)
  local copies, waits for them, and re-layouts: 10.8 us -> 0 us
  waiting for transfers between devices: 3.85 us -> 7.02 us
  Pallas kernels: 8.27 us -> 10.7 us
  starting transfers between devices: 9.08 us -> 8.31 us
    unnamed x34 -> x0, local copies, waits for them, and re-layouts: 10.8 us -> none
    pallas_call x4, Pallas kernels: 4.79 us -> 7.21 us  [the longest x1 2.28 us: on_device(): pl.pallas_call(offset_kernel, out_shape=(pltpu.HBM(edge_shape, F32), held...]
    all_to_all x1, waiting for transfers between devices: 3.46 us -> 5.33 us  [on_device(): got = lax.all_to_all(send, 'flow', 0, 0, tiled=True)]
    ppermute x1, waiting for transfers between devices: 0.26 us -> 1.69 us  [on_device(): lax.ppermute(right, 'lat', [(i, (i + 1) % lat_n) for i in range(lat_n)])]
    all_to_all x1, starting transfers between devices: 6.53 us -> 5.82 us  [on_device(): got = lax.all_to_all(send, 'flow', 0, 0, tiled=True)]
    ppermute x1, starting transfers between devices: 0.54 us -> 0.01 us  [on_device(): lax.ppermute(right, 'lat', [(i, (i + 1) % lat_n) for i in range(lat_n)])]
    ppermute x1, starting transfers between devices: 2.01 us -> 2.49 us  [on_device(): lax.ppermute(left, 'lat', [((i + 1) % lat_n, i) for i in range(lat_n)])]
  transfers between devices with their start and end apart: 3 -> 3, of which waited for: 3 -> 2; matrix products, arithmetic and copies ran while one was open for 0% -> 0% of each run, Pallas kernels for 5% -> 9%
where the time goes in v3:
time: 35.6 us; the launch traced here: 35.3 us
  Pallas kernels  10.7 us (30%)
  blocking collectives  9.29 us (26%)
  starting transfers between devices  8.31 us (23%)
  waiting for transfers between devices  7.02 us (20%)
    all_to_all x1, blocking collectives, on_device(): traces = lax.all_to_all(back, 'flow', 0, 0, tiled=True)  9.29 us
    all_to_all x1, starting transfers between devices, on_device(): got = lax.all_to_all(send, 'flow', 0, 0, tiled=True)  5.82 us
    all_to_all x1, waiting for transfers between devices, on_device(): got = lax.all_to_all(send, 'flow', 0, 0, tiled=True)  5.33 us
    ppermute x1, starting transfers between devices, on_device(): lax.ppermute(left, 'lat', [((i + 1) % lat_n, i) for i in range(lat_n)])  2.49 us
    pallas_call x1, Pallas kernels, on_device(): pl.pallas_call(offset_kernel, out_shape=(pltpu.HBM(edge_shape, F32), held...  2.28 us
    pallas_call x1, Pallas kernels, on_device(): pl.pallas_call(final_kernel, out_shape=shape(conc_old.shape, BF16), in_sp...  2.14 us
    pallas_call x1, Pallas kernels, on_device(): pl.pallas_call(rest_kernel, out_shape=(held((species, levels, rest, 2 * L...  1.79 us
    pallas_call x1, Pallas kernels, on_device(): pl.pallas_call(load_kernel, out_shape=(held((species, tiles, levels, dofs...  1.77 us
  transfers between devices with their start and end apart: 3, of which 2 were waited for; matrix products, arithmetic and copies ran while one was open for 0% of the time, Pallas kernels for 9%

profile of v3, /device:TPU:0, one launch (start us, length us, event | category | flops | bytes accessed | tf_op | source)
XLA Modules:
  0.0 35.3 jit_solution(8180484917497611876)
XLA Ops:
  0.0 1.8 %load_edges.1 = (f32[2,4,8,64,128]{4,3,2,1,0:T(8,128)S(1)}, f32[8,512]{1,0:T(8,128)S(1)}, s32[8,512]{1,0:T(8,128)S(1)}, f32[2,4,64,80]{3,2,1,0:T(8,128)S(1)}, f3...) custom-call(f32[2,8,64,512]{3,2,1,0:T(8,128)} %conc_hbm.1, f32[8,512]{1,0:T(8,128)} %vel_hbm.1, ...), custom_call_target="tpu_custom_call" | custom-call | tf_op jit(solution)/shard_map/load_edges/pallas_call | solution.py:347
  1.8 2.5 %collective-permute-start.1 = (f32[24,128]{1,0:T(8,128)S(1)}, f32[24,128]{1,0:T(8,128)S(1)}, u32[]{:S(2)}, u32[]{:S(2)}) collective-permute-start(f32[24,128]{1,0:T(8,128)S(1)} %get-tuple-element.34.own_left_ref), channel_id=1, source_target_pairs={{1,0},{2,1},{3,2},{0,3},{5,4},{6,5},{7,6},{4,7},{9,8},{10,9},{11,1... | collective-permute-start | bytes 36872 | tf_op jit(solution)/shard_map/ppermute | solution.py:365
  4.3 0.0 collective-permute-start
  4.3 1.4 %inner_sources.1 = (f32[2,8,48,256]{3,2,1,0:T(8,128)S(1)}, f32[2,8,2,64,128]{4,3,2,1,0:T(8,128)S(1)}, f32[2,8,16,256]{3,2,1,0:T(8,128)S(1)}, bf16[2,64,192]{2,1,...) custom-call(f32[2,4,8,64,128]{4,3,2,1,0:T(8,128)S(1)} %get-tuple-ele, ...), custom_call_target="tpu_custom_call" | custom-call | flops 805306368 | bytes 4194304 | tf_op jit(solution)/shard_map/inner_sources/pallas_call | solution.py:368
  5.7 1.7 %collective-permute-done.from_left_ref = f32[16,128]{1,0:T(8,128)S(1)} collective-permute-done((f32[16,128]{1,0:T(8,128)S(1)}, f32[16,128]{1,0:T(8,128)S(1)}, u32[]{:S(2)}, u32[]{:S(2)}) %collective-permute-start) | collective-permute-done | bytes 8224 | tf_op jit(solution)/shard_map/ppermute | solution.py:364
  7.3 0.0 collective-permute-done.1.from_right_ref
  7.3 2.3 %slab_offsets.1 = (f32[2,8,2,64,128]{4,3,2,1,0:T(8,128)}, f32[2,8,16,512]{3,2,1,0:T(8,128)S(1)}, f32[8,24,128]{2,1,0:T(8,128)}) custom-call(f32[2,8,2,64,128]{4,3,2,1,0:T(8,128)S(1)} %get-tuple-element.28.rim_ref, f32[2,8,16,256]{3,2,1,0:T(8,128)S(1)} %get-tuple-element.29.mid_top_ref, s32[8,512]{1,0:T(8,128)S(1)} %get-tuple-element.26.type_ref, ...), custom_call_target="tpu_custom_call" | custom-call | tf_op jit(solution)/shard_map/slab_offsets/pallas_call | solution.py:390
  9.6 5.8 %all-to-all-start = ((f32[8,24,128]{2,1,0:T(8,128)}), f32[8,24,128]{2,1,0:T(8,128)S(1)}, u32[]{:S(2)}, u32[]{:S(2)}) async-start(f32[8,24,128]{2,1,0:T(8,128)} %get-tuple-element.42), calls=%async_computation | async-start | bytes 196608 | tf_op jit(solution)/shard_map/all_to_all | solution.py:409
  15.4 1.8 %rest_sources.1 = (f32[2,8,48,256]{3,2,1,0:T(8,128)S(1)}, f32[4,16,16,128]{3,2,1,0:T(8,128)S(1)}) custom-call(f32[2,8,2,64,128]{4,3,2,1,0:T(8,128)} %get-tuple-element.37.edge_hbm, s32[8,512]{1,0:T(8,128)S(1)} %get-tuple-element.26.type_ref, bf16[2,192,192]{2,1,0:T(8,128)(2,1)S(1)} %get-tuple-element.38.a_rest_ref, ...), custom_call_target="tpu_custom_call" | custom-call | flops 603979776 | bytes 4194304 | tf_op jit(solution)/shard_map/rest_sources/pallas_call | solution.py:411
  17.2 5.3 %all-to-all-done.got_ref = f32[8,24,128]{2,1,0:T(8,128)S(1)} async-done(((f32[8,24,128]{2,1,0:T(8,128)}), f32[8,24,128]{2,1,0:T(8,128)S(1)}, u32[]{:S(2)}, u32[]{:S(2)}) %all-to-all-start) | async-done | bytes 98336 | tf_op jit(solution)/shard_map/all_to_all | solution.py:409
  22.6 1.3 %owner_sweep.1 = f32[8,16,128]{2,1,0:T(8,128)S(1)} custom-call(f32[4,16,16,128]{3,2,1,0:T(8,128)S(1)} %get-tuple-element.41.coef_ref, f32[8,24,128]{2,1,0:T(8,128)S(1)} %all-to-all-done.got_ref), custom_call_target="tpu_custom_call" | custom-call | tf_op jit(solution)/shard_map/owner_sweep/pallas_call | solution.py:424
  23.9 9.3 %all_to_all.10.got_ref = f32[8,16,128]{2,1,0:T(8,128)S(1)} all-to-all(f32[8,16,128]{2,1,0:T(8,128)S(1)} %owner_sweep.1), channel_id=1, replica_groups=mesh['flow'=8,'lat'=4] {'flow'}, dimensions={0} | all-to-all | bytes 131072 | tf_op jit(solution)/shard_map/all_to_all | solution.py:432
  33.2 2.1 %final_sweep.1 = bf16[2,8,64,512]{3,2,1,0:T(8,128)(2,1)} custom-call(f32[2,8,16,512]{3,2,1,0:T(8,128)S(1)} %get-tuple-element.35.top_ref, f32[2,8,48,256]{3,2,1,0:T(8,128)S(1)} %get-tuple-element.36.inner_rest_ref, f32[2,8,48,256]{3,2,1,0:T(8,128)S(1)} %get-tuple-element.40.outer_rest_ref, s32[8,512]{1,0:T(8,128)S(1)} %get-tuple-element.26.type_ref, ...), custom_call_target="tpu_custom_call" | custom-call | tf_op jit(solution)/shard_map/final_sweep/pallas_call | solution.py:437
Async XLA Ops:
  1.8 5.6 %collective-permute-start.1 = (f32[24,128]{1,0:T(8,128)S(1)}, f32[24,128]{1,0:T(8,128)S(1)}, u32[]{:S(2)}, u32[]{:S(2)}) collective-permute-start(f32[24,128]{1,0:T(8,128)S(1)} %get-tuple-element.34.own_left_ref), channel_id=1, source_target_pairs={{1,0},{2,1},{3,2},{0,3},{5,4},{6,5},{7,6},{4,7},{9,8},{10,9},{11,1... | collective-permute-start | bytes 36872 | tf_op jit(solution)/shard_map/ppermute | solution.py:365
  4.3 3.1 %collective-permute-start = (f32[16,128]{1,0:T(8,128)S(1)}, f32[16,128]{1,0:T(8,128)S(1)}, u32[]{:S(2)}, u32[]{:S(2)}) collective-permute-start(f32[16,128]{1,0:T(8,128)S(1)} %get-tuple-element.33.own_right_ref), channel_id=1, source_target_pairs={{0,1},{1,2},{2,3},{3,0},{4,5},{5,6},{6,7},{7,4},{8,9},{9,10},{10,1... | collective-permute-start | bytes 24584 | tf_op jit(solution)/shard_map/ppermute | solution.py:364
  9.6 12.9 %all-to-all-start = ((f32[8,24,128]{2,1,0:T(8,128)}), f32[8,24,128]{2,1,0:T(8,128)S(1)}, u32[]{:S(2)}, u32[]{:S(2)}) async-start(f32[8,24,128]{2,1,0:T(8,128)} %get-tuple-element.42), calls=%async_computation | async-start | bytes 196608 | tf_op jit(solution)/shard_map/all_to_all | solution.py:409

commit v4 on v3

v4 whole, which is shorter than its diff:
```python
import jax
import jax.numpy as jnp
from jax import lax
from jax.experimental import pallas as pl
from jax.experimental.pallas import tpu as pltpu
from jax.sharding import PartitionSpec as P

F32 = jnp.float32
BF16 = jnp.bfloat16
VMEM = pl.BlockSpec(memory_space=pltpu.VMEM)
HBM = pl.BlockSpec(memory_space=pltpu.HBM)
LANES = 128
PARAMS = pltpu.CompilerParams(vmem_limit_bytes=20 << 20)


def lane_index(shape):
    return lax.broadcasted_iota(jnp.int32, shape, len(shape) - 1)


def split(x):
    hi = x.astype(BF16)
    return hi, (x - hi.astype(F32)).astype(BF16)


def stacked_parts(x):
    hi, lo = split(x)
    return jnp.concatenate([hi, lo, hi], axis=0)


def pick(per_type, types, rows):
    columns = per_type.shape[1]
    grid = per_type.reshape(-1, rows // 8, 8, columns)
    out = grid[0]
    for t in range(1, grid.shape[0]):
        out = jnp.where((types == t)[None], grid[t], out)
    return out.reshape(rows, columns)


def masked_parts(x, masks):
    hi, lo = split(x)
    parts = []
    for mask in masks:
        his = hi * mask
        parts += [his, lo * mask, his]
    return jnp.concatenate(parts, axis=0)


def masks_of(type_ref, level, types_n, rows):
    types = jnp.broadcast_to(type_ref[level : level + 1], (rows, type_ref.shape[1]))
    return [jnp.where(types == t, 1.0, 0.0).astype(BF16) for t in range(types_n)]


def mm(a, b):
    return jnp.dot(a, b, preferred_element_type=F32)


def pair_lane(s, l, species):
    return s * (LANES // species) + l


def placed(pieces, rows):
    lane = lane_index((rows, LANES))
    tile = jnp.zeros((rows, LANES), F32)
    for array, source, target, count in pieces:
        moved = pltpu.roll(array, (target - source) % LANES, 1) if target != source else array
        tile = jnp.where((lane >= target) & (lane < target + count), moved, tile)
    return tile


def summed(terms):
    while len(terms) > 1:
        terms = [a + b for a, b in zip(terms[::2], terms[1::2])]
    return terms[0]


def high_low(x):
    hi = x.astype(BF16).astype(F32)
    return hi, x - hi


def table_parts(table_ref, s, t):
    dofs, wide_n = table_ref.shape[2:]
    return high_low(jnp.concatenate([table_ref[s, t], jnp.zeros((dofs, LANES - wide_n), F32)], axis=1))


def source_rows(hi, lo, dofs):
    twice = jnp.where(lane_index(hi.shape) < dofs, hi, pltpu.roll(hi, dofs, 1))
    return jnp.concatenate([twice, lo[:, :dofs]], axis=1).astype(BF16)


def fill_top_tables(table_ref, a_top_ref, c1_ref, c2_ref, small_ref, coef_ref):
    species, types_n, dofs, _ = table_ref.shape
    trace = small_ref.shape[2]
    rest = dofs - trace
    share = LANES // species
    below = []
    for s in range(species):
        tops, single = [], []
        for t in range(types_n):
            hi, lo = (part[rest:] for part in table_parts(table_ref, s, t))
            small_ref[s, t] = table_ref[s, t, rest:, dofs:]
            tops.append(source_rows(hi, lo, dofs))
            pieces = [(hi, dofs, 0, trace), (hi, dofs, trace, trace), (lo, dofs, 2 * trace, trace)]
            single.append(placed(pieces, trace))
            below.append((hi + lo, dofs, s * share + t * trace, trace))
        a_top_ref[s] = jnp.concatenate(tops, axis=0)
        c1_ref[s] = jnp.concatenate(single, axis=0).astype(BF16)[:, : 3 * trace]
    fill_coefs(coef_ref, small_ref)
    below = placed(below, trace)
    products = []
    for t in range(types_n):
        terms = [coef_ref[t, k] * below[k : k + 1] for k in range(trace)]
        products.append(high_low(summed(terms)))
    for s in range(species):
        double = []
        for t in range(types_n):
            at = s * share + t * trace
            for hi, lo in products:
                pieces = [(hi, at, 0, trace), (hi, at, trace, trace), (lo, at, 2 * trace, trace)]
                double.append(placed(pieces, trace))
        c2_ref[s] = jnp.concatenate(double, axis=0).astype(BF16)[:, : 3 * trace]


def fill_late_tables(table_ref, a_rest_ref, c_ref):
    species, types_n, dofs, _ = table_ref.shape
    count = c_ref.shape[2]
    trace = count // (3 * types_n)
    rest = dofs - trace
    for s in range(species):
        parts = [table_parts(table_ref, s, t) for t in range(types_n)]
        a_rest_ref[s] = jnp.concatenate([source_rows(hi[:rest], lo[:rest], dofs) for hi, lo in parts], axis=0)
        tiles = []
        for start in range(0, count, LANES):
            pieces = []
            for at in range(start, min(count, start + LANES), trace):
                k = at // trace
                pieces.append((parts[k // 3][(0, 0, 1)[k % 3]], dofs, at - start, trace))
            tile = placed(pieces, dofs)
            tiles.append(jnp.concatenate([tile[rest:], tile[:rest]], axis=0).astype(BF16))
        c_ref[s] = jnp.concatenate(tiles, axis=1)[:, :count]


def load_kernel(
    conc_hbm, vel_hbm, type_hbm, table_hbm, inlet_hbm, x_ref, vel_ref, type_ref, table_ref, inlet_ref, right_ref, left_ref,
    sems, small_sems,
):
    species, tiles_n, levels, dofs, _ = x_ref.shape
    trace = right_ref.shape[0]
    stride = dofs // trace
    small = ((vel_hbm, vel_ref), (type_hbm, type_ref), (table_hbm, table_ref), (inlet_hbm, inlet_ref))
    small = [pltpu.make_async_copy(*ends, small_sems.at[i]) for i, ends in enumerate(small)]
    copies = []
    small[0].start()
    for i in [0, tiles_n - 1, *range(1, tiles_n - 1)]:
        for s in range(species):
            block = conc_hbm.at[s, :, :, pl.ds(i * LANES, LANES)]
            copies.append(pltpu.make_async_copy(block, x_ref.at[s, i], sems.at[s * tiles_n + i]))
            copies[-1].start()
    for copy in small[1:]:
        copy.start()
    small[0].wait()
    lane = lane_index((levels, LANES))
    on_diag = lane % (LANES // species) == lax.broadcasted_iota(jnp.int32, lane.shape, 0)
    face = jnp.broadcast_to(vel_ref[:, :1], (levels, LANES))
    face = jnp.sum(jnp.where(on_diag, face, 0.0), axis=0, keepdims=True)
    left_ref[trace:] = jnp.broadcast_to(face, (left_ref.shape[0] - trace, LANES))
    for copy in copies[: 2 * species]:
        copy.wait()
    lane = lane_index((trace, LANES))
    right = jnp.zeros((trace, LANES), F32)
    left = jnp.zeros((trace, LANES), F32)
    for s in range(species):
        for l in range(levels):
            p = pair_lane(s, l, species)
            last = x_ref[s, tiles_n - 1, l, pl.ds(stride - 1, trace, stride=stride), :]
            first = x_ref[s, 0, l, pl.ds(0, trace, stride=stride), :]
            right = jnp.where(lane == p, pltpu.roll(last, (p + 1) % LANES, 1), right)
            left = jnp.where(lane == p, pltpu.roll(first, p, 1) if p else first, left)
    right_ref[...] = right
    left_ref[:trace] = left
    for copy in copies[2 * species :] + small[1:]:
        copy.wait()


def fill_coefs(coef_ref, small_ref):
    types_n, trace, _, width = coef_ref.shape
    species = small_ref.shape[0]
    which = lane_index((trace, width)) // (width // species)
    for t in range(types_n):
        for j in range(trace):
            value = jnp.broadcast_to(small_ref[0, t, :, j : j + 1], (trace, width))
            for s in range(1, species):
                other = jnp.broadcast_to(small_ref[s, t, :, j : j + 1], (trace, width))
                value = jnp.where(which == s, other, value)
            coef_ref[t, j] = value


def two_levels(trace_in, c2_ref, s, types, trace):
    return pick(mm(c2_ref[s], stacked_parts(trace_in)), types, trace)


def one_level(trace_in, c1_ref, s, types, trace):
    return pick(mm(c1_ref[s], stacked_parts(trace_in)), types, trace)


def inner_kernel(
    x_ref, vel_ref, type_ref, table_ref, inlet_ref, source_hbm, mid_top_ref, offset_ref, a_top_ref, c1_ref, c2_ref,
    small_ref, coef_ref, source_ref, store_sems,
):
    species, levels, tiles_n, dofs, _ = source_ref.shape
    columns = tiles_n * LANES
    trace = inlet_ref.shape[1]
    types_n = small_ref.shape[1]
    stride = dofs // trace
    fill_top_tables(table_ref, a_top_ref, c1_ref, c2_ref, small_ref, coef_ref)
    lane = lane_index((trace, columns))
    zero, three = pl.ds(0, trace, stride=stride), pl.ds(stride - 1, trace, stride=stride)
    stores = []
    tops = [[] for _ in range(species)]
    traces = []
    start = (lax.axis_index("flow") == 0).astype(F32)
    for l in range(levels):
        velocity = jnp.broadcast_to(vel_ref[l : l + 1], (trace, columns))
        plus = jnp.where(lane > 0, jnp.maximum(velocity, 0.0), 0.0)
        minus = jnp.minimum(velocity, 0.0)
        types = jnp.broadcast_to(type_ref[l : l + 1], (8, columns))
        for s in range(species):
            views = [x_ref.at[s, i, l] for i in range(tiles_n)]
            low = jnp.concatenate([view[zero, :] for view in views], axis=1)
            high = jnp.concatenate([view[three, :] for view in views], axis=1)
            flux = plus * pltpu.roll(high, 1, 1) + minus * low
            out = jnp.where(lane == columns - 1, 0.0, pltpu.roll(flux, columns - 1, 1))
            low, high = low + flux, high - out
            for i, view in enumerate(views):
                source_ref[s, l, i] = view[...]
                source_ref[s, l, i, zero, :] = low[:, i * LANES : (i + 1) * LANES]
                source_ref[s, l, i, three, :] = high[:, i * LANES : (i + 1) * LANES]
            source = jnp.concatenate([source_ref[s, l, i] for i in range(tiles_n)], axis=1)
            top = pick(mm(a_top_ref[s], stacked_parts(source)), types, trace)
            tops[s].append(top)
            mid_top_ref[s, l] = top[:, LANES : columns - LANES]
        if l % 2:
            below = jnp.broadcast_to(type_ref[l - 1 : l], (8, columns))
            both = below * types_n + types
            for s in range(species):
                lower, upper = tops[s][-2:]
                if l == 1:
                    traces.append(inlet_ref[s] * start)
                added = one_level(lower, c1_ref, s, types, trace) + upper
                traces[s] = two_levels(traces[s], c2_ref, s, both, trace) + added
        if (l + 1) % (levels // 2) == 0:
            part = pl.ds(l + 1 - levels // 2, levels // 2)
            for s in range(species):
                ends = source_ref.at[s, part], source_hbm.at[s, part]
                stores.append(pltpu.make_async_copy(*ends, store_sems.at[len(stores)]))
                stores[-1].start()
    for s in range(species):
        offset_ref[s] = traces[s]
    for copy in stores:
        copy.wait()


def trace_step(state, types, coef_ref):
    types_n, trace = coef_ref.shape[:2]
    chosen = [types == float(t) for t in range(1, types_n)]
    terms = []
    for j in range(trace):
        coef = coef_ref[0, j]
        for t in range(1, types_n):
            coef = jnp.where(chosen[t - 1], coef_ref[t, j], coef)
        terms.append(coef * state[j : j + 1])
    return summed(terms)


def halo_kernel(
    offset_ref, type_ref, a_top_ref, coef_ref, own_right_ref, own_left_ref, from_left_ref, from_right_ref,
    send_ref, flux_ref, delta_ref,
):
    species, trace, columns = offset_ref.shape
    levels = type_ref.shape[0]
    dofs = delta_ref.shape[0]
    stride = dofs // trace
    lat, lat_n = lax.axis_index("lat"), lax.axis_size("lat")
    has_left = (lat > 0).astype(F32)
    has_right = (lat < lat_n - 1).astype(F32)
    far_edge = LANES // species // 2

    def face(ref):
        return jnp.broadcast_to(ref[trace : trace + 1], (trace, LANES))

    coming = jnp.maximum(face(own_left_ref), 0.0) * from_left_ref[...] * has_left
    velocity = face(from_right_ref)
    leaving = jnp.maximum(velocity, 0.0) * own_right_ref[...]
    leaving = -(leaving + jnp.minimum(velocity, 0.0) * from_right_ref[:trace]) * has_right
    flux_ref[0] = coming
    flux_ref[1] = leaving
    lane = lane_index((trace, LANES))
    within = lane % (LANES // species)
    near, far = within < levels, (within >= far_edge) & (within < far_edge + levels)
    delta_ref[...] = jnp.zeros((dofs, LANES), F32)
    delta_ref[pl.ds(0, trace, stride=stride), :] = jnp.where(near, coming, 0.0)
    delta_ref[pl.ds(stride - 1, trace, stride=stride), :] = jnp.where(
        far, pltpu.roll(leaving, far_edge, 1), 0.0
    )
    types = type_ref[...].astype(F32)
    sub = lax.broadcasted_iota(jnp.int32, (levels, LANES), 0)
    spot = lane_index((levels, LANES)) % (LANES // species)
    here = jnp.where(spot == sub, jnp.broadcast_to(types[:, :1], (levels, LANES)), 0.0)
    there = jnp.broadcast_to(types[:, columns - 1 :], (levels, LANES))
    here = here + jnp.where(spot == sub + far_edge, there, 0.0)
    edge_types = jnp.broadcast_to(jnp.sum(here, axis=0, keepdims=True), (trace, LANES))
    parts = stacked_parts(delta_ref[...])
    added = pick(mm(a_top_ref[0], parts), edge_types[:8], trace)
    for s in range(1, species):
        other = pick(mm(a_top_ref[s], parts), edge_types[:8], trace)
        added = jnp.where(lane < s * (LANES // species), added, other)
    state = added
    for l in range(1, levels):
        state = trace_step(state, pltpu.roll(edge_types, LANES - l, 1), coef_ref)
        state = state + pltpu.roll(added, LANES - l, 1)
    traces = []
    for s in range(species):
        at = pair_lane(s, 0, species)
        first = pltpu.roll(state, LANES - at, 1) if at else state
        last = pltpu.roll(state, LANES - 1 - at - far_edge, 1)
        first = offset_ref[s, :, :LANES] + jnp.where(lane == 0, first, 0.0)
        last = offset_ref[s, :, columns - LANES :] + jnp.where(lane == LANES - 1, last, 0.0)
        traces.append(jnp.concatenate([first, offset_ref[s, :, LANES : columns - LANES], last], axis=1))
    width = send_ref.shape[2]
    if width == LANES:
        half = width // 2
        low = lane_index((trace, width)) < half
        low_t = lane_index((levels, width)) < half
        for k in range(columns // width):
            a, b = (traces[s][:, k * width : (k + 1) * width] for s in (0, 1))
            t = types[:, k * width : (k + 1) * width]
            swapped = pltpu.roll(t, half, 1)
            send_ref[2 * k, :trace] = jnp.where(low, a, pltpu.roll(b, half, 1))
            send_ref[2 * k + 1, :trace] = jnp.where(low, pltpu.roll(a, half, 1), b)
            send_ref[2 * k, trace:] = jnp.where(low_t, t, swapped)
            send_ref[2 * k + 1, trace:] = jnp.where(low_t, swapped, t)
    else:
        for s in range(species):
            send_ref[s, :trace] = traces[s]
            send_ref[s, trace:] = types


def rest_kernel(
    source_hbm, flux_ref, type_ref, a_top_ref, table_ref, small_ref, rest_ref, edge_top_ref, c_ref, coef_ref, a_rest_ref,
    source_ref, sems,
):
    species, levels, tiles_n, dofs, _ = source_ref.shape
    columns = tiles_n * LANES
    rest = rest_ref.shape[2]
    trace = dofs - rest
    stride = dofs // trace
    copies = []
    for h in range(2):
        for s in range(species):
            part = pl.ds(h * (levels // 2), levels // 2)
            ends = source_hbm.at[s, part], source_ref.at[s, part]
            copies.append(pltpu.make_async_copy(*ends, sems.at[len(copies)]))
            copies[-1].start()
    fill_late_tables(table_ref, a_rest_ref, c_ref)
    fill_coefs(coef_ref, small_ref)
    lane = lane_index((trace, LANES))
    zero, three = pl.ds(0, trace, stride=stride), pl.ds(stride - 1, trace, stride=stride)
    for l in range(levels):
        types = jnp.broadcast_to(type_ref[l : l + 1], (8, columns))
        edge_types = jnp.concatenate([types[:, :LANES], types[:, columns - LANES :]], axis=1)
        if l % (levels // 2) == 0:
            for s in range(species):
                copies[(l // (levels // 2)) * species + s].wait()
        for s in range(species):
            p = pair_lane(s, l, species)
            first = pltpu.roll(flux_ref[0], (LANES - p) % LANES, 1)
            last = pltpu.roll(flux_ref[1], LANES - 1 - p, 1)
            end = tiles_n - 1
            low, high = source_ref[s, l, 0, zero, :], source_ref[s, l, end, three, :]
            source_ref[s, l, 0, zero, :] = low + jnp.where(lane == 0, first, 0.0)
            source_ref[s, l, end, three, :] = high + jnp.where(lane == LANES - 1, last, 0.0)
            parts = stacked_parts(jnp.concatenate([source_ref[s, l, i] for i in range(tiles_n)], axis=1))
            rest_ref[s, l] = pick(mm(a_rest_ref[s], parts), types, rest)
            outer = jnp.concatenate([parts[:, :LANES], parts[:, columns - LANES :]], axis=1)
            edge_top_ref[s, l] = pick(mm(a_top_ref[s], outer), edge_types, trace)


def owner_kernel(coef_ref, got_ref, out_ref):
    slabs, _, width = got_ref.shape
    trace = coef_ref.shape[1]
    levels = got_ref.shape[1] - trace
    out_ref[0] = jnp.zeros((trace, width), F32)

    def slab(g, state):
        out_ref[g] = state
        for l in range(levels):
            types = jnp.broadcast_to(got_ref[g, trace + l : trace + l + 1], (trace, width))
            state = trace_step(state, types, coef_ref)
        return state + got_ref[g, :trace]

    last = lax.fori_loop(1, slabs - 1, slab, got_ref[0, :trace])
    out_ref[slabs - 1] = last


def final_kernel(
    mid_top_ref, edge_top_ref, rest_ref, type_ref, inlet_ref, c_ref, c1_ref, c2_ref, got_ref, out_hbm, o_ref, sems
):
    species, levels, rest, columns = rest_ref.shape
    trace = inlet_ref.shape[1]
    types_n = c_ref.shape[2] // (3 * trace)
    width = got_ref.shape[2]
    is_first = lax.axis_index("flow") == 0
    if width == LANES:
        half = width // 2
        low = lane_index((trace, width)) < half
        tiles = [[], []]
        for k in range(columns // width):
            a, b = got_ref[2 * k], got_ref[2 * k + 1]
            tiles[0].append(jnp.where(low, a, pltpu.roll(b, half, 1)))
            tiles[1].append(jnp.where(low, pltpu.roll(a, half, 1), b))
        received = [jnp.concatenate(t, axis=1) for t in tiles]
    else:
        received = [got_ref[s] for s in range(species)]
    both = range(species)
    inflow = {(0, s): jnp.where(is_first, inlet_ref[s], received[s]) for s in both}
    types = [jnp.broadcast_to(type_ref[l : l + 1], (8, columns)) for l in range(levels)]

    def top(s, l):
        edge = edge_top_ref[s, l]
        return jnp.concatenate([edge[:, :LANES], mid_top_ref[s, l], edge[:, LANES:]], axis=1)

    added = {}
    for l in range(0, levels - 2, 2):
        for s in both:
            added[l, s] = one_level(top(s, l), c1_ref, s, types[l + 1], trace) + top(s, l + 1)
    copies = []

    def solve(l):
        masks = masks_of(type_ref, l, types_n, trace)
        for s in both:
            moved = mm(c_ref[s], masked_parts(inflow[l, s], masks))
            outflow = moved[:trace] + top(s, l)
            if l % 2 == 0:
                inflow[l + 1, s] = outflow
            o_ref[s, l, rest:] = outflow.astype(BF16)
            o_ref[s, l, :rest] = (moved[trace:] + rest_ref[s, l]).astype(BF16)
            copies.append(pltpu.make_async_copy(o_ref.at[s, l], out_hbm.at[s, l], sems.at[s * levels + l]))
            copies[-1].start()

    for l in range(0, levels, 2):
        if l + 2 < levels:
            for s in both:
                ahead = two_levels(inflow[l, s], c2_ref, s, types[l] * types_n + types[l + 1], trace)
                inflow[l + 2, s] = ahead + added[l, s]
        if l:
            solve(l - 1)
        solve(l)
    solve(levels - 1)
    for copy in copies:
        copy.wait()


def on_device(conc_old, lat_velocity, elem_type, inlet_trace, solve_table):
    species, levels, dofs, columns = conc_old.shape
    types_n = solve_table.shape[1]
    trace = inlet_trace.shape[1]
    flow_n = lax.axis_size("flow")
    lat_n = lax.axis_size("lat")
    pairs = species * levels
    tiles = columns // LANES
    inner = columns - 2 * LANES
    rest = dofs - trace

    def shape(dims, kind=F32):
        return jax.ShapeDtypeStruct(dims, kind)

    def held(dims, kind=F32):
        return pltpu.VMEM(dims, kind)

    def far(array):
        return pltpu.with_memory_space_constraint(array, pltpu.HBM)

    def cost(rows, count):
        flops = 2 * 3 * types_n * rows * dofs * count * pairs
        return pl.CostEstimate(
            flops=flops, bytes_accessed=8 * pairs * dofs * columns, transcendentals=0
        )

    x, velocity, types, table, inlet, right, left = pl.pallas_call(
        load_kernel,
        out_shape=(
            held((species, tiles, levels, dofs, LANES)),
            held(lat_velocity.shape),
            held(elem_type.shape, elem_type.dtype),
            held(solve_table.shape),
            held(inlet_trace.shape),
            shape((trace, LANES)),
            shape((trace + 8, LANES)),
        ),
        in_specs=[HBM] * 5,
        out_specs=(VMEM,) * 7,
        scratch_shapes=[pltpu.SemaphoreType.DMA((species * tiles,)), pltpu.SemaphoreType.DMA((4,))],
        compiler_params=PARAMS,
        name="load_edges",
    )(far(conc_old), far(lat_velocity), far(elem_type), far(solve_table), far(inlet_trace))
    from_left = lax.ppermute(right, "lat", [(i, (i + 1) % lat_n) for i in range(lat_n)])
    from_right = lax.ppermute(left, "lat", [((i + 1) % lat_n, i) for i in range(lat_n)])


    source_shape = (species, levels, tiles, dofs, LANES)
    source, mid_top, offset, a_top, c_one, c_two, small, coef = pl.pallas_call(
        inner_kernel,
        out_shape=(
            pltpu.HBM(source_shape, F32),
            held((species, levels, trace, inner)),
            held((species, trace, columns)),
            held((species, types_n * trace, 3 * dofs), BF16),
            held((species, types_n * trace, 3 * trace), BF16),
            held((species, types_n * types_n * trace, 3 * trace), BF16),
            held((species, types_n, trace, trace)),
            held((types_n, trace, trace, LANES)),
        ),
        in_specs=[VMEM] * 5,
        out_specs=(HBM,) + (VMEM,) * 7,
        scratch_shapes=[pltpu.VMEM(source_shape, F32), pltpu.SemaphoreType.DMA((2 * species,))],
        compiler_params=PARAMS,
        cost_estimate=cost(dofs, columns),
        name="inner_sources",
    )(x, velocity, types, table, inlet)

    packed = 2 * columns == LANES * flow_n and species == 2
    send_shape = (flow_n, trace + levels, LANES) if packed else (species, trace + levels, columns)
    send, flux = pl.pallas_call(
        halo_kernel,
        out_shape=(shape(send_shape), held((2, trace, LANES))),
        in_specs=[VMEM] * 8,
        out_specs=(VMEM, VMEM),
        scratch_shapes=[pltpu.VMEM((dofs, LANES), F32)],
        compiler_params=PARAMS,
        name="halo_offsets",
    )(offset, types, a_top, coef, right, left, from_left, from_right)
    part = columns // flow_n
    if not packed:
        send = send.reshape(species, trace + levels, flow_n, part)
        send = send.transpose(2, 1, 0, 3).reshape(flow_n, trace + levels, species * part)
    got = lax.all_to_all(send, "flow", 0, 0, tiled=True)

    rest_terms, edge_top, c_all, owner_coef = pl.pallas_call(
        rest_kernel,
        out_shape=(
            held((species, levels, rest, columns)),
            held((species, levels, trace, 2 * LANES)),
            held((species, dofs, 3 * types_n * trace), BF16),
            held((types_n, trace, trace, species * part)),
        ),
        in_specs=[HBM] + [VMEM] * 5,
        out_specs=(VMEM,) * 4,
        scratch_shapes=[
            pltpu.VMEM((species, types_n * rest, 3 * dofs), BF16),
            pltpu.VMEM(source_shape, F32),
            pltpu.SemaphoreType.DMA((2 * species,)),
        ],
        compiler_params=PARAMS,
        cost_estimate=cost(rest, columns),
        name="rest_sources",
    )(far(source), flux, types, a_top, table, small)
    back = pl.pallas_call(
        owner_kernel,
        out_shape=shape((flow_n, trace, species * part)),
        in_specs=[VMEM, VMEM],
        out_specs=VMEM,
        compiler_params=PARAMS,
        name="owner_sweep",
    )(owner_coef, got)
    traces = lax.all_to_all(back, "flow", 0, 0, tiled=True)
    if not packed:
        traces = traces.reshape(flow_n, trace, species, part)
        traces = traces.transpose(2, 1, 0, 3).reshape(species, trace, columns)

    return pl.pallas_call(
        final_kernel,
        out_shape=shape(conc_old.shape, BF16),
        in_specs=[VMEM] * 9,
        out_specs=HBM,
        scratch_shapes=[
            pltpu.VMEM(conc_old.shape, BF16),
            pltpu.SemaphoreType.DMA((pairs,)),
        ],
        compiler_params=PARAMS,
        name="final_sweep",
    )(mid_top, edge_top, rest_terms, types, inlet, c_all, c_one, c_two, traces)


def solution(mesh):
    in_specs = (
        P(None, "flow", None, "lat"),
        P("flow", "lat"),
        P("flow", "lat"),
        P(None, None, "lat"),
        P(),
    )
    out_specs = P(None, "flow", None, "lat")
    return jax.shard_map(
        on_device, mesh=mesh, in_specs=in_specs, out_specs=out_specs, check_vma=False
    )
```

time: 35.6 us -> 34.6 us (0.972)
  waiting for transfers between devices: 7.02 us -> 4.59 us
  Pallas kernels: 10.7 us -> 12.1 us
    pallas_call x3, Pallas kernels: 5.44 us -> 6.86 us  [the longest x1 2.86 us: on_device(): pl.pallas_call(rest_kernel, out_shape=(held((species, levels, rest, colum...]
    ppermute x1, waiting for transfers between devices: 1.69 us -> 0.33 us  [on_device(): lax.ppermute(right, 'lat', [(i, (i + 1) % lat_n) for i in range(lat_n)])]
    all_to_all x1, waiting for transfers between devices: 5.33 us -> 4.26 us  [on_device(): got = lax.all_to_all(send, 'flow', 0, 0, tiled=True)]
  transfers between devices with their start and end apart: 3 -> 3, of which waited for: 2 -> 2; matrix products, arithmetic and copies ran while one was open for 0% -> 0% of each run, Pallas kernels for 9% -> 16%
where the time goes in v4:
time: 34.6 us; the launch traced here: 34.3 us
  Pallas kernels  12.1 us (35%)
  blocking collectives  9.29 us (27%)
  starting transfers between devices  8.3 us (24%)
  waiting for transfers between devices  4.59 us (13%)
    all_to_all x1, blocking collectives, on_device(): traces = lax.all_to_all(back, 'flow', 0, 0, tiled=True)  9.29 us
    all_to_all x1, starting transfers between devices, on_device(): got = lax.all_to_all(send, 'flow', 0, 0, tiled=True)  5.81 us
    all_to_all x1, waiting for transfers between devices, on_device(): got = lax.all_to_all(send, 'flow', 0, 0, tiled=True)  4.26 us
    pallas_call x1, Pallas kernels, on_device(): pl.pallas_call(rest_kernel, out_shape=(held((species, levels, rest, colum...  2.86 us
    pallas_call x1, Pallas kernels, on_device(): pl.pallas_call(inner_kernel, out_shape=(pltpu.HBM(source_shape, F32), hel...  2.73 us
    ppermute x1, starting transfers between devices, on_device(): lax.ppermute(left, 'lat', [((i + 1) % lat_n, i) for i in range(lat_n)])  2.49 us
    pallas_call x1, Pallas kernels, on_device(): pl.pallas_call(final_kernel, out_shape=shape(conc_old.shape, BF16), in_sp...  2.11 us
    pallas_call x1, Pallas kernels, on_device(): pl.pallas_call(load_kernel, out_shape=(held((species, tiles, levels, dofs...  1.75 us
  transfers between devices with their start and end apart: 3, of which 2 were waited for; matrix products, arithmetic and copies ran while one was open for 0% of the time, Pallas kernels for 16%

profile of v4, /device:TPU:0, one launch (start us, length us, event | category | flops | bytes accessed | tf_op | source)
XLA Modules:
  0.0 34.3 jit_solution(12404879173952604342)
XLA Ops:
  0.0 1.7 %load_edges.1 = (f32[2,4,8,64,128]{4,3,2,1,0:T(8,128)S(1)}, f32[8,512]{1,0:T(8,128)S(1)}, s32[8,512]{1,0:T(8,128)S(1)}, f32[2,4,64,80]{3,2,1,0:T(8,128)S(1)}, f3...) custom-call(f32[2,8,64,512]{3,2,1,0:T(8,128)} %conc_hbm.1, f32[8,512]{1,0:T(8,128)} %vel_hbm.1, ...), custom_call_target="tpu_custom_call" | custom-call | tf_op jit(solution)/shard_map/load_edges/pallas_call | solution.py:489
  1.8 2.5 %collective-permute-start.1 = (f32[24,128]{1,0:T(8,128)S(1)}, f32[24,128]{1,0:T(8,128)S(1)}, u32[]{:S(2)}, u32[]{:S(2)}) collective-permute-start(f32[24,128]{1,0:T(8,128)S(1)} %get-tuple-element.37.own_left_ref), channel_id=1, source_target_pairs={{1,0},{2,1},{3,2},{0,3},{5,4},{6,5},{7,6},{4,7},{9,8},{10,9},{11,1... | collective-permute-start | bytes 36872 | tf_op jit(solution)/shard_map/ppermute | solution.py:507
  4.2 0.0 collective-permute-start
  4.2 2.7 %inner_sources.1 = (f32[2,8,4,64,128]{4,3,2,1,0:T(8,128)}, f32[2,8,16,256]{3,2,1,0:T(8,128)S(1)}, f32[2,16,512]{2,1,0:T(8,128)S(1)}, bf16[2,64,192]{2,1,0:T(8,12...) custom-call(f32[2,4,8,64,128]{4,3,2,1,0:T(8,128)S(1)} %get-tuple-ele, ...), custom_call_target="tpu_custom_call" | custom-call | flops 805306368 | bytes 4194304 | tf_op jit(solution)/shard_map/inner_sources/pallas_call | solution.py:511
  7.0 0.3 collective-permute-done.from_left_ref
  7.3 0.0 collective-permute-done.1.from_right_ref
  7.3 1.3 %halo_offsets.1 = (f32[8,24,128]{2,1,0:T(8,128)}, f32[2,16,128]{2,1,0:T(8,128)S(1)}) custom-call(f32[2,16,512]{2,1,0:T(8,128)S(1)} %get-tuple-element.33.offset_ref, s32[8,512]{1,0:T(8,128)S(1)} %get-tuple-element.28.type_ref, bf16[2,64,192]{2,1,0:T(8,128)(2,1)S(1)} %get-tuple-element.34.a_top_ref, f32[4,16,16,128]{3,2,1,0:T(8,128)S(1)} %get-tuple-element.35.coef_ref, ...), custom_call_target="tpu_custom_call" | custom-call | tf_op jit(solution)/shard_map/halo_offsets/pallas_call | solution.py:533
  8.6 5.8 %all-to-all-start = ((f32[8,24,128]{2,1,0:T(8,128)}), f32[8,24,128]{2,1,0:T(8,128)S(1)}, u32[]{:S(2)}, u32[]{:S(2)}) async-start(f32[8,24,128]{2,1,0:T(8,128)} %get-tuple-element.46), calls=%async_computation | async-start | bytes 196608 | tf_op jit(solution)/shard_map/all_to_all | solution.py:546
  14.4 2.9 %rest_sources.1 = (f32[2,8,48,512]{3,2,1,0:T(8,128)S(1)}, f32[2,8,16,256]{3,2,1,0:T(8,128)S(1)}, bf16[2,64,192]{2,1,0:T(8,128)(2,1)S(1)}, f32[4,16,16,128]{3,2,1,0:T(8,128)S(1)}) custom-call(f32[2,8,4,64,128]{4,3,2,1,0:T(8,128)} %get-tuple-element.32.source_hbm, f32[2,16,128]{2,1,0:T(8,128)S(1)} %get-tuple-element.38.flux_ref, ...), custom_call_target="tpu_custom_call" | custom-call | flops 603979776 | bytes 4194304 | tf_op jit(solution)/shard_map/rest_sources/pallas_call | solution.py:548
  17.3 4.3 %all-to-all-done.got_ref = f32[8,24,128]{2,1,0:T(8,128)S(1)} async-done(((f32[8,24,128]{2,1,0:T(8,128)}), f32[8,24,128]{2,1,0:T(8,128)S(1)}, u32[]{:S(2)}, u32[]{:S(2)}) %all-to-all-start) | async-done | bytes 98336 | tf_op jit(solution)/shard_map/all_to_all | solution.py:546
  21.5 1.3 %owner_sweep.1 = f32[8,16,128]{2,1,0:T(8,128)S(1)} custom-call(f32[4,16,16,128]{3,2,1,0:T(8,128)S(1)} %get-tuple-element.45.coef_ref, f32[8,24,128]{2,1,0:T(8,128)S(1)} %all-to-all-done.got_ref), custom_call_target="tpu_custom_call" | custom-call | tf_op jit(solution)/shard_map/owner_sweep/pallas_call | solution.py:567
  22.9 9.3 %all_to_all.10.got_ref = f32[8,16,128]{2,1,0:T(8,128)S(1)} all-to-all(f32[8,16,128]{2,1,0:T(8,128)S(1)} %owner_sweep.1), channel_id=1, replica_groups=mesh['flow'=8,'lat'=4] {'flow'}, dimensions={0} | all-to-all | bytes 131072 | tf_op jit(solution)/shard_map/all_to_all | solution.py:575
  32.2 2.1 %final_sweep.1 = bf16[2,8,64,512]{3,2,1,0:T(8,128)(2,1)} custom-call(f32[2,8,16,256]{3,2,1,0:T(8,128)S(1)} %get-tuple-element.31.mid_top_ref, f32[2,8,16,256]{3,2,1,0:T(8,128)S(1)} %get-tuple-element.40.edge_top_ref, f32[2,8,48,512]{3,2,1,0:T(8,128)S(1)} %get-tuple-element.41.rest_ref, s32[8,512]{1,0:T(8,128)S(1)} %get-tuple-element.28.type_ref, ...), custom_call_target="tpu_custom_call" | custom-call | tf_op jit(solution)/shard_map/final_sweep/pallas_call | solution.py:580
Async XLA Ops:
  1.8 5.6 %collective-permute-start.1 = (f32[24,128]{1,0:T(8,128)S(1)}, f32[24,128]{1,0:T(8,128)S(1)}, u32[]{:S(2)}, u32[]{:S(2)}) collective-permute-start(f32[24,128]{1,0:T(8,128)S(1)} %get-tuple-element.37.own_left_ref), channel_id=1, source_target_pairs={{1,0},{2,1},{3,2},{0,3},{5,4},{6,5},{7,6},{4,7},{9,8},{10,9},{11,1... | collective-permute-start | bytes 36872 | tf_op jit(solution)/shard_map/ppermute | solution.py:507
  4.2 3.1 %collective-permute-start = (f32[16,128]{1,0:T(8,128)S(1)}, f32[16,128]{1,0:T(8,128)S(1)}, u32[]{:S(2)}, u32[]{:S(2)}) collective-permute-start(f32[16,128]{1,0:T(8,128)S(1)} %get-tuple-element.36.own_right_ref), channel_id=1, source_target_pairs={{0,1},{1,2},{2,3},{3,0},{4,5},{5,6},{6,7},{7,4},{8,9},{9,10},{10,1... | collective-permute-start | bytes 24584 | tf_op jit(solution)/shard_map/ppermute | solution.py:506
  8.6 12.9 %all-to-all-start = ((f32[8,24,128]{2,1,0:T(8,128)}), f32[8,24,128]{2,1,0:T(8,128)S(1)}, u32[]{:S(2)}, u32[]{:S(2)}) async-start(f32[8,24,128]{2,1,0:T(8,128)} %get-tuple-element.46), calls=%async_computation | async-start | bytes 196608 | tf_op jit(solution)/shard_map/all_to_all | solution.py:546

commit v5 on v4

--- a/solution.py
+++ b/solution.py
@@ -142,7 +142,7 @@
 
 def load_kernel(
     conc_hbm, vel_hbm, type_hbm, table_hbm, inlet_hbm, x_ref, vel_ref, type_ref, table_ref, inlet_ref, right_ref, left_ref,
-    sems, small_sems,
+    near_ref, far_ref, sems, small_sems,
 ):
     species, tiles_n, levels, dofs, _ = x_ref.shape
     trace = right_ref.shape[0]
@@ -178,6 +178,11 @@
             left = jnp.where(lane == p, pltpu.roll(first, p, 1) if p else first, left)
     right_ref[...] = right
     left_ref[:trace] = left
+    is_even = lax.axis_index("lat") % 2 == 0
+    near_ref[:trace] = jnp.where(is_even, right, left)
+    far_ref[:trace] = jnp.where(is_even, left, right)
+    near_ref[trace:] = left_ref[trace:]
+    far_ref[trace:] = left_ref[trace:]
     for copy in copies[2 * species :] + small[1:]:
         copy.wait()
 
@@ -273,7 +278,7 @@
 
 
 def halo_kernel(
-    offset_ref, type_ref, a_top_ref, coef_ref, own_right_ref, own_left_ref, from_left_ref, from_right_ref,
+    offset_ref, type_ref, a_top_ref, coef_ref, own_right_ref, own_left_ref, near_ref, far_ref,
     send_ref, flux_ref, delta_ref,
 ):
     species, trace, columns = offset_ref.shape
@@ -288,10 +293,13 @@
     def face(ref):
         return jnp.broadcast_to(ref[trace : trace + 1], (trace, LANES))
 
-    coming = jnp.maximum(face(own_left_ref), 0.0) * from_left_ref[...] * has_left
-    velocity = face(from_right_ref)
+    is_even = lat % 2 == 0
+    from_left = jnp.where(is_even, far_ref[:trace], near_ref[:trace])
+    from_right = jnp.where(is_even, near_ref[:trace], far_ref[:trace])
+    coming = jnp.maximum(face(own_left_ref), 0.0) * from_left * has_left
+    velocity = jnp.where(is_even, face(near_ref), face(far_ref))
     leaving = jnp.maximum(velocity, 0.0) * own_right_ref[...]
-    leaving = -(leaving + jnp.minimum(velocity, 0.0) * from_right_ref[:trace]) * has_right
+    leaving = -(leaving + jnp.minimum(velocity, 0.0) * from_right) * has_right
     flux_ref[0] = coming
     flux_ref[1] = leaving
     lane = lane_index((trace, LANES))
@@ -486,7 +494,7 @@
             flops=flops, bytes_accessed=8 * pairs * dofs * columns, transcendentals=0
         )
 
-    x, velocity, types, table, inlet, right, left = pl.pallas_call(
+    x, velocity, types, table, inlet, right, left, near, far_side = pl.pallas_call(
         load_kernel,
         out_shape=(
             held((species, tiles, levels, dofs, LANES)),
@@ -494,17 +502,22 @@
             held(elem_type.shape, elem_type.dtype),
             held(solve_table.shape),
             held(inlet_trace.shape),
-            shape((trace, LANES)),
+            held((trace, LANES)),
+            held((trace + 8, LANES)),
+            shape((trace + 8, LANES)),
             shape((trace + 8, LANES)),
         ),
         in_specs=[HBM] * 5,
-        out_specs=(VMEM,) * 7,
+        out_specs=(VMEM,) * 9,
         scratch_shapes=[pltpu.SemaphoreType.DMA((species * tiles,)), pltpu.SemaphoreType.DMA((4,))],
         compiler_params=PARAMS,
         name="load_edges",
     )(far(conc_old), far(lat_velocity), far(elem_type), far(solve_table), far(inlet_trace))
-    from_left = lax.ppermute(right, "lat", [(i, (i + 1) % lat_n) for i in range(lat_n)])
-    from_right = lax.ppermute(left, "lat", [((i + 1) % lat_n, i) for i in range(lat_n)])
+    assert lat_n % 2 == 0
+    near_got = lax.ppermute(near, "lat", [(i, i ^ 1) for i in range(lat_n)])
+    swap = [(i, (i - 1) % lat_n if i % 2 == 0 else (i + 1) % lat_n) for i in range(lat_n)]
+    swap = [(i, j) for i, j in swap if abs(i - j) == 1]
+    far_got = lax.ppermute(far_side, "lat", swap)
 
 
     source_shape = (species, levels, tiles, dofs, LANES)
@@ -538,7 +551,7 @@
         scratch_shapes=[pltpu.VMEM((dofs, LANES), F32)],
         compiler_params=PARAMS,
         name="halo_offsets",
-    )(offset, types, a_top, coef, right, left, from_left, from_right)
+    )(offset, types, a_top, coef, right, left, near_got, far_got)
     part = columns // flow_n
     if not packed:
         send = send.reshape(species, trace + levels, flow_n, part)

time: 34.6 us -> 34.4 us (level); the launches traced: 34.3 us -> 33.7 us
    ppermute x2, starting transfers between devices: 2.49 us -> 1.21 us  [the longest x1 0.65 us: on_device(): far_got = lax.ppermute(far_side, 'lat', swap)]
    all_to_all x1, starting transfers between devices: 5.81 us -> 6.81 us  [on_device(): got = lax.all_to_all(send, 'flow', 0, 0, tiled=True)]
  transfers between devices with their start and end apart: 3 -> 3, of which waited for: 2 -> 1; matrix products, arithmetic and copies ran while one was open for 0% -> 0% of each run, Pallas kernels for 16% -> 17%
where the time goes in v5:
time: 34.4 us; the launch traced here: 33.7 us
  Pallas kernels  12.1 us (35%)
  blocking collectives  9.29 us (27%)
  starting transfers between devices  8.02 us (23%)
  waiting for transfers between devices  4.27 us (12%)
    all_to_all x1, blocking collectives, on_device(): traces = lax.all_to_all(back, 'flow', 0, 0, tiled=True)  9.29 us
    all_to_all x1, starting transfers between devices, on_device(): got = lax.all_to_all(send, 'flow', 0, 0, tiled=True)  6.81 us
    all_to_all x1, waiting for transfers between devices, on_device(): got = lax.all_to_all(send, 'flow', 0, 0, tiled=True)  4.26 us
    pallas_call x1, Pallas kernels, on_device(): pl.pallas_call(rest_kernel, out_shape=(held((species, levels, rest, colum...  2.86 us
    pallas_call x1, Pallas kernels, on_device(): pl.pallas_call(inner_kernel, out_shape=(pltpu.HBM(source_shape, F32), hel...  2.74 us
    pallas_call x1, Pallas kernels, on_device(): pl.pallas_call(final_kernel, out_shape=shape(conc_old.shape, BF16), in_sp...  2.11 us
    pallas_call x1, Pallas kernels, on_device(): pl.pallas_call(load_kernel, out_shape=(held((species, tiles, levels, dofs...  1.75 us
    pallas_call x1, Pallas kernels, on_device(): pl.pallas_call(owner_kernel, out_shape=shape((flow_n, trace, species * pa...  1.34 us
  transfers between devices with their start and end apart: 3, of which 1 were waited for; matrix products, arithmetic and copies ran while one was open for 0% of the time, Pallas kernels for 17%

profile of v5, /device:TPU:0, one launch (start us, length us, event | category | flops | bytes accessed | tf_op | source)
XLA Modules:
  0.0 33.7 jit_solution(12615079434086191803)
XLA Ops:
  0.0 1.7 %load_edges.1 = (f32[2,4,8,64,128]{4,3,2,1,0:T(8,128)S(1)}, f32[8,512]{1,0:T(8,128)S(1)}, s32[8,512]{1,0:T(8,128)S(1)}, f32[2,4,64,80]{3,2,1,0:T(8,128)S(1)}, f3...) custom-call(f32[2,8,64,512]{3,2,1,0:T(8,128)} %conc_hbm.1, ...), custom_call_target="tpu_custom_call" | custom-call | tf_op jit(solution)/shard_map/load_edges/pallas_call | solution.py:497
  1.8 0.6 %collective-permute-start = (f32[24,128]{1,0:T(8,128)S(1)}, f32[24,128]{1,0:T(8,128)S(1)}, u32[]{:S(2)}, u32[]{:S(2)}) collective-permute-start(f32[24,128]{1,0:T(8,128)S(1)} %get-tuple-element.40), channel_id=1, source_target_pairs={{0,1},{1,0},{2,3},{3,2},{4,5},{5,4},{6,7},{7,6},{8,9},{9,8},{10,11... | collective-permute-start | bytes 36872 | tf_op jit(solution)/shard_map/ppermute | solution.py:517
  2.3 0.7 %collective-permute-start.1 = (f32[24,128]{1,0:T(8,128)S(1)}, f32[24,128]{1,0:T(8,128)S(1)}, u32[]{:S(2)}, u32[]{:S(2)}) collective-permute-start(f32[24,128]{1,0:T(8,128)S(1)} %get-tuple-element.41), channel_id=1, source_target_pairs={{1,2},{2,1},{5,6},{6,5},{9,10},{10,9},{13,14},{14,13},{17,18},{18,... | collective-permute-start | bytes 36872 | tf_op jit(solution)/shard_map/ppermute | solution.py:520
  3.0 2.7 %inner_sources.1 = (f32[2,8,4,64,128]{4,3,2,1,0:T(8,128)}, f32[2,8,16,256]{3,2,1,0:T(8,128)S(1)}, f32[2,16,512]{2,1,0:T(8,128)S(1)}, bf16[2,64,192]{2,1,0:T(8,12...) custom-call(f32[2,4,8,64,128]{4,3,2,1,0:T(8,128)S(1)} %get-tuple-ele, ...), custom_call_target="tpu_custom_call" | custom-call | flops 805306368 | bytes 4194304 | tf_op jit(solution)/shard_map/inner_sources/pallas_call | solution.py:524
  5.7 0.0 collective-permute-done.near_ref
  5.7 0.0 collective-permute-done.1.far_ref
  5.7 1.3 %halo_offsets.1 = (f32[8,24,128]{2,1,0:T(8,128)}, f32[2,16,128]{2,1,0:T(8,128)S(1)}) custom-call(f32[2,16,512]{2,1,0:T(8,128)S(1)} %get-tuple-element.35.offset_ref, s32[8,512]{1,0:T(8,128)S(1)} %get-tuple-element.30.type_ref, bf16[2,64,192]{2,1,0:T(8,128)(2,1)S(1)} %get-tuple-element.36.a_top_ref, f32[4,16,16,128]{3,2,1,0:T(8,128)S(1)} %get-tuple-element.37.coef_ref, ...), custom_call_target="tpu_custom_call" | custom-call | tf_op jit(solution)/shard_map/halo_offsets/pallas_call | solution.py:546
  7.0 6.8 %all-to-all-start = ((f32[8,24,128]{2,1,0:T(8,128)}), f32[8,24,128]{2,1,0:T(8,128)S(1)}, u32[]{:S(2)}, u32[]{:S(2)}) async-start(f32[8,24,128]{2,1,0:T(8,128)} %get-tuple-element.50), calls=%async_computation | async-start | bytes 196608 | tf_op jit(solution)/shard_map/all_to_all | solution.py:559
  13.8 2.9 %rest_sources.1 = (f32[2,8,48,512]{3,2,1,0:T(8,128)S(1)}, f32[2,8,16,256]{3,2,1,0:T(8,128)S(1)}, bf16[2,64,192]{2,1,0:T(8,128)(2,1)S(1)}, f32[4,16,16,128]{3,2,1,0:T(8,128)S(1)}) custom-call(f32[2,8,4,64,128]{4,3,2,1,0:T(8,128)} %get-tuple-element.34.source_hbm, f32[2,16,128]{2,1,0:T(8,128)S(1)} %get-tuple-element.42.flux_ref, ...), custom_call_target="tpu_custom_call" | custom-call | flops 603979776 | bytes 4194304 | tf_op jit(solution)/shard_map/rest_sources/pallas_call | solution.py:561
  16.7 4.3 %all-to-all-done.got_ref = f32[8,24,128]{2,1,0:T(8,128)S(1)} async-done(((f32[8,24,128]{2,1,0:T(8,128)}), f32[8,24,128]{2,1,0:T(8,128)S(1)}, u32[]{:S(2)}, u32[]{:S(2)}) %all-to-all-start) | async-done | bytes 98336 | tf_op jit(solution)/shard_map/all_to_all | solution.py:559
  21.0 1.3 %owner_sweep.1 = f32[8,16,128]{2,1,0:T(8,128)S(1)} custom-call(f32[4,16,16,128]{3,2,1,0:T(8,128)S(1)} %get-tuple-element.49.coef_ref, f32[8,24,128]{2,1,0:T(8,128)S(1)} %all-to-all-done.got_ref), custom_call_target="tpu_custom_call" | custom-call | tf_op jit(solution)/shard_map/owner_sweep/pallas_call | solution.py:580
  22.3 9.3 %all_to_all.10.got_ref = f32[8,16,128]{2,1,0:T(8,128)S(1)} all-to-all(f32[8,16,128]{2,1,0:T(8,128)S(1)} %owner_sweep.1), channel_id=1, replica_groups=mesh['flow'=8,'lat'=4] {'flow'}, dimensions={0} | all-to-all | bytes 131072 | tf_op jit(solution)/shard_map/all_to_all | solution.py:588
  31.6 2.1 %final_sweep.1 = bf16[2,8,64,512]{3,2,1,0:T(8,128)(2,1)} custom-call(f32[2,8,16,256]{3,2,1,0:T(8,128)S(1)} %get-tuple-element.33.mid_top_ref, f32[2,8,16,256]{3,2,1,0:T(8,128)S(1)} %get-tuple-element.44.edge_top_ref, f32[2,8,48,512]{3,2,1,0:T(8,128)S(1)} %get-tuple-element.45.rest_ref, s32[8,512]{1,0:T(8,128)S(1)} %get-tuple-element.30.type_ref, ...), custom_call_target="tpu_custom_call" | custom-call | tf_op jit(solution)/shard_map/final_sweep/pallas_call | solution.py:593
Async XLA Ops:
  1.8 4.0 %collective-permute-start = (f32[24,128]{1,0:T(8,128)S(1)}, f32[24,128]{1,0:T(8,128)S(1)}, u32[]{:S(2)}, u32[]{:S(2)}) collective-permute-start(f32[24,128]{1,0:T(8,128)S(1)} %get-tuple-element.40), channel_id=1, source_target_pairs={{0,1},{1,0},{2,3},{3,2},{4,5},{5,4},{6,7},{7,6},{8,9},{9,8},{10,11... | collective-permute-start | bytes 36872 | tf_op jit(solution)/shard_map/ppermute | solution.py:517
  2.3 3.4 %collective-permute-start.1 = (f32[24,128]{1,0:T(8,128)S(1)}, f32[24,128]{1,0:T(8,128)S(1)}, u32[]{:S(2)}, u32[]{:S(2)}) collective-permute-start(f32[24,128]{1,0:T(8,128)S(1)} %get-tuple-element.41), channel_id=1, source_target_pairs={{1,2},{2,1},{5,6},{6,5},{9,10},{10,9},{13,14},{14,13},{17,18},{18,... | collective-permute-start | bytes 36872 | tf_op jit(solution)/shard_map/ppermute | solution.py:520
  7.0 13.9 %all-to-all-start = ((f32[8,24,128]{2,1,0:T(8,128)}), f32[8,24,128]{2,1,0:T(8,128)S(1)}, u32[]{:S(2)}, u32[]{:S(2)}) async-start(f32[8,24,128]{2,1,0:T(8,128)} %get-tuple-element.50), calls=%async_computation | async-start | bytes 196608 | tf_op jit(solution)/shard_map/all_to_all | solution.py:559

commit v6 on v5

--- a/solution.py
+++ b/solution.py
@@ -1,3 +1,5 @@
+import functools
+
 import jax
 import jax.numpy as jnp
 from jax import lax
@@ -370,7 +372,10 @@
             copies.append(pltpu.make_async_copy(*ends, sems.at[len(copies)]))
             copies[-1].start()
     fill_late_tables(table_ref, a_rest_ref, c_ref)
-    fill_coefs(coef_ref, small_ref)
+    if len(coef_ref.shape) == 2:
+        fill_rows(coef_ref, small_ref)
+    else:
+        fill_coefs(coef_ref, small_ref)
     lane = lane_index((trace, LANES))
     zero, three = pl.ds(0, trace, stride=stride), pl.ds(stride - 1, trace, stride=stride)
     for l in range(levels):
@@ -391,6 +396,54 @@
             rest_ref[s, l] = pick(mm(a_rest_ref[s], parts), types, rest)
             outer = jnp.concatenate([parts[:, :LANES], parts[:, columns - LANES :]], axis=1)
             edge_top_ref[s, l] = pick(mm(a_top_ref[s], outer), edge_types, trace)
+
+
+def fill_rows(rows_ref, small_ref):
+    species, types_n, trace, _ = small_ref.shape
+    count = species * types_n
+    lane = lane_index((trace, LANES))
+    for j in range(trace):
+        block = jnp.zeros((trace, LANES), F32)
+        for t in range(types_n):
+            for s in range(species):
+                value = jnp.broadcast_to(small_ref[s, t, :, j : j + 1], (trace, LANES))
+                block = jnp.where(lane % count == t * species + s, value, block)
+        high, left = high_low(block)
+        middle, low = high_low(left)
+        block = jnp.where(lane < count, high, jnp.where(lane < 2 * count, middle, low))
+        rows_ref[j * trace : (j + 1) * trace] = block.astype(BF16)[:, : 3 * count]
+
+
+def owner_rows_kernel(species, rows_ref, got_ref, out_ref, coef_ref):
+    slabs, _, width = got_ref.shape
+    trace = out_ref.shape[1]
+    levels = got_ref.shape[1] - trace
+    depth = rows_ref.shape[1]
+    count = depth // 3
+    row = (lax.broadcasted_iota(jnp.int32, (depth, width), 0) % count).astype(F32)
+    which = (lane_index((depth, width)) // (width // species)).astype(F32)
+
+    def select(g):
+        hot = []
+        for l in range(levels):
+            types = jnp.broadcast_to(got_ref[g, trace + l : trace + l + 1], (depth, width))
+            hot.append(jnp.where(types * species + which == row, 1.0, 0.0).astype(BF16))
+        coefs = mm(rows_ref[...], jnp.concatenate(hot, axis=1))
+        for l in range(levels):
+            coef_ref[g % 2, l] = coefs[:, l * width : (l + 1) * width]
+
+    out_ref[0] = jnp.zeros((trace, width), F32)
+    state = got_ref[0, :trace]
+    select(1)
+    for g in range(1, slabs - 1):
+        out_ref[g] = state
+        if g + 1 < slabs - 1:
+            select(g + 1)
+        for l in range(levels):
+            coefs = [coef_ref[g % 2, l, j * trace : (j + 1) * trace] for j in range(trace)]
+            state = summed([coef * state[j : j + 1] for j, coef in enumerate(coefs)])
+        state = state + got_ref[g, :trace]
+    out_ref[slabs - 1] = state
 
 
 def owner_kernel(coef_ref, got_ref, out_ref):
@@ -558,13 +611,19 @@
         send = send.transpose(2, 1, 0, 3).reshape(flow_n, trace + levels, species * part)
     got = lax.all_to_all(send, "flow", 0, 0, tiled=True)
 
+    if packed:
+        owner_shape = held((trace * trace, 3 * types_n * species), BF16)
+        owner, owner_scratch = functools.partial(owner_rows_kernel, species), [pltpu.VMEM((2, levels, trace * trace, LANES), F32)]
+    else:
+        owner_shape = held((types_n, trace, trace, species * part))
+        owner, owner_scratch = owner_kernel, []
     rest_terms, edge_top, c_all, owner_coef = pl.pallas_call(
         rest_kernel,
         out_shape=(
             held((species, levels, rest, columns)),
             held((species, levels, trace, 2 * LANES)),
             held((species, dofs, 3 * types_n * trace), BF16),
-            held((types_n, trace, trace, species * part)),
+            owner_shape,
         ),
         in_specs=[HBM] + [VMEM] * 5,
         out_specs=(VMEM,) * 4,
@@ -578,7 +637,8 @@
         name="rest_sources",
     )(far(source), flux, types, a_top, table, small)
     back = pl.pallas_call(
-        owner_kernel,
+        owner,
+        scratch_shapes=owner_scratch,
         out_shape=shape((flow_n, trace, species * part)),
         in_specs=[VMEM, VMEM],
         out_specs=VMEM,

time: 34.4 us -> 34 us (0.988)
  no operation moved by 1% of the time
where the time goes in v6:
time: 34 us; the launch traced here: 33.4 us
  Pallas kernels  11.8 us (35%)
  blocking collectives  9.29 us (27%)
  starting transfers between devices  8.02 us (24%)
  waiting for transfers between devices  4.17 us (12%)
    all_to_all x1, blocking collectives, on_device(): traces = lax.all_to_all(back, 'flow', 0, 0, tiled=True)  9.29 us
    all_to_all x1, starting transfers between devices, on_device(): got = lax.all_to_all(send, 'flow', 0, 0, tiled=True)  6.81 us
    all_to_all x1, waiting for transfers between devices, on_device(): got = lax.all_to_all(send, 'flow', 0, 0, tiled=True)  4.17 us
    pallas_call x1, Pallas kernels, on_device(): pl.pallas_call(rest_kernel, out_shape=(held((species, levels, rest, colum...  2.95 us
    pallas_call x1, Pallas kernels, on_device(): pl.pallas_call(inner_kernel, out_shape=(pltpu.HBM(source_shape, F32), hel...  2.74 us
    pallas_call x1, Pallas kernels, on_device(): pl.pallas_call(final_kernel, out_shape=shape(conc_old.shape, BF16), in_sp...  2.12 us
    pallas_call x1, Pallas kernels, on_device(): pl.pallas_call(load_kernel, out_shape=(held((species, tiles, levels, dofs...  1.75 us
    pallas_call x1, Pallas kernels, on_device(): pl.pallas_call(halo_kernel, out_shape=(shape(send_shape), held((2, trace,...  1.29 us
  transfers between devices with their start and end apart: 3, of which 1 were waited for; matrix products, arithmetic and copies ran while one was open for 0% of the time, Pallas kernels for 17%

profile of v6, /device:TPU:0, one launch (start us, length us, event | category | flops | bytes accessed | tf_op | source)
XLA Modules:
  0.0 33.4 jit_solution(6012643198175759917)
XLA Ops:
  0.0 1.7 %load_edges.1 = (f32[2,4,8,64,128]{4,3,2,1,0:T(8,128)S(1)}, f32[8,512]{1,0:T(8,128)S(1)}, s32[8,512]{1,0:T(8,128)S(1)}, f32[2,4,64,80]{3,2,1,0:T(8,128)S(1)}, f3...) custom-call(f32[2,8,64,512]{3,2,1,0:T(8,128)} %conc_hbm.1, ...), custom_call_target="tpu_custom_call" | custom-call | tf_op jit(solution)/shard_map/load_edges/pallas_call | solution.py:550
  1.8 0.6 %collective-permute-start = (f32[24,128]{1,0:T(8,128)S(1)}, f32[24,128]{1,0:T(8,128)S(1)}, u32[]{:S(2)}, u32[]{:S(2)}) collective-permute-start(f32[24,128]{1,0:T(8,128)S(1)} %get-tuple-element.40), channel_id=1, source_target_pairs={{0,1},{1,0},{2,3},{3,2},{4,5},{5,4},{6,7},{7,6},{8,9},{9,8},{10,11... | collective-permute-start | bytes 36872 | tf_op jit(solution)/shard_map/ppermute | solution.py:570
  2.3 0.7 %collective-permute-start.1 = (f32[24,128]{1,0:T(8,128)S(1)}, f32[24,128]{1,0:T(8,128)S(1)}, u32[]{:S(2)}, u32[]{:S(2)}) collective-permute-start(f32[24,128]{1,0:T(8,128)S(1)} %get-tuple-element.41), channel_id=1, source_target_pairs={{1,2},{2,1},{5,6},{6,5},{9,10},{10,9},{13,14},{14,13},{17,18},{18,... | collective-permute-start | bytes 36872 | tf_op jit(solution)/shard_map/ppermute | solution.py:573
  3.0 2.7 %inner_sources.1 = (f32[2,8,4,64,128]{4,3,2,1,0:T(8,128)}, f32[2,8,16,256]{3,2,1,0:T(8,128)S(1)}, f32[2,16,512]{2,1,0:T(8,128)S(1)}, bf16[2,64,192]{2,1,0:T(8,12...) custom-call(f32[2,4,8,64,128]{4,3,2,1,0:T(8,128)S(1)} %get-tuple-ele, ...), custom_call_target="tpu_custom_call" | custom-call | flops 805306368 | bytes 4194304 | tf_op jit(solution)/shard_map/inner_sources/pallas_call | solution.py:577
  5.7 0.0 collective-permute-done.near_ref
  5.7 0.0 collective-permute-done.1.far_ref
  5.7 1.3 %halo_offsets.1 = (f32[8,24,128]{2,1,0:T(8,128)}, f32[2,16,128]{2,1,0:T(8,128)S(1)}) custom-call(f32[2,16,512]{2,1,0:T(8,128)S(1)} %get-tuple-element.35.offset_ref, s32[8,512]{1,0:T(8,128)S(1)} %get-tuple-element.30.type_ref, bf16[2,64,192]{2,1,0:T(8,128)(2,1)S(1)} %get-tuple-element.36.a_top_ref, f32[4,16,16,128]{3,2,1,0:T(8,128)S(1)} %get-tuple-element.37.coef_ref, ...), custom_call_target="tpu_custom_call" | custom-call | tf_op jit(solution)/shard_map/halo_offsets/pallas_call | solution.py:599
  7.0 6.8 %all-to-all-start = ((f32[8,24,128]{2,1,0:T(8,128)}), f32[8,24,128]{2,1,0:T(8,128)S(1)}, u32[]{:S(2)}, u32[]{:S(2)}) async-start(f32[8,24,128]{2,1,0:T(8,128)} %get-tuple-element.50), calls=%async_computation | async-start | bytes 196608 | tf_op jit(solution)/shard_map/all_to_all | solution.py:612
  13.8 2.9 %rest_sources.1 = (f32[2,8,48,512]{3,2,1,0:T(8,128)S(1)}, f32[2,8,16,256]{3,2,1,0:T(8,128)S(1)}, bf16[2,64,192]{2,1,0:T(8,128)(2,1)S(1)}, bf16[256,24]{1,0:T(8,128)(2,1)S(1)}) custom-call(f32[2,8,4,64,128]{4,3,2,1,0:T(8,128)} %get-tuple-element.34.source_hbm, f32[2,16,128]{2,1,0:T(8,128)S(1)} %get-tuple-element.42.flux_ref, ...), custom_call_target="tpu_custom_call" | custom-call | flops 603979776 | bytes 4194304 | tf_op jit(solution)/shard_map/rest_sources/pallas_call | solution.py:620
  16.8 4.2 %all-to-all-done.got_ref = f32[8,24,128]{2,1,0:T(8,128)S(1)} async-done(((f32[8,24,128]{2,1,0:T(8,128)}), f32[8,24,128]{2,1,0:T(8,128)S(1)}, u32[]{:S(2)}, u32[]{:S(2)}) %all-to-all-start) | async-done | bytes 98336 | tf_op jit(solution)/shard_map/all_to_all | solution.py:612
  21.0 1.0 %owner_sweep.1 = f32[8,16,128]{2,1,0:T(8,128)S(1)} custom-call(bf16[256,24]{1,0:T(8,128)(2,1)S(1)} %get-tuple-element.49.rows_ref, f32[8,24,128]{2,1,0:T(8,128)S(1)} %all-to-all-done.got_ref), custom_call_target="tpu_custom_call" | custom-call | tf_op jit(solution)/shard_map/owner_sweep/pallas_call | solution.py:639
  22.0 9.3 %all_to_all.10.got_ref = f32[8,16,128]{2,1,0:T(8,128)S(1)} all-to-all(f32[8,16,128]{2,1,0:T(8,128)S(1)} %owner_sweep.1), channel_id=1, replica_groups=mesh['flow'=8,'lat'=4] {'flow'}, dimensions={0} | all-to-all | bytes 131072 | tf_op jit(solution)/shard_map/all_to_all | solution.py:648
  31.3 2.1 %final_sweep.1 = bf16[2,8,64,512]{3,2,1,0:T(8,128)(2,1)} custom-call(f32[2,8,16,256]{3,2,1,0:T(8,128)S(1)} %get-tuple-element.33.mid_top_ref, f32[2,8,16,256]{3,2,1,0:T(8,128)S(1)} %get-tuple-element.44.edge_top_ref, f32[2,8,48,512]{3,2,1,0:T(8,128)S(1)} %get-tuple-element.45.rest_ref, s32[8,512]{1,0:T(8,128)S(1)} %get-tuple-element.30.type_ref, ...), custom_call_target="tpu_custom_call" | custom-call | tf_op jit(solution)/shard_map/final_sweep/pallas_call | solution.py:653
Async XLA Ops:
  1.8 4.0 %collective-permute-start = (f32[24,128]{1,0:T(8,128)S(1)}, f32[24,128]{1,0:T(8,128)S(1)}, u32[]{:S(2)}, u32[]{:S(2)}) collective-permute-start(f32[24,128]{1,0:T(8,128)S(1)} %get-tuple-element.40), channel_id=1, source_target_pairs={{0,1},{1,0},{2,3},{3,2},{4,5},{5,4},{6,7},{7,6},{8,9},{9,8},{10,11... | collective-permute-start | bytes 36872 | tf_op jit(solution)/shard_map/ppermute | solution.py:570
  2.3 3.4 %collective-permute-start.1 = (f32[24,128]{1,0:T(8,128)S(1)}, f32[24,128]{1,0:T(8,128)S(1)}, u32[]{:S(2)}, u32[]{:S(2)}) collective-permute-start(f32[24,128]{1,0:T(8,128)S(1)} %get-tuple-element.41), channel_id=1, source_target_pairs={{1,2},{2,1},{5,6},{6,5},{9,10},{10,9},{13,14},{14,13},{17,18},{18,... | collective-permute-start | bytes 36872 | tf_op jit(solution)/shard_map/ppermute | solution.py:573
  7.0 13.9 %all-to-all-start = ((f32[8,24,128]{2,1,0:T(8,128)}), f32[8,24,128]{2,1,0:T(8,128)S(1)}, u32[]{:S(2)}, u32[]{:S(2)}) async-start(f32[8,24,128]{2,1,0:T(8,128)} %get-tuple-element.50), calls=%async_computation | async-start | bytes 196608 | tf_op jit(solution)/shard_map/all_to_all | solution.py:612

commit v7 on v6

--- a/solution.py
+++ b/solution.py
@@ -568,9 +568,14 @@
     )(far(conc_old), far(lat_velocity), far(elem_type), far(solve_table), far(inlet_trace))
     assert lat_n % 2 == 0
     near_got = lax.ppermute(near, "lat", [(i, i ^ 1) for i in range(lat_n)])
-    swap = [(i, (i - 1) % lat_n if i % 2 == 0 else (i + 1) % lat_n) for i in range(lat_n)]
-    swap = [(i, j) for i, j in swap if abs(i - j) == 1]
-    far_got = lax.ppermute(far_side, "lat", swap)
+    assert flow_n % 2 == 0
+    swap = []
+    for f in range(flow_n):
+        for i in range(lat_n):
+            other = i - 1 if i % 2 == 0 else i + 1
+            target = f * lat_n + other if 0 <= other < lat_n else (f ^ 1) * lat_n + i
+            swap.append((f * lat_n + i, target))
+    far_got = lax.ppermute(far_side, ("flow", "lat"), swap)
 
 
     source_shape = (species, levels, tiles, dofs, LANES)

time: 34 us -> 34.2 us (level); the launches traced: 33.4 us -> 33.9 us
    ppermute x1, starting transfers between devices: 0.65 us -> 2.55 us  [on_device(): far_got = lax.ppermute(far_side, ('flow', 'lat'), swap)]
    all_to_all x1, starting transfers between devices: 6.81 us -> 5.24 us  [on_device(): got = lax.all_to_all(send, 'flow', 0, 0, tiled=True)]
where the time goes in v7:
time: 34.2 us; the launch traced here: 33.9 us
  Pallas kernels  11.8 us (35%)
  blocking collectives  9.29 us (27%)
  starting transfers between devices  8.35 us (24%)
  waiting for transfers between devices  4.42 us (13%)
    all_to_all x1, blocking collectives, on_device(): traces = lax.all_to_all(back, 'flow', 0, 0, tiled=True)  9.29 us
    all_to_all x1, starting transfers between devices, on_device(): got = lax.all_to_all(send, 'flow', 0, 0, tiled=True)  5.24 us
    all_to_all x1, waiting for transfers between devices, on_device(): got = lax.all_to_all(send, 'flow', 0, 0, tiled=True)  4.42 us
    pallas_call x1, Pallas kernels, on_device(): pl.pallas_call(rest_kernel, out_shape=(held((species, levels, rest, colum...  2.95 us
    pallas_call x1, Pallas kernels, on_device(): pl.pallas_call(inner_kernel, out_shape=(pltpu.HBM(source_shape, F32), hel...  2.73 us
    ppermute x1, starting transfers between devices, on_device(): far_got = lax.ppermute(far_side, ('flow', 'lat'), swap)  2.55 us
    pallas_call x1, Pallas kernels, on_device(): pl.pallas_call(final_kernel, out_shape=shape(conc_old.shape, BF16), in_sp...  2.12 us
    pallas_call x1, Pallas kernels, on_device(): pl.pallas_call(load_kernel, out_shape=(held((species, tiles, levels, dofs...  1.75 us
  transfers between devices with their start and end apart: 3, of which 1 were waited for; matrix products, arithmetic and copies ran while one was open for 0% of the time, Pallas kernels for 17%

profile of v7, /device:TPU:0, one launch (start us, length us, event | category | flops | bytes accessed | tf_op | source)
XLA Modules:
  0.0 33.9 jit_solution(2484441436098448647)
XLA Ops:
  0.0 1.7 %load_edges.1 = (f32[2,4,8,64,128]{4,3,2,1,0:T(8,128)S(1)}, f32[8,512]{1,0:T(8,128)S(1)}, s32[8,512]{1,0:T(8,128)S(1)}, f32[2,4,64,80]{3,2,1,0:T(8,128)S(1)}, f3...) custom-call(f32[2,8,64,512]{3,2,1,0:T(8,128)} %conc_hbm.1, ...), custom_call_target="tpu_custom_call" | custom-call | tf_op jit(solution)/shard_map/load_edges/pallas_call | solution.py:550
  1.8 0.6 %collective-permute-start = (f32[24,128]{1,0:T(8,128)S(1)}, f32[24,128]{1,0:T(8,128)S(1)}, u32[]{:S(2)}, u32[]{:S(2)}) collective-permute-start(f32[24,128]{1,0:T(8,128)S(1)} %get-tuple-element.40), channel_id=1, source_target_pairs={{0,1},{1,0},{2,3},{3,2},{4,5},{5,4},{6,7},{7,6},{8,9},{9,8},{10,11... | collective-permute-start | bytes 36872 | tf_op jit(solution)/shard_map/ppermute | solution.py:570
  2.3 2.6 %collective-permute-start.1 = (f32[24,128]{1,0:T(8,128)S(1)}, f32[24,128]{1,0:T(8,128)S(1)}, u32[]{:S(2)}, u32[]{:S(2)}) collective-permute-start(f32[24,128]{1,0:T(8,128)S(1)} %get-tuple-element.41), channel_id=1, source_target_pairs={{0,4},{1,2},{2,1},{3,7},{4,0},{5,6},{6,5},{7,3},{8,12},{9,10},{10,... | collective-permute-start | bytes 36872 | tf_op jit(solution)/shard_map/ppermute | solution.py:578
  4.9 2.7 %inner_sources.1 = (f32[2,8,4,64,128]{4,3,2,1,0:T(8,128)}, f32[2,8,16,256]{3,2,1,0:T(8,128)S(1)}, f32[2,16,512]{2,1,0:T(8,128)S(1)}, bf16[2,64,192]{2,1,0:T(8,12...) custom-call(f32[2,4,8,64,128]{4,3,2,1,0:T(8,128)S(1)} %get-tuple-ele, ...), custom_call_target="tpu_custom_call" | custom-call | flops 805306368 | bytes 4194304 | tf_op jit(solution)/shard_map/inner_sources/pallas_call | solution.py:582
  7.6 0.0 collective-permute-done.near_ref
  7.6 0.0 collective-permute-done.1.far_ref
  7.6 1.3 %halo_offsets.1 = (f32[8,24,128]{2,1,0:T(8,128)}, f32[2,16,128]{2,1,0:T(8,128)S(1)}) custom-call(f32[2,16,512]{2,1,0:T(8,128)S(1)} %get-tuple-element.35.offset_ref, s32[8,512]{1,0:T(8,128)S(1)} %get-tuple-element.30.type_ref, bf16[2,64,192]{2,1,0:T(8,128)(2,1)S(1)} %get-tuple-element.36.a_top_ref, f32[4,16,16,128]{3,2,1,0:T(8,128)S(1)} %get-tuple-element.37.coef_ref, ...), custom_call_target="tpu_custom_call" | custom-call | tf_op jit(solution)/shard_map/halo_offsets/pallas_call | solution.py:604
  8.9 5.2 %all-to-all-start = ((f32[8,24,128]{2,1,0:T(8,128)}), f32[8,24,128]{2,1,0:T(8,128)S(1)}, u32[]{:S(2)}, u32[]{:S(2)}) async-start(f32[8,24,128]{2,1,0:T(8,128)} %get-tuple-element.50), calls=%async_computation | async-start | bytes 196608 | tf_op jit(solution)/shard_map/all_to_all | solution.py:617
  14.2 2.9 %rest_sources.1 = (f32[2,8,48,512]{3,2,1,0:T(8,128)S(1)}, f32[2,8,16,256]{3,2,1,0:T(8,128)S(1)}, bf16[2,64,192]{2,1,0:T(8,128)(2,1)S(1)}, bf16[256,24]{1,0:T(8,128)(2,1)S(1)}) custom-call(f32[2,8,4,64,128]{4,3,2,1,0:T(8,128)} %get-tuple-element.34.source_hbm, f32[2,16,128]{2,1,0:T(8,128)S(1)} %get-tuple-element.42.flux_ref, ...), custom_call_target="tpu_custom_call" | custom-call | flops 603979776 | bytes 4194304 | tf_op jit(solution)/shard_map/rest_sources/pallas_call | solution.py:625
  17.1 4.4 %all-to-all-done.got_ref = f32[8,24,128]{2,1,0:T(8,128)S(1)} async-done(((f32[8,24,128]{2,1,0:T(8,128)}), f32[8,24,128]{2,1,0:T(8,128)S(1)}, u32[]{:S(2)}, u32[]{:S(2)}) %all-to-all-start) | async-done | bytes 98336 | tf_op jit(solution)/shard_map/all_to_all | solution.py:617
  21.5 1.0 %owner_sweep.1 = f32[8,16,128]{2,1,0:T(8,128)S(1)} custom-call(bf16[256,24]{1,0:T(8,128)(2,1)S(1)} %get-tuple-element.49.rows_ref, f32[8,24,128]{2,1,0:T(8,128)S(1)} %all-to-all-done.got_ref), custom_call_target="tpu_custom_call" | custom-call | tf_op jit(solution)/shard_map/owner_sweep/pallas_call | solution.py:644
  22.5 9.3 %all_to_all.10.got_ref = f32[8,16,128]{2,1,0:T(8,128)S(1)} all-to-all(f32[8,16,128]{2,1,0:T(8,128)S(1)} %owner_sweep.1), channel_id=1, replica_groups=mesh['flow'=8,'lat'=4] {'flow'}, dimensions={0} | all-to-all | bytes 131072 | tf_op jit(solution)/shard_map/all_to_all | solution.py:653
  31.8 2.1 %final_sweep.1 = bf16[2,8,64,512]{3,2,1,0:T(8,128)(2,1)} custom-call(f32[2,8,16,256]{3,2,1,0:T(8,128)S(1)} %get-tuple-element.33.mid_top_ref, f32[2,8,16,256]{3,2,1,0:T(8,128)S(1)} %get-tuple-element.44.edge_top_ref, f32[2,8,48,512]{3,2,1,0:T(8,128)S(1)} %get-tuple-element.45.rest_ref, s32[8,512]{1,0:T(8,128)S(1)} %get-tuple-element.30.type_ref, ...), custom_call_target="tpu_custom_call" | custom-call | tf_op jit(solution)/shard_map/final_sweep/pallas_call | solution.py:658
Async XLA Ops:
  1.8 5.9 %collective-permute-start = (f32[24,128]{1,0:T(8,128)S(1)}, f32[24,128]{1,0:T(8,128)S(1)}, u32[]{:S(2)}, u32[]{:S(2)}) collective-permute-start(f32[24,128]{1,0:T(8,128)S(1)} %get-tuple-element.40), channel_id=1, source_target_pairs={{0,1},{1,0},{2,3},{3,2},{4,5},{5,4},{6,7},{7,6},{8,9},{9,8},{10,11... | collective-permute-start | bytes 36872 | tf_op jit(solution)/shard_map/ppermute | solution.py:570
  2.3 5.3 %collective-permute-start.1 = (f32[24,128]{1,0:T(8,128)S(1)}, f32[24,128]{1,0:T(8,128)S(1)}, u32[]{:S(2)}, u32[]{:S(2)}) collective-permute-start(f32[24,128]{1,0:T(8,128)S(1)} %get-tuple-element.41), channel_id=1, source_target_pairs={{0,4},{1,2},{2,1},{3,7},{4,0},{5,6},{6,5},{7,3},{8,12},{9,10},{10,... | collective-permute-start | bytes 36872 | tf_op jit(solution)/shard_map/ppermute | solution.py:578
  8.9 12.6 %all-to-all-start = ((f32[8,24,128]{2,1,0:T(8,128)}), f32[8,24,128]{2,1,0:T(8,128)S(1)}, u32[]{:S(2)}, u32[]{:S(2)}) async-start(f32[8,24,128]{2,1,0:T(8,128)} %get-tuple-element.50), calls=%async_computation | async-start | bytes 196608 | tf_op jit(solution)/shard_map/all_to_all | solution.py:617
